TPU v7x, 256 devices: a whole 4x4x8 slice. The times are simulated.
256 devices in a mesh: gz: 16 (over z, y_hi), xy: 16 (over x, y_lo, core).
Axes of the slice: x: 4, y: 4 (y_hi: 2, y_lo: 2; y = y_hi * 2 + y_lo), z: 8, core: 2. Of those that a mesh axis runs over, the one named last changes fastest.
Arguments:
- view_one: float32 [256, 1024, 256], P('gz', 'xy'), may hold values from 0.2 to 5
- view_two: float32 [256, 1024, 256], P('gz', 'xy'), may hold values from 0.2 to 5
- estimate: float32 [256, 1024, 256], P('gz', 'xy'), may hold values from 0.5 to 2
- psf: float32 [2, 3, 15], replicated, may hold values from 0.05 to 1
Outputs:
- updated: float32 [256, 1024, 256], P('gz', 'xy')
All inputs are finite; a program needn't handle non-finite values.
Results may differ from a plain program's by a relative error of at most 0.00005.
Values sent between devices are 32-bit elements; how exact they have to be, the bound alone decides.
No kernel may reach another device: no remote copies, remote signals or barrier semaphores. Data moves between devices by JAX's collectives and lax.ppermute only.
A program may use at most 64 MiB of HBM per device.

v0:
```python
import jax
import jax.numpy as jnp
from jax import lax
from jax.sharding import PartitionSpec as P

ITERS = 2


def with_halo(cells, sides, width):
    for axis, dim in sides:
        count = lax.axis_size(axis)
        ends = count - 1
        head = lax.slice_in_dim(cells, 0, width, axis=dim)
        tail = lax.slice_in_dim(cells, cells.shape[dim] - width, cells.shape[dim], axis=dim)
        cells = jnp.concatenate(
            [
                lax.ppermute(tail, axis, [(i, (i + 1) % count) for i in range(ends)]),
                cells,
                lax.ppermute(head, axis, [((i + 1) % count, i) for i in range(ends)]),
            ],
            axis=dim,
        )
    return cells


def swapped(value, axis, bit):
    mask = 2**bit
    pairs = [(source, source ^ mask) for source in range(lax.axis_size(axis))]
    return lax.ppermute(value, axis, pairs)


def taps_along(padded, weights, dim, length):
    total = weights[0] * lax.slice_in_dim(padded, 0, length, axis=dim)
    for tap_index in range(1, weights.shape[0]):
        total = total + weights[tap_index] * lax.slice_in_dim(
            padded, tap_index, tap_index + length, axis=dim
        )
    return total


def band_matrix(weights, width):
    positions = jnp.arange(width)
    offsets = positions[:, None] - positions[None, :] + weights.shape[0] // 2
    matrix = jnp.zeros((width, width), jnp.float32)
    for tap_index in range(weights.shape[0]):
        matrix = matrix + weights[tap_index] * (offsets == tap_index).astype(jnp.float32)
    return matrix


def apply_blur(field, kernels):
    half = kernels.shape[1] // 2
    depth, rows, width = field.shape
    padded = with_halo(field, (("gz", 0),), half)
    along_z = taps_along(padded, kernels[0], 0, depth)
    padded_rows = with_halo(along_z, (("xy", 1),), half)
    along_y = taps_along(padded_rows, kernels[1], 1, rows)
    flat = along_y.reshape(depth * rows, width)
    result = jnp.dot(
        flat,
        band_matrix(kernels[2], width),
        precision=lax.Precision.HIGHEST,
        preferred_element_type=jnp.float32,
    )
    return result.reshape(depth, rows, width)


def mirror(field):
    for bit_index in range(lax.axis_size("gz").bit_length() - 1):
        field = swapped(field, "gz", bit_index)
    return field[::-1]


def local(view_one, view_two, estimate, psf):
    kernels = psf / jnp.sum(psf, axis=2, keepdims=True)
    forward_one = kernels[0]
    adjoint_one = kernels[0][:, ::-1]
    forward_two = kernels[1]
    adjoint_two = kernels[1][:, ::-1]
    for step_index in range(ITERS):
        back_one = apply_blur(view_one / apply_blur(estimate, forward_one), adjoint_one)
        blurred_two = apply_blur(mirror(estimate), forward_two)
        back_two = mirror(apply_blur(view_two / blurred_two, adjoint_two))
        estimate = estimate * (back_one + back_two) * 0.5
    return estimate


def solution(mesh):
    return jax.shard_map(
        local,
        mesh=mesh,
        in_specs=(P("gz", "xy", None), P("gz", "xy", None), P("gz", "xy", None), P()),
        out_specs=P("gz", "xy", None),
        check_vma=False,
    )
```

profile of v0, /device:TPU:30, one launch (start us, length us, event | category | flops | bytes accessed | tf_op | source)
XLA Modules:
  0.0 997.9 jit_solution(1821000939702189815)
XLA Ops:
  1.2 25.4 %collective-permute-done.8 = f32[16,64,256]{2,1,0:T(8,128)S(1)} collective-permute-done((f32[16,64,256]{2,1,0:T(8,128)}, f32[16,64,256]{2,1,0:T(8,128)S(1)}, u32[]{:S(2)}, u32[]{:S(2)}) %collective-permute-start.8) | collective-permute-done | bytes 1048608 | tf_op jit(solution)/shard_map/ppermute | solution.py:29
  28.5 22.3 %collective-permute-done.9 = f32[16,64,256]{2,1,0:T(8,128)S(1)} collective-permute-done((f32[16,64,256]{2,1,0:T(8,128)S(1)}, f32[16,64,256]{2,1,0:T(8,128)S(1)}, u32[]{:S(2)}, u32[]{:S(2)}) %collective-permute-start.9) | collective-permute-done | bytes 1048608 | tf_op jit(solution)/shard_map/ppermute | solution.py:29
  54.1 44.1 %collective-permute-done.10 = f32[16,64,256]{2,1,0:T(8,128)S(1)} collective-permute-done((f32[16,64,256]{2,1,0:T(8,128)S(1)}, f32[16,64,256]{2,1,0:T(8,128)S(1)}, u32[]{:S(2)}, u32[]{:S(2)}) %collective-permute-start.10) | collective-permute-done | bytes 1048608 | tf_op jit(solution)/shard_map/ppermute | solution.py:29
  98.2 6.2 collective-permute-start.11
  104.4 45.9 %collective-permute-done.11 = f32[16,64,256]{2,1,0:T(8,128)S(1)} collective-permute-done((f32[16,64,256]{2,1,0:T(8,128)S(1)}, f32[16,64,256]{2,1,0:T(8,128)S(1)}, u32[]{:S(2)}, u32[]{:S(2)}) %collective-permute-start.11) | collective-permute-done | bytes 1048608 | tf_op jit(solution)/shard_map/ppermute | solution.py:29
  152.4 5.5 collective-permute-start.13
  159.6 15.4 %collective-permute-done.12 = f32[7,64,256]{2,1,0:T(8,128)S(1)} collective-permute-done((f32[7,64,256]{2,1,0:T(8,128)S(1)}, f32[7,64,256]{2,1,0:T(8,128)S(1)}, u32[]{:S(2)}, u32[]{:S(2)}) %collective-permute-start.12) | collective-permute-done | bytes 458784 | tf_op jit(solution)/shard_map/ppermute | solution.py:17
  175.0 13.0 %fusion.597 = f32[16,64,256]{2,1,0:T(8,128)S(1)} fusion(f32[16,64,256]{2,1,0:T(8,128)S(1)} %rev.14, f32[7,64,256]{2,1,0:T(8,128)} %collective-permute-done.13, f32[7,64,256]{2,1,0:T(8,128)S(1)} %collective-permute-done.12, f32[]{:T(128)} %bitcast.114, f32[]{:T(128)} %bitcast.113, f32[]{:T(128)} %bitcast.112, f32[]{:T(128)} %bitcast.111, f32[]{:T(128)} %bitcast.110, ...), kind=kLoop, calls=%fused_computation.865 | loop fusion | flops 11272192 | bytes 3014716 | tf_op jit(solution)/shard_map/add | solution.py:35
  196.2 21.3 %convolution_divide_fusion.2 = f32[16,64,256]{2,1,0:T(8,128)S(1)} fusion(f32[16,64,256]{2,1,0:T(8,128)S(1)} %copy-done.3, f32[16,64,256]{2,1,0:T(8,128)S(1)} %fusion.597, f32[16,7,256]{2,1,0:T(8,128)S(1)} %collective-permute-done.15, f32[16,7,256]{2,1,0:T(8,128)S(1)} %collective-permute-done.14, f32[]{:T(128)} %bitcast.128, f32[]{:T(128)} %bitcast.127, ...), kind=kOutput, calls=%fused_computation.266 | convolution fusion | flops 819855360 | bytes 3375224 | tf_op jit(solution)/shard_map/dot_general | solution.py:58
  219.5 5.5 collective-permute-start.17
  225.6 14.8 %collective-permute-done.16 = f32[7,64,256]{2,1,0:T(8,128)S(1)} collective-permute-done((f32[7,64,256]{2,1,0:T(8,128)S(1)}, f32[7,64,256]{2,1,0:T(8,128)S(1)}, u32[]{:S(2)}, u32[]{:S(2)}) %collective-permute-start.16) | collective-permute-done | bytes 458784 | tf_op jit(solution)/shard_map/ppermute | solution.py:17
  240.4 11.3 %fusion.559 = f32[16,64,256]{2,1,0:T(8,128)S(1)} fusion(f32[16,64,256]{2,1,0:T(8,128)S(1)} %convolution_divide_fusion.2, f32[7,64,256]{2,1,0:T(8,128)S(1)} %collective-permute-done.17, f32[7,64,256]{2,1,0:T(8,128)S(1)} %collective-permute-done.16, f32[]{:T(128)} %bitcast.158, f32[]{:T(128)} %bitcast.157, f32[]{:T(128)} %bitcast.156, f32[]{:T(128)} %bitcast.155, ...), kind=kLoop, calls=%fused_computation.827 | loop fusion | flops 11272192 | bytes 3014716 | tf_op jit(solution)/shard_map/add | solution.py:35
  253.7 6.5 collective-permute-start.19
  262.9 21.6 %fusion.206 = f32[16,64,256]{2,1,0:T(8,128)S(1)} fusion(f32[16,64,256]{2,1,0:T(8,128)S(1)} %fusion.559, f32[16,7,256]{2,1,0:T(8,128)S(1)} %collective-permute-done.19, f32[16,7,256]{2,1,0:T(8,128)S(1)} %collective-permute-done.18, f32[]{:T(128)} %bitcast.172, f32[]{:T(128)} %bitcast.171, f32[]{:T(128)} %bitcast.170, f32[]{:T(128)} %bitcast.169, ...), kind=kOutput, calls=%fused_computation.522 | convolution fusion | flops 819593216 | bytes 2326648 | tf_op jit(solution)/shard_map/dot_general | solution.py:58
  286.8 5.5 collective-permute-start.1
  293.7 32.0 %collective-permute-done = f32[7,64,256]{2,1,0:T(8,128)S(1)} collective-permute-done((f32[7,64,256]{2,1,0:T(8,128)S(1)}, f32[7,64,256]{2,1,0:T(8,128)S(1)}, u32[]{:S(2)}, u32[]{:S(2)}) %collective-permute-start) | collective-permute-done | bytes 458784 | tf_op jit(solution)/shard_map/ppermute | solution.py:17
  326.1 11.1 %fusion.732 = f32[16,64,256]{2,1,0:T(8,128)S(1)} fusion(f32[23,64,256]{2,1,0:T(8,128)S(1)} %constant_dynamic-update-slice_fusion.2, f32[23,64,256]{2,1,0:T(8,128)S(1)} %get-tuple-element.27, f32[16,64,256]{2,1,0:T(8,128)S(1)} %copy-done, f32[]{:T(128)} %bitcast.19, f32[]{:T(128)} %bitcast.18, f32[]{:T(128)} %bitcast.17, f32[]{:T(128)} %bitcast.16, ...), kind=kLoop, calls=%fused_computation.1015 | loop fusion | flops 7602176 | bytes 16777276 | tf_op jit(solution)/shard_map/add | solution.py:35
  339.2 7.5 collective-permute-start.3
  350.7 22.0 %convolution_divide_fusion.3 = f32[16,64,256]{2,1,0:T(8,128)S(1)} fusion(f32[16,64,256]{2,1,0:T(8,128)S(1)} %copy-done.5, f32[16,64,256]{2,1,0:T(8,128)S(1)} %fusion.732, f32[16,7,256]{2,1,0:T(8,128)S(1)} %collective-permute-done.3, f32[16,7,256]{2,1,0:T(8,128)S(1)} %collective-permute-done.2, f32[]{:T(128)} %bitcast.33, f32[]{:T(128)} %bitcast.32, ...), kind=kOutput, calls=%fused_computation.267 | convolution fusion | flops 819855360 | bytes 3375224 | tf_op jit(solution)/shard_map/dot_general | solution.py:58
  380.8 10.4 %collective-permute-done.22 = f32[16,64,256]{2,1,0:T(8,128)S(1)} collective-permute-done((f32[16,64,256]{2,1,0:T(8,128)S(1)}, f32[16,64,256]{2,1,0:T(8,128)S(1)}, u32[]{:S(2)}, u32[]{:S(2)}) %collective-permute-start.22) | collective-permute-done | bytes 1048608 | tf_op jit(solution)/shard_map/ppermute | solution.py:29
  395.4 27.3 %collective-permute-done.5 = f32[7,64,256]{2,1,0:T(8,128)S(1)} collective-permute-done((f32[7,64,256]{2,1,0:T(8,128)S(1)}, f32[7,64,256]{2,1,0:T(8,128)S(1)}, u32[]{:S(2)}, u32[]{:S(2)}) %collective-permute-start.5) | collective-permute-done | bytes 458784 | tf_op jit(solution)/shard_map/ppermute | solution.py:19
  422.7 11.3 %fusion.635 = f32[16,64,256]{2,1,0:T(8,128)S(1)} fusion(f32[16,64,256]{2,1,0:T(8,128)S(1)} %convolution_divide_fusion.3, f32[7,64,256]{2,1,0:T(8,128)S(1)} %collective-permute-done.5, f32[7,64,256]{2,1,0:T(8,128)S(1)} %collective-permute-done.4, f32[]{:T(128)} %bitcast.63, f32[]{:T(128)} %bitcast.62, f32[]{:T(128)} %bitcast.61, f32[]{:T(128)} %bitcast.60, ...), kind=kLoop, calls=%fused_computation.903 | loop fusion | flops 11272192 | bytes 3014716 | tf_op jit(solution)/shard_map/add | solution.py:35
  435.9 13.2 %collective-permute-start.7 = (f32[16,7,256]{2,1,0:T(8,128)S(1)}, f32[16,7,256]{2,1,0:T(8,128)S(1)}, u32[]{:S(2)}, u32[]{:S(2)}) collective-permute-start(f32[16,7,256]{2,1,0:T(8,128)S(1)} %get-tuple-element.22), channel_id=1, source_target_pairs={{1,0},{2,1},{3,2},{4,3},{5,4},{6,5},{7,6},{8,7},{9,8},{10,9},{11,1... | collective-permute-start | bytes 344072 | tf_op jit(solution)/shard_map/ppermute | solution.py:19
  451.9 22.8 %broadcast_multiply_fusion = (f32[16,64,256]{2,1,0:T(8,128)S(1)}, f32[16,64,256]{2,1,0:T(8,128)}) fusion(f32[16,64,256]{2,1,0:T(8,128)S(1)} %copy-done, f32[16,64,256]{2,1,0:T(8,128)S(1)} %collective-permute-done.23, f32[]{:T(128)} %bitcast.93, f32[]{:T(128)} %bitcast.92, f32[]{:T(128)} %bitcast.91, f32[]{:T(128)} %bitcast.90, f32[]{:T(128)} %bitcast.89, ...), kind=kOutput, calls=%fused_computation.1052 | convolution fusion | flops 820379648 | bytes 5472376 | tf_op jit(solution)/shard_map/dot_general | solution.py:58
  474.6 16.3 %collective-permute-done.32 = f32[16,64,256]{2,1,0:T(8,128)S(1)} collective-permute-done((f32[16,64,256]{2,1,0:T(8,128)S(1)}, f32[16,64,256]{2,1,0:T(8,128)S(1)}, u32[]{:S(2)}, u32[]{:S(2)}) %collective-permute-start.32) | collective-permute-done | bytes 1048608 | tf_op jit(solution)/shard_map/ppermute | solution.py:29
  490.9 8.1 collective-permute-start.33
  499.0 22.0 %collective-permute-done.33 = f32[16,64,256]{2,1,0:T(8,128)S(1)} collective-permute-done((f32[16,64,256]{2,1,0:T(8,128)S(1)}, f32[16,64,256]{2,1,0:T(8,128)S(1)}, u32[]{:S(2)}, u32[]{:S(2)}) %collective-permute-start.33) | collective-permute-done | bytes 1048608 | tf_op jit(solution)/shard_map/ppermute | solution.py:29
  521.0 45.3 %collective-permute-done.34 = f32[16,64,256]{2,1,0:T(8,128)S(1)} collective-permute-done((f32[16,64,256]{2,1,0:T(8,128)S(1)}, f32[16,64,256]{2,1,0:T(8,128)S(1)}, u32[]{:S(2)}, u32[]{:S(2)}) %collective-permute-start.34) | collective-permute-done | bytes 1048608 | tf_op jit(solution)/shard_map/ppermute | solution.py:29
  566.4 62.0 %collective-permute-start.35 = (f32[16,64,256]{2,1,0:T(8,128)S(1)}, f32[16,64,256]{2,1,0:T(8,128)S(1)}, u32[]{:S(2)}, u32[]{:S(2)}) collective-permute-start(f32[16,64,256]{2,1,0:T(8,128)S(1)} %collective-permute-done.34), channel_id=1, source_target_pairs={{0,128},{16,144},{32,160},{48,176},{64,192},{80,208},{96,224},{112... | collective-permute-start | bytes 3145736 | tf_op jit(solution)/shard_map/ppermute | solution.py:29
  628.3 22.2 %collective-permute-done.35 = f32[16,64,256]{2,1,0:T(8,128)S(1)} collective-permute-done((f32[16,64,256]{2,1,0:T(8,128)S(1)}, f32[16,64,256]{2,1,0:T(8,128)S(1)}, u32[]{:S(2)}, u32[]{:S(2)}) %collective-permute-start.35) | collective-permute-done | bytes 1048608 | tf_op jit(solution)/shard_map/ppermute | solution.py:29
  654.2 6.2 collective-permute-start.37
  660.5 8.0 collective-permute-done.36
  668.5 13.6 %fusion.445 = f32[16,64,256]{2,1,0:T(8,128)S(1)} fusion(f32[16,64,256]{2,1,0:T(8,128)S(1)} %rev.16, f32[7,64,256]{2,1,0:T(8,128)} %collective-permute-done.37, f32[7,64,256]{2,1,0:T(8,128)} %collective-permute-done.36, f32[]{:T(128)} %bitcast.114, f32[]{:T(128)} %bitcast.113, f32[]{:T(128)} %bitcast.112, f32[]{:T(128)} %bitcast.111, f32[]{:T(128)} %bitcast.110, ...), kind=kLoop, calls=%fused_computation.713 | loop fusion | flops 11272192 | bytes 3014716 | tf_op jit(solution)/shard_map/add | solution.py:35
  690.2 21.3 %convolution_divide_fusion = f32[16,64,256]{2,1,0:T(8,128)S(1)} fusion(f32[16,64,256]{2,1,0:T(8,128)S(1)} %copy-done.4, f32[16,64,256]{2,1,0:T(8,128)S(1)} %fusion.445, f32[16,7,256]{2,1,0:T(8,128)S(1)} %collective-permute-done.39, f32[16,7,256]{2,1,0:T(8,128)S(1)} %collective-permute-done.38, f32[]{:T(128)} %bitcast.128, f32[]{:T(128)} %bitcast.127, ...), kind=kOutput, calls=%fused_computation.264 | convolution fusion | flops 819855360 | bytes 3375224 | tf_op jit(solution)/shard_map/dot_general | solution.py:58
  719.3 15.5 %collective-permute-done.40 = f32[7,64,256]{2,1,0:T(8,128)S(1)} collective-permute-done((f32[7,64,256]{2,1,0:T(8,128)S(1)}, f32[7,64,256]{2,1,0:T(8,128)S(1)}, u32[]{:S(2)}, u32[]{:S(2)}) %collective-permute-start.40) | collective-permute-done | bytes 458784 | tf_op jit(solution)/shard_map/ppermute | solution.py:17
  734.8 11.3 %fusion.407 = f32[16,64,256]{2,1,0:T(8,128)S(1)} fusion(f32[16,64,256]{2,1,0:T(8,128)S(1)} %convolution_divide_fusion, f32[7,64,256]{2,1,0:T(8,128)S(1)} %collective-permute-done.41, f32[7,64,256]{2,1,0:T(8,128)S(1)} %collective-permute-done.40, f32[]{:T(128)} %bitcast.158, f32[]{:T(128)} %bitcast.157, f32[]{:T(128)} %bitcast.156, f32[]{:T(128)} %bitcast.155, ...), kind=kLoop, calls=%fused_computation.675 | loop fusion | flops 11272192 | bytes 3014716 | tf_op jit(solution)/shard_map/add | solution.py:35
  754.4 21.6 %fusion.4 = f32[16,64,256]{2,1,0:T(8,128)S(1)} fusion(f32[16,64,256]{2,1,0:T(8,128)S(1)} %fusion.407, f32[16,7,256]{2,1,0:T(8,128)S(1)} %collective-permute-done.43, f32[16,7,256]{2,1,0:T(8,128)S(1)} %collective-permute-done.42, f32[]{:T(128)} %bitcast.172, f32[]{:T(128)} %bitcast.171, f32[]{:T(128)} %bitcast.170, f32[]{:T(128)} %bitcast.169, ...), kind=kOutput, calls=%fused_computation.368 | convolution fusion | flops 819593216 | bytes 2326648 | tf_op jit(solution)/shard_map/dot_general | solution.py:58
  776.6 8.6 collective-permute-start.24
  787.1 26.5 %collective-permute-done.44 = f32[16,64,256]{2,1,0:T(8,128)} collective-permute-done((f32[16,64,256]{2,1,0:T(8,128)S(1)}, f32[16,64,256]{2,1,0:T(8,128)}, u32[]{:S(2)}, u32[]{:S(2)}) %collective-permute-start.44) | collective-permute-done | bytes 1048608 | tf_op jit(solution)/shard_map/ppermute | solution.py:29
  819.5 12.5 %fusion.521 = f32[16,64,256]{2,1,0:T(8,128)S(1)} fusion(f32[16,64,256]{2,1,0:T(8,128)S(1)} %get-tuple-element.225, f32[7,64,256]{2,1,0:T(8,128)} %collective-permute-done.25, f32[7,64,256]{2,1,0:T(8,128)} %collective-permute-done.24, f32[16,64,256]{2,1,0:T(8,128)S(1)} %copy-done.1, f32[]{:T(128)S(6)} %mul.2065, f32[]{:T(128)} %bitcast.19, f32[]{:T(128)} %bitcast.18, ...), kind=kLoop, calls=%fused_computation.789 | loop fusion | flops 11272192 | bytes 4063292 | tf_op jit(solution)/shard_map/add | solution.py:35
  833.9 5.8 collective-permute-start.27
  839.8 7.2 collective-permute-start.46
  847.0 21.9 %convolution_divide_fusion.1 = f32[16,64,256]{2,1,0:T(8,128)S(1)} fusion(f32[16,64,256]{2,1,0:T(8,128)S(1)} %copy-done.6, f32[16,64,256]{2,1,0:T(8,128)S(1)} %fusion.521, f32[16,7,256]{2,1,0:T(8,128)S(1)} %collective-permute-done.27, f32[16,7,256]{2,1,0:T(8,128)S(1)} %collective-permute-done.26, f32[]{:T(128)} %bitcast.33, f32[]{:T(128)} %bitcast.32, ...), kind=kOutput, calls=%fused_computation.265 | convolution fusion | flops 819855360 | bytes 3375224 | tf_op jit(solution)/shard_map/dot_general | solution.py:58
  876.4 12.3 %collective-permute-done.46 = f32[16,64,256]{2,1,0:T(8,128)S(1)} collective-permute-done((f32[16,64,256]{2,1,0:T(8,128)}, f32[16,64,256]{2,1,0:T(8,128)S(1)}, u32[]{:S(2)}, u32[]{:S(2)}) %collective-permute-start.46) | collective-permute-done | bytes 1048608 | tf_op jit(solution)/shard_map/ppermute | solution.py:29
  888.6 51.6 %collective-permute-start.47 = (f32[16,64,256]{2,1,0:T(8,128)S(1)}, f32[16,64,256]{2,1,0:T(8,128)S(1)}, u32[]{:S(2)}, u32[]{:S(2)}) collective-permute-start(f32[16,64,256]{2,1,0:T(8,128)S(1)} %collective-permute-done.46), channel_id=1, source_target_pairs={{0,128},{16,144},{32,160},{48,176},{64,192},{80,208},{96,224},{112... | collective-permute-start | bytes 3145736 | tf_op jit(solution)/shard_map/ppermute | solution.py:29
  940.2 11.3 %fusion.483 = f32[16,64,256]{2,1,0:T(8,128)S(1)} fusion(f32[16,64,256]{2,1,0:T(8,128)S(1)} %convolution_divide_fusion.1, f32[7,64,256]{2,1,0:T(8,128)S(1)} %collective-permute-done.29, f32[7,64,256]{2,1,0:T(8,128)S(1)} %collective-permute-done.28, f32[]{:T(128)} %bitcast.63, f32[]{:T(128)} %bitcast.62, f32[]{:T(128)} %bitcast.61, f32[]{:T(128)} %bitcast.60, ...), kind=kLoop, calls=%fused_computation.751 | loop fusion | flops 11272192 | bytes 3014716 | tf_op jit(solution)/shard_map/add | solution.py:35
  959.6 15.4 %collective-permute-done.47 = f32[16,64,256]{2,1,0:T(8,128)S(1)} collective-permute-done((f32[16,64,256]{2,1,0:T(8,128)S(1)}, f32[16,64,256]{2,1,0:T(8,128)S(1)}, u32[]{:S(2)}, u32[]{:S(2)}) %collective-permute-start.47) | collective-permute-done | bytes 1048608 | tf_op jit(solution)/shard_map/ppermute | solution.py:29
  974.9 22.8 %multiply_multiply_fusion = f32[16,64,256]{2,1,0:T(8,128)} fusion(f32[16,64,256]{2,1,0:T(8,128)S(1)} %collective-permute-done.47, f32[16,64,256]{2,1,0:T(8,128)S(1)} %fusion.483, f32[16,7,256]{2,1,0:T(8,128)S(1)} %collective-permute-done.31, f32[16,7,256]{2,1,0:T(8,128)S(1)} %collective-permute-done.30, f32[]{:T(128)} %bitcast.77, f32[]{:T(128)} %bitcast.76, ...), kind=kOutput, calls=%fused_computation.1042 | convolution fusion | flops 820641792 | bytes 4423800 | tf_op jit(solution)/shard_map/dot_general | solution.py:58
  (117 shorter events, 105.7 us)
Async XLA Ops:
  0.0 26.6 %collective-permute-start.8 = (f32[16,64,256]{2,1,0:T(8,128)}, f32[16,64,256]{2,1,0:T(8,128)S(1)}, u32[]{:S(2)}, u32[]{:S(2)}) collective-permute-start(f32[16,64,256]{2,1,0:T(8,128)} %param.6), channel_id=1, source_target_pairs={{0,16},{16,0},{32,48},{48,32},{64,80},{80,64},{96,112},{112,96},{1... | collective-permute-start | bytes 3145736 | tf_op jit(solution)/shard_map/ppermute | solution.py:29
  26.6 24.2 %collective-permute-start.9 = (f32[16,64,256]{2,1,0:T(8,128)S(1)}, f32[16,64,256]{2,1,0:T(8,128)S(1)}, u32[]{:S(2)}, u32[]{:S(2)}) collective-permute-start(f32[16,64,256]{2,1,0:T(8,128)S(1)} %collective-permute-done.8), channel_id=1, source_target_pairs={{0,32},{16,48},{32,0},{48,16},{64,96},{80,112},{96,64},{112,80},{1... | collective-permute-start | bytes 3145736 | tf_op jit(solution)/shard_map/ppermute | solution.py:29
  50.8 47.4 %collective-permute-start.10 = (f32[16,64,256]{2,1,0:T(8,128)S(1)}, f32[16,64,256]{2,1,0:T(8,128)S(1)}, u32[]{:S(2)}, u32[]{:S(2)}) collective-permute-start(f32[16,64,256]{2,1,0:T(8,128)S(1)} %collective-permute-done.9), channel_id=1, source_target_pairs={{0,64},{16,80},{32,96},{48,112},{64,0},{80,16},{96,32},{112,48},{1... | collective-permute-start | bytes 3145736 | tf_op jit(solution)/shard_map/ppermute | solution.py:29
  98.2 52.1 %collective-permute-start.11 = (f32[16,64,256]{2,1,0:T(8,128)S(1)}, f32[16,64,256]{2,1,0:T(8,128)S(1)}, u32[]{:S(2)}, u32[]{:S(2)}) collective-permute-start(f32[16,64,256]{2,1,0:T(8,128)S(1)} %collective-permute-done.10), channel_id=1, source_target_pairs={{0,128},{16,144},{32,160},{48,176},{64,192},{80,208},{96,224},{112... | collective-permute-start | bytes 3145736 | tf_op jit(solution)/shard_map/ppermute | solution.py:29
  150.4 24.6 %collective-permute-start.12 = (f32[7,64,256]{2,1,0:T(8,128)S(1)}, f32[7,64,256]{2,1,0:T(8,128)S(1)}, u32[]{:S(2)}, u32[]{:S(2)}) collective-permute-start(f32[7,64,256]{2,1,0:T(8,128)S(1)} %slice.2335), channel_id=1, source_target_pairs={{0,16},{16,32},{32,48},{48,64},{64,80},{80,96},{96,112},{112,128},... | collective-permute-start | bytes 1376264 | tf_op jit(solution)/shard_map/ppermute | solution.py:17
  152.4 22.6 %collective-permute-start.13 = (f32[7,64,256]{2,1,0:T(8,128)S(1)}, f32[7,64,256]{2,1,0:T(8,128)}, u32[]{:S(2)}, u32[]{:S(2)}) collective-permute-start(f32[7,64,256]{2,1,0:T(8,128)S(1)} %slice.2352), channel_id=1, source_target_pairs={{16,0},{32,16},{48,32},{64,48},{80,64},{96,80},{112,96},{128,112},... | collective-permute-start | bytes 1376264 | tf_op jit(solution)/shard_map/ppermute | solution.py:19
  188.1 6.3 collective-permute-start.14
  190.0 6.1 collective-permute-start.15
  217.5 22.9 %collective-permute-start.16 = (f32[7,64,256]{2,1,0:T(8,128)S(1)}, f32[7,64,256]{2,1,0:T(8,128)S(1)}, u32[]{:S(2)}, u32[]{:S(2)}) collective-permute-start(f32[7,64,256]{2,1,0:T(8,128)S(1)} %get-tuple-element.33), channel_id=1, source_target_pairs={{0,16},{16,32},{32,48},{48,64},{64,80},{80,96},{96,112},{112,128},... | collective-permute-start | bytes 1376264 | tf_op jit(solution)/shard_map/ppermute | solution.py:17
  219.5 21.0 %collective-permute-start.17 = (f32[7,64,256]{2,1,0:T(8,128)S(1)}, f32[7,64,256]{2,1,0:T(8,128)S(1)}, u32[]{:S(2)}, u32[]{:S(2)}) collective-permute-start(f32[7,64,256]{2,1,0:T(8,128)S(1)} %get-tuple-element.34), channel_id=1, source_target_pairs={{16,0},{32,16},{48,32},{64,48},{80,64},{96,80},{112,96},{128,112},... | collective-permute-start | bytes 1376264 | tf_op jit(solution)/shard_map/ppermute | solution.py:19
  251.7 9.9 collective-permute-start.18
  253.7 9.2 collective-permute-start.19
  284.5 41.2 %collective-permute-start.20 = (f32[16,64,256]{2,1,0:T(8,128)S(1)}, f32[16,64,256]{2,1,0:T(8,128)S(1)}, u32[]{:S(2)}, u32[]{:S(2)}) collective-permute-start(f32[16,64,256]{2,1,0:T(8,128)S(1)} %fusion.206), channel_id=1, source_target_pairs={{0,16},{16,0},{32,48},{48,32},{64,80},{80,64},{96,112},{112,96},{1... | collective-permute-start | bytes 3145736 | tf_op jit(solution)/shard_map/ppermute | solution.py:29
  284.8 40.8 %collective-permute-start = (f32[7,64,256]{2,1,0:T(8,128)S(1)}, f32[7,64,256]{2,1,0:T(8,128)S(1)}, u32[]{:S(2)}, u32[]{:S(2)}) collective-permute-start(f32[7,64,256]{2,1,0:T(8,128)S(1)} %get-tuple-element.29), channel_id=1, source_target_pairs={{0,16},{16,32},{32,48},{48,64},{64,80},{80,96},{96,112},{112,128},... | collective-permute-start | bytes 1376264 | tf_op jit(solution)/shard_map/ppermute | solution.py:17
  286.8 39.3 %collective-permute-start.1 = (f32[7,64,256]{2,1,0:T(8,128)S(1)}, f32[7,64,256]{2,1,0:T(8,128)S(1)}, u32[]{:S(2)}, u32[]{:S(2)}) collective-permute-start(f32[7,64,256]{2,1,0:T(8,128)S(1)} %get-tuple-element.30), channel_id=1, source_target_pairs={{16,0},{32,16},{48,32},{64,48},{80,64},{96,80},{112,96},{128,112},... | collective-permute-start | bytes 1376264 | tf_op jit(solution)/shard_map/ppermute | solution.py:19
  325.7 21.1 %collective-permute-start.21 = (f32[16,64,256]{2,1,0:T(8,128)S(1)}, f32[16,64,256]{2,1,0:T(8,128)S(1)}, u32[]{:S(2)}, u32[]{:S(2)}) collective-permute-start(f32[16,64,256]{2,1,0:T(8,128)S(1)} %collective-permute-done.20), channel_id=1, source_target_pairs={{0,32},{16,48},{32,0},{48,16},{64,96},{80,112},{96,64},{112,80},{1... | collective-permute-start | bytes 3145736 | tf_op jit(solution)/shard_map/ppermute | solution.py:29
  337.3 13.1 %collective-permute-start.2 = (f32[16,7,256]{2,1,0:T(8,128)S(1)}, f32[16,7,256]{2,1,0:T(8,128)S(1)}, u32[]{:S(2)}, u32[]{:S(2)}) collective-permute-start(f32[16,7,256]{2,1,0:T(8,128)S(1)} %get-tuple-element.25), channel_id=1, source_target_pairs={{0,1},{1,2},{2,3},{3,4},{4,5},{5,6},{6,7},{7,8},{8,9},{9,10},{10,1... | collective-permute-start | bytes 344072 | tf_op jit(solution)/shard_map/ppermute | solution.py:17
  339.2 11.4 %collective-permute-start.3 = (f32[16,7,256]{2,1,0:T(8,128)S(1)}, f32[16,7,256]{2,1,0:T(8,128)S(1)}, u32[]{:S(2)}, u32[]{:S(2)}) collective-permute-start(f32[16,7,256]{2,1,0:T(8,128)S(1)} %get-tuple-element.26), channel_id=1, source_target_pairs={{1,0},{2,1},{3,2},{4,3},{5,4},{6,5},{7,6},{8,7},{9,8},{10,9},{11,1... | collective-permute-start | bytes 344072 | tf_op jit(solution)/shard_map/ppermute | solution.py:19
  346.8 44.5 %collective-permute-start.22 = (f32[16,64,256]{2,1,0:T(8,128)S(1)}, f32[16,64,256]{2,1,0:T(8,128)S(1)}, u32[]{:S(2)}, u32[]{:S(2)}) collective-permute-start(f32[16,64,256]{2,1,0:T(8,128)S(1)} %collective-permute-done.21), channel_id=1, source_target_pairs={{0,64},{16,80},{32,96},{48,112},{64,0},{80,16},{96,32},{112,48},{1... | collective-permute-start | bytes 3145736 | tf_op jit(solution)/shard_map/ppermute | solution.py:29
  372.7 22.6 %collective-permute-start.4 = (f32[7,64,256]{2,1,0:T(8,128)S(1)}, f32[7,64,256]{2,1,0:T(8,128)S(1)}, u32[]{:S(2)}, u32[]{:S(2)}) collective-permute-start(f32[7,64,256]{2,1,0:T(8,128)S(1)} %get-tuple-element.23), channel_id=1, source_target_pairs={{0,16},{16,32},{32,48},{48,64},{64,80},{80,96},{96,112},{112,128},... | collective-permute-start | bytes 1376264 | tf_op jit(solution)/shard_map/ppermute | solution.py:17
  376.8 45.9 %collective-permute-start.5 = (f32[7,64,256]{2,1,0:T(8,128)S(1)}, f32[7,64,256]{2,1,0:T(8,128)S(1)}, u32[]{:S(2)}, u32[]{:S(2)}) collective-permute-start(f32[7,64,256]{2,1,0:T(8,128)S(1)} %get-tuple-element.24), channel_id=1, source_target_pairs={{16,0},{32,16},{48,32},{64,48},{80,64},{96,80},{112,96},{128,112},... | collective-permute-start | bytes 1376264 | tf_op jit(solution)/shard_map/ppermute | solution.py:19
  391.3 60.6 %collective-permute-start.23 = (f32[16,64,256]{2,1,0:T(8,128)S(1)}, f32[16,64,256]{2,1,0:T(8,128)S(1)}, u32[]{:S(2)}, u32[]{:S(2)}) collective-permute-start(f32[16,64,256]{2,1,0:T(8,128)S(1)} %collective-permute-done.22), channel_id=1, source_target_pairs={{0,128},{16,144},{32,160},{48,176},{64,192},{80,208},{96,224},{112... | collective-permute-start | bytes 3145736 | tf_op jit(solution)/shard_map/ppermute | solution.py:29
  434.0 16.6 %collective-permute-start.6 = (f32[16,7,256]{2,1,0:T(8,128)S(1)}, f32[16,7,256]{2,1,0:T(8,128)S(1)}, u32[]{:S(2)}, u32[]{:S(2)}) collective-permute-start(f32[16,7,256]{2,1,0:T(8,128)S(1)} %get-tuple-element.21), channel_id=1, source_target_pairs={{0,1},{1,2},{2,3},{3,4},{4,5},{5,6},{6,7},{7,8},{8,9},{9,10},{10,1... | collective-permute-start | bytes 344072 | tf_op jit(solution)/shard_map/ppermute | solution.py:17
  435.9 16.0 %collective-permute-start.7 = (f32[16,7,256]{2,1,0:T(8,128)S(1)}, f32[16,7,256]{2,1,0:T(8,128)S(1)}, u32[]{:S(2)}, u32[]{:S(2)}) collective-permute-start(f32[16,7,256]{2,1,0:T(8,128)S(1)} %get-tuple-element.22), channel_id=1, source_target_pairs={{1,0},{2,1},{3,2},{4,3},{5,4},{6,5},{7,6},{8,7},{9,8},{10,9},{11,1... | collective-permute-start | bytes 344072 | tf_op jit(solution)/shard_map/ppermute | solution.py:19
  474.6 16.3 %collective-permute-start.32 = (f32[16,64,256]{2,1,0:T(8,128)S(1)}, f32[16,64,256]{2,1,0:T(8,128)S(1)}, u32[]{:S(2)}, u32[]{:S(2)}) collective-permute-start(f32[16,64,256]{2,1,0:T(8,128)S(1)} %get-tuple-element.225), channel_id=1, source_target_pairs={{0,16},{16,0},{32,48},{48,32},{64,80},{80,64},{96,112},{112,96},{1... | collective-permute-start | bytes 3145736 | tf_op jit(solution)/shard_map/ppermute | solution.py:29
  490.9 30.1 %collective-permute-start.33 = (f32[16,64,256]{2,1,0:T(8,128)S(1)}, f32[16,64,256]{2,1,0:T(8,128)S(1)}, u32[]{:S(2)}, u32[]{:S(2)}) collective-permute-start(f32[16,64,256]{2,1,0:T(8,128)S(1)} %collective-permute-done.32), channel_id=1, source_target_pairs={{0,32},{16,48},{32,0},{48,16},{64,96},{80,112},{96,64},{112,80},{1... | collective-permute-start | bytes 3145736 | tf_op jit(solution)/shard_map/ppermute | solution.py:29
  521.0 45.3 %collective-permute-start.34 = (f32[16,64,256]{2,1,0:T(8,128)S(1)}, f32[16,64,256]{2,1,0:T(8,128)S(1)}, u32[]{:S(2)}, u32[]{:S(2)}) collective-permute-start(f32[16,64,256]{2,1,0:T(8,128)S(1)} %collective-permute-done.33), channel_id=1, source_target_pairs={{0,64},{16,80},{32,96},{48,112},{64,0},{80,16},{96,32},{112,48},{1... | collective-permute-start | bytes 3145736 | tf_op jit(solution)/shard_map/ppermute | solution.py:29
  566.4 84.2 %collective-permute-start.35 = (f32[16,64,256]{2,1,0:T(8,128)S(1)}, f32[16,64,256]{2,1,0:T(8,128)S(1)}, u32[]{:S(2)}, u32[]{:S(2)}) collective-permute-start(f32[16,64,256]{2,1,0:T(8,128)S(1)} %collective-permute-done.34), channel_id=1, source_target_pairs={{0,128},{16,144},{32,160},{48,176},{64,192},{80,208},{96,224},{112... | collective-permute-start | bytes 3145736 | tf_op jit(solution)/shard_map/ppermute | solution.py:29
  651.4 17.1 %collective-permute-start.36 = (f32[7,64,256]{2,1,0:T(8,128)}, f32[7,64,256]{2,1,0:T(8,128)}, u32[]{:S(2)}, u32[]{:S(2)}) collective-permute-start(f32[7,64,256]{2,1,0:T(8,128)} %slice.2553), channel_id=1, source_target_pairs={{0,16},{16,32},{32,48},{48,64},{64,80},{80,96},{96,112},{112,128},... | collective-permute-start | bytes 1376264 | tf_op jit(solution)/shard_map/ppermute | solution.py:17
  654.2 14.4 %collective-permute-start.37 = (f32[7,64,256]{2,1,0:T(8,128)}, f32[7,64,256]{2,1,0:T(8,128)}, u32[]{:S(2)}, u32[]{:S(2)}) collective-permute-start(f32[7,64,256]{2,1,0:T(8,128)} %slice.2562), channel_id=1, source_target_pairs={{16,0},{32,16},{48,32},{64,48},{80,64},{96,80},{112,96},{128,112},... | collective-permute-start | bytes 1376264 | tf_op jit(solution)/shard_map/ppermute | solution.py:19
  682.1 6.3 collective-permute-start.38
  684.0 6.1 collective-permute-start.39
  711.6 23.3 %collective-permute-start.40 = (f32[7,64,256]{2,1,0:T(8,128)S(1)}, f32[7,64,256]{2,1,0:T(8,128)S(1)}, u32[]{:S(2)}, u32[]{:S(2)}) collective-permute-start(f32[7,64,256]{2,1,0:T(8,128)S(1)} %get-tuple-element.15), channel_id=1, source_target_pairs={{0,16},{16,32},{32,48},{48,64},{64,80},{80,96},{96,112},{112,128},... | collective-permute-start | bytes 1376264 | tf_op jit(solution)/shard_map/ppermute | solution.py:17
  714.6 20.3 %collective-permute-start.41 = (f32[7,64,256]{2,1,0:T(8,128)S(1)}, f32[7,64,256]{2,1,0:T(8,128)S(1)}, u32[]{:S(2)}, u32[]{:S(2)}) collective-permute-start(f32[7,64,256]{2,1,0:T(8,128)S(1)} %get-tuple-element.16), channel_id=1, source_target_pairs={{16,0},{32,16},{48,32},{64,48},{80,64},{96,80},{112,96},{128,112},... | collective-permute-start | bytes 1376264 | tf_op jit(solution)/shard_map/ppermute | solution.py:19
  746.1 6.4 collective-permute-start.42
  748.1 6.3 collective-permute-start.43
  776.0 37.6 %collective-permute-start.44 = (f32[16,64,256]{2,1,0:T(8,128)S(1)}, f32[16,64,256]{2,1,0:T(8,128)}, u32[]{:S(2)}, u32[]{:S(2)}) collective-permute-start(f32[16,64,256]{2,1,0:T(8,128)S(1)} %fusion.4), channel_id=1, source_target_pairs={{0,16},{16,0},{32,48},{48,32},{64,80},{80,64},{96,112},{112,96},{1... | collective-permute-start | bytes 3145736 | tf_op jit(solution)/shard_map/ppermute | solution.py:29
  776.6 42.9 %collective-permute-start.24 = (f32[7,64,256]{2,1,0:T(8,128)S(1)}, f32[7,64,256]{2,1,0:T(8,128)}, u32[]{:S(2)}, u32[]{:S(2)}) collective-permute-start(f32[7,64,256]{2,1,0:T(8,128)S(1)} %get-tuple-element.11), channel_id=1, source_target_pairs={{0,16},{16,32},{32,48},{48,64},{64,80},{80,96},{96,112},{112,128},... | collective-permute-start | bytes 1376264 | tf_op jit(solution)/shard_map/ppermute | solution.py:17
  785.1 34.3 %collective-permute-start.25 = (f32[7,64,256]{2,1,0:T(8,128)S(1)}, f32[7,64,256]{2,1,0:T(8,128)}, u32[]{:S(2)}, u32[]{:S(2)}) collective-permute-start(f32[7,64,256]{2,1,0:T(8,128)S(1)} %get-tuple-element.12), channel_id=1, source_target_pairs={{16,0},{32,16},{48,32},{64,48},{80,64},{96,80},{112,96},{128,112},... | collective-permute-start | bytes 1376264 | tf_op jit(solution)/shard_map/ppermute | solution.py:19
  813.5 26.2 %collective-permute-start.45 = (f32[16,64,256]{2,1,0:T(8,128)}, f32[16,64,256]{2,1,0:T(8,128)}, u32[]{:S(2)}, u32[]{:S(2)}) collective-permute-start(f32[16,64,256]{2,1,0:T(8,128)} %collective-permute-done.44), channel_id=1, source_target_pairs={{0,32},{16,48},{32,0},{48,16},{64,96},{80,112},{96,64},{112,80},{1... | collective-permute-start | bytes 3145736 | tf_op jit(solution)/shard_map/ppermute | solution.py:29
  832.0 15.0 %collective-permute-start.26 = (f32[16,7,256]{2,1,0:T(8,128)S(1)}, f32[16,7,256]{2,1,0:T(8,128)S(1)}, u32[]{:S(2)}, u32[]{:S(2)}) collective-permute-start(f32[16,7,256]{2,1,0:T(8,128)S(1)} %get-tuple-element.9), channel_id=1, source_target_pairs={{0,1},{1,2},{2,3},{3,4},{4,5},{5,6},{6,7},{7,8},{8,9},{9,10},{10,1... | collective-permute-start | bytes 344072 | tf_op jit(solution)/shard_map/ppermute | solution.py:17
  833.9 13.1 %collective-permute-start.27 = (f32[16,7,256]{2,1,0:T(8,128)S(1)}, f32[16,7,256]{2,1,0:T(8,128)S(1)}, u32[]{:S(2)}, u32[]{:S(2)}) collective-permute-start(f32[16,7,256]{2,1,0:T(8,128)S(1)} %get-tuple-element.10), channel_id=1, source_target_pairs={{1,0},{2,1},{3,2},{4,3},{5,4},{6,5},{7,6},{8,7},{9,8},{10,9},{11,1... | collective-permute-start | bytes 344072 | tf_op jit(solution)/shard_map/ppermute | solution.py:19
  839.8 48.9 %collective-permute-start.46 = (f32[16,64,256]{2,1,0:T(8,128)}, f32[16,64,256]{2,1,0:T(8,128)S(1)}, u32[]{:S(2)}, u32[]{:S(2)}) collective-permute-start(f32[16,64,256]{2,1,0:T(8,128)} %collective-permute-done.45), channel_id=1, source_target_pairs={{0,64},{16,80},{32,96},{48,112},{64,0},{80,16},{96,32},{112,48},{1... | collective-permute-start | bytes 3145736 | tf_op jit(solution)/shard_map/ppermute | solution.py:29
  869.0 71.2 %collective-permute-start.28 = (f32[7,64,256]{2,1,0:T(8,128)S(1)}, f32[7,64,256]{2,1,0:T(8,128)S(1)}, u32[]{:S(2)}, u32[]{:S(2)}) collective-permute-start(f32[7,64,256]{2,1,0:T(8,128)S(1)} %get-tuple-element.7), channel_id=1, source_target_pairs={{0,16},{16,32},{32,48},{48,64},{64,80},{80,96},{96,112},{112,128},... | collective-permute-start | bytes 1376264 | tf_op jit(solution)/shard_map/ppermute | solution.py:17
  871.6 68.6 %collective-permute-start.29 = (f32[7,64,256]{2,1,0:T(8,128)S(1)}, f32[7,64,256]{2,1,0:T(8,128)S(1)}, u32[]{:S(2)}, u32[]{:S(2)}) collective-permute-start(f32[7,64,256]{2,1,0:T(8,128)S(1)} %get-tuple-element.8), channel_id=1, source_target_pairs={{16,0},{32,16},{48,32},{64,48},{80,64},{96,80},{112,96},{128,112},... | collective-permute-start | bytes 1376264 | tf_op jit(solution)/shard_map/ppermute | solution.py:19
  888.6 86.3 %collective-permute-start.47 = (f32[16,64,256]{2,1,0:T(8,128)S(1)}, f32[16,64,256]{2,1,0:T(8,128)S(1)}, u32[]{:S(2)}, u32[]{:S(2)}) collective-permute-start(f32[16,64,256]{2,1,0:T(8,128)S(1)} %collective-permute-done.46), channel_id=1, source_target_pairs={{0,128},{16,144},{32,160},{48,176},{64,192},{80,208},{96,224},{112... | collective-permute-start | bytes 3145736 | tf_op jit(solution)/shard_map/ppermute | solution.py:29
  951.5 6.3 collective-permute-start.30
  953.4 6.1 collective-permute-start.31
  (7 other events, 326.2 us)
where the time goes:
time: 1010 us; the launch traced here: 998 us
  waiting for transfers between devices  435 us (43%)
  starting transfers between devices  280 us (28%)
  matrix products  175 us (17%)
  other arithmetic  95.4 us (9%)
  local copies, waits for them, and re-layouts  10.9 us (1%)
    ppermute x16, waiting for transfers between devices, swapped(): return lax.ppermute(value, axis, pairs)  308 us
    dot_general x8, matrix products, apply_blur(): jnp.dot(flat, band_matrix(kernels[2], width), precision=lax.Precision.HIG...  175 us
    ppermute x16, starting transfers between devices, swapped(): return lax.ppermute(value, axis, pairs)  154 us
    add x8, other arithmetic, taps_along(): total + weights[tap_index] * lax.slice_in_dim(padded, tap_index, tap_inde...  95.2 us
    ppermute x16, waiting for transfers between devices, with_halo(): lax.ppermute(tail, axis, [(i, (i + 1) % count) for i in range(ends)])  89.1 us
    ppermute x16, starting transfers between devices, with_halo(): lax.ppermute(head, axis, [((i + 1) % count, i) for i in range(ends)])  85.1 us
    ppermute x16, starting transfers between devices, with_halo(): lax.ppermute(tail, axis, [(i, (i + 1) % count) for i in range(ends)])  41.3 us
    ppermute x16, waiting for transfers between devices, with_halo(): lax.ppermute(head, axis, [((i + 1) % count, i) for i in range(ends)])  37.4 us
  transfers between devices with their start and end apart: 48, of which 29 were waited for; matrix products, arithmetic and copies ran while one was open for 10% of the time, Pallas kernels for 0%

commit v1 on v0

v1 whole, which is shorter than its diff:
```python
import functools

import jax
import jax.numpy as jnp
from jax import lax
from jax.experimental import pallas as pl
from jax.experimental.pallas import tpu as pltpu
from jax.sharding import PartitionSpec as P

EDGE = 8
CHUNK = 4
F32 = jnp.float32
BF16 = jnp.bfloat16


def moved(value, axis, target):
    count = lax.axis_size(axis)
    pairs = [(i, target(i)) for i in range(count) if 0 <= target(i) < count]
    return lax.ppermute(value, axis, pairs)


def split(value):
    high = value.astype(BF16)
    low = (value - high.astype(F32)).astype(BF16)
    return high, low


def split_outside(value):
    high = lax.reduce_precision(value, 8, 7)
    return high.astype(BF16), (value - high).astype(BF16)


def band(weights, rows, columns, shift):
    offsets = jnp.arange(rows)[:, None] - jnp.arange(columns)[None, :] + shift
    matrix = jnp.zeros((rows, columns), F32)
    for tap in range(weights.shape[0]):
        matrix = matrix + jnp.where(offsets == tap, weights[tap], 0.0)
    return matrix


def filters(kernels, rows, width):
    taps = kernels.shape[1]
    half = taps // 2
    forward = band(kernels[1], rows + 2 * EDGE, rows, half - EDGE).T
    lefts = []
    for matrix in (forward, forward.T):
        high, low = split_outside(matrix)
        lefts.append(jnp.concatenate([high, high, low], axis=1))
    across = band(kernels[2], width, width, half)
    rights = []
    for matrix in (across, across.T):
        high, low = split_outside(matrix)
        rights.append(jnp.stack([high, low]))
    return kernels[0], lefts[0], lefts[1], rights[0], rights[1]


def gather_planes(taps, planes, depth):
    outs = []
    for z in range(depth):
        total = taps[0] * planes[z]
        for t in range(1, len(taps)):
            total = total + taps[t] * planes[z + t]
        outs.append(total)
    return outs


def scatter_planes(tap_lists, plane_lists):
    depth = len(plane_lists[0])
    count = len(tap_lists[0])
    outs = []
    for o in range(depth + count - 1):
        total = None
        for taps, planes in zip(tap_lists, plane_lists):
            for z in range(max(0, o - count + 1), min(depth, o + 1)):
                term = taps[o - z] * planes[z]
                total = term if total is None else total + term
        outs.append(total)
    return outs


def z_forward(taps, field, out_ref):
    center, z_low, z_high, y_low, y_high = field
    depth, rows, width = center.shape
    reach = z_low.shape[0]

    def strip(first_row, planes_of):
        for lane in range(0, width, 128):
            lanes = pl.ds(lane, 128)
            planes = planes_of(lanes)
            for z, total in enumerate(gather_planes(taps, planes, depth)):
                out_ref[z, pl.ds(first_row, EDGE), lanes] = total

    def inner(step, carry):
        row = pl.multiple_of(step * EDGE, EDGE)

        def planes_of(lanes):
            window = pl.ds(row, EDGE)
            return (
                [z_low[z, window, lanes] for z in range(reach)]
                + [center[z, window, lanes] for z in range(depth)]
                + [z_high[z, window, lanes] for z in range(reach)]
            )

        strip(row + EDGE, planes_of)
        return carry

    lax.fori_loop(0, rows // EDGE, inner, 0)
    strip(0, lambda lanes: [y_low[z, :, lanes] for z in range(depth + 2 * reach)])
    strip(rows + EDGE, lambda lanes: [y_high[z, :, lanes] for z in range(depth + 2 * reach)])


def left_product(matrix, value):
    high, low = split(value)
    stacked = jnp.concatenate([high, low, high], axis=0)
    return jnp.dot(matrix, stacked, preferred_element_type=F32)


def right_product(value, matrix_ref):
    high, low = split(value)
    dot = functools.partial(jnp.dot, preferred_element_type=F32)
    return dot(high, matrix_ref[0]) + dot(low, matrix_ref[0]) + dot(high, matrix_ref[1])


def blurred_chunk(along_z, first, left, right):
    rows = [left_product(left[...], along_z[first + k]) for k in range(CHUNK)]
    return right_product(jnp.concatenate(rows, axis=0), right)


def back_chunk(ratio, first, left, right, out_ref):
    rows = out_ref.shape[1] - 2 * EDGE
    across = right_product(ratio, right)
    for k in range(CHUNK):
        out_ref[first + k] = left_product(left[...], across[k * rows : (k + 1) * rows])


def z_back(tap_lists, sources, outs, extra):
    center, y_low, y_high = outs
    depth = sources[0].shape[0]
    rows, width = center.shape[1:]

    def strip(source_row, out_ref, extra_ref, out_row):
        for lane in range(0, width, 128):
            lanes = pl.ds(lane, 128)
            plane_lists = [
                [ref[z, pl.ds(source_row, EDGE), lanes] for z in range(depth)] for ref in sources
            ]
            for o, total in enumerate(scatter_planes(tap_lists, plane_lists)):
                if extra_ref is not None:
                    total = total + extra_ref[o, pl.ds(out_row, EDGE), lanes]
                out_ref[o, pl.ds(out_row, EDGE), lanes] = total

    def inner(step, carry):
        row = pl.multiple_of(step * EDGE, EDGE)
        strip(row + EDGE, center, extra and extra[0], row)
        return carry

    lax.fori_loop(0, rows // EDGE, inner, 0)
    strip(0, y_low, extra and extra[1], 0)
    strip(rows + EDGE, y_high, extra and extra[2], 0)


def read_taps(ref, view, flip):
    taps = [ref[view, t] for t in range(ref.shape[1])]
    return taps[::-1] if flip else taps


def first_kernel(taps_ref, *refs):
    field, refs = refs[:5], refs[5:]
    view_one = refs[0]
    left_one, back_left_one, right_one, back_right_one, left_two, right_two = refs[1:7]
    partial, blurred_two = refs[7:10], refs[10]
    along_z, back = refs[11:13]
    depth, rows, _ = view_one.shape
    one, two = read_taps(taps_ref, 0, False), read_taps(taps_ref, 1, True)
    z_forward(one, field, along_z)
    for first in range(0, depth, CHUNK):
        blurred = blurred_chunk(along_z, first, left_one, right_one)
        seen = jnp.concatenate([view_one[first + k] for k in range(CHUNK)], axis=0)
        back_chunk(seen / blurred, first, back_left_one, back_right_one, back)
    z_back([one], [back], partial, None)
    z_forward(two, field, along_z)
    for first in range(0, depth, CHUNK):
        blurred = blurred_chunk(along_z, first, left_two, right_two)
        for k in range(CHUNK):
            blurred_two[first + k] = blurred[k * rows : (k + 1) * rows]


def second_kernel(taps_ref, blurred_two, view_two, back_left, back_right, *refs):
    extra, outs, back = refs[:3], refs[3:6], refs[6]
    depth = view_two.shape[0]
    for first in range(0, depth, CHUNK):
        ratio = jnp.concatenate(
            [view_two[depth - 1 - first - k] / blurred_two[first + k] for k in range(CHUNK)],
            axis=0,
        )
        back_chunk(ratio, first, back_left, back_right, back)
    z_back([read_taps(taps_ref, 1, True)], [back], outs, extra)


def both_kernel(taps_ref, *refs):
    field, refs = refs[:5], refs[5:]
    views, refs = refs[:2], refs[2:]
    matrices = (refs[:4], refs[4:8])
    outs, along_z, backs = refs[8:11], refs[11], refs[12:14]
    depth = views[0].shape[0]
    taps = [read_taps(taps_ref, 0, False), read_taps(taps_ref, 1, True)]
    for v in range(2):
        left, back_left, right, back_right = matrices[v]
        z_forward(taps[v], field, along_z)
        for first in range(0, depth, CHUNK):
            blurred = blurred_chunk(along_z, first, left, right)
            planes = [first + k if v == 0 else depth - 1 - first - k for k in range(CHUNK)]
            seen = jnp.concatenate([views[v][z] for z in planes], axis=0)
            back_chunk(seen / blurred, first, back_left, back_right, backs[v])
    z_back(taps, backs, outs, None)


def call(kernel, arrays, outs, scratch):
    vmem = pl.BlockSpec(memory_space=pltpu.VMEM)
    return pl.pallas_call(
        kernel,
        out_shape=[jax.ShapeDtypeStruct(shape, F32) for shape in outs],
        in_specs=[pl.BlockSpec(memory_space=pltpu.SMEM)] + [vmem] * (len(arrays) - 1),
        out_specs=[vmem] * len(outs),
        scratch_shapes=[pltpu.VMEM(shape, F32) for shape in scratch],
    )(*arrays)


def row_halos(center, z_low, z_high):
    def rows(window):
        return jnp.concatenate([z_low[:, window], center[:, window], z_high[:, window]], axis=0)

    low = moved(rows(slice(-EDGE, None)), "xy", lambda i: i + 1)
    high = moved(rows(slice(None, EDGE)), "xy", lambda i: i - 1)
    return low, high


def rows_added(partial):
    center, low, high = partial
    from_below = moved(high, "xy", lambda i: i + 1)
    from_above = moved(low, "xy", lambda i: i - 1)
    rows = center.shape[1]
    return jnp.concatenate(
        [
            center[:, :EDGE] + from_below,
            center[:, EDGE : rows - EDGE],
            center[:, rows - EDGE :] + from_above,
        ],
        axis=1,
    )


def local(view_one, view_two, estimate, psf):
    depth, rows, width = estimate.shape
    kernels = psf / jnp.sum(psf, axis=2, keepdims=True)
    reach = psf.shape[2] // 2
    z_taps = kernels[:, 0]
    one = filters(kernels[0], rows, width)[1:]
    two = filters(kernels[1], rows, width)[1:]

    z_low = moved(estimate[depth - reach :], "gz", lambda i: i + 1)
    z_high = moved(estimate[:reach], "gz", lambda i: i - 1)
    count = lax.axis_size("gz")
    view_two = moved(view_two, "gz", lambda i: count - 1 - i)

    full = depth + 2 * reach
    partial_shapes = [(full, rows, width), (full, EDGE, width), (full, EDGE, width)]
    tall = (depth, rows + 2 * EDGE, width)

    y_low, y_high = row_halos(estimate, z_low, z_high)
    field = (estimate, z_low, z_high, y_low, y_high)
    *partial, blurred_two = call(
        first_kernel,
        (z_taps, *field, view_one, *one, two[0], two[2]),
        partial_shapes + [view_one.shape],
        [tall, tall],
    )
    partial = call(
        second_kernel,
        (z_taps, blurred_two, view_two, two[1], two[3], *partial),
        partial_shapes,
        [tall],
    )
    total = rows_added(partial)
    overlap = 2 * reach
    below = total[:overlap] + moved(total[full - overlap :], "gz", lambda i: i + 1)
    above = total[full - overlap :] + moved(total[:overlap], "gz", lambda i: i - 1)
    z_low = z_low * below[:reach] * 0.5
    z_high = z_high * above[reach:] * 0.5
    estimate = (
        estimate
        * jnp.concatenate([below[reach:], total[overlap : full - overlap], above[:reach]], axis=0)
        * 0.5
    )

    y_low, y_high = row_halos(estimate, z_low, z_high)
    field = (estimate, z_low, z_high, y_low, y_high)
    partial = call(
        both_kernel,
        (z_taps, *field, view_one, view_two, *one, *two),
        partial_shapes,
        [tall, tall, tall],
    )
    total = rows_added(partial)
    from_below = moved(total[full - reach :], "gz", lambda i: i + 1)
    from_above = moved(total[:reach], "gz", lambda i: i - 1)
    center = total[reach : full - reach]
    center = jnp.concatenate(
        [
            center[:reach] + from_below,
            center[reach : depth - reach],
            center[depth - reach :] + from_above,
        ],
        axis=0,
    )
    return estimate * center * 0.5


def solution(mesh):
    return jax.shard_map(
        local,
        mesh=mesh,
        in_specs=(P("gz", "xy", None), P("gz", "xy", None), P("gz", "xy", None), P()),
        out_specs=P("gz", "xy", None),
        check_vma=False,
    )
```

time: 1010 us -> 264 us (0.26)
  the two profiles are of different devices: /device:TPU:30 before, /device:TPU:39 now
where the time goes in v1:
time: 264 us; the launch traced here: 262 us
  other arithmetic  88.8 us (34%)
  waiting for transfers between devices  78.2 us (30%)
  starting transfers between devices  49.5 us (19%)
  Pallas kernels  32.3 us (12%)
  local copies, waits for them, and re-layouts  12.6 us (5%)
    ppermute x15, waiting for transfers between devices, moved(): return lax.ppermute(value, axis, pairs)  78.2 us
    convert_element_type x8, other arithmetic, split_outside(): return (high.astype(BF16), (value - high).astype(BF16))  76.9 us
    ppermute x15, starting transfers between devices, moved(): return lax.ppermute(value, axis, pairs)  49.5 us
    pallas_call x3, Pallas kernels, call(): pl.pallas_call(kernel, out_shape=[jax.ShapeDtypeStruct(shape, F32) for sh...  32.3 us
  transfers between devices with their start and end apart: 15, of which 8 were waited for; matrix products, arithmetic and copies ran while one was open for 35% of the time, Pallas kernels for 4%

profile of v1, /device:TPU:39, one launch (start us, length us, event | category | flops | bytes accessed | tf_op | source)
XLA Modules:
  0.0 261.9 jit_solution(11129934404147094791)
XLA Ops:
  0.0 1.2 fusion.82
  1.2 4.4 %collective-permute-start.1 = (f32[7,64,256]{2,1,0:T(8,128)S(1)}, f32[7,64,256]{2,1,0:T(8,128)S(1)}, u32[]{:S(2)}, u32[]{:S(2)}) collective-permute-start(f32[7,64,256]{2,1,0:T(8,128)S(1)} %get-tuple-element.37), channel_id=1, source_target_pairs={{16,0},{32,16},{48,32},{64,48},{80,64},{96,80},{112,96},{128,112},... | collective-permute-start | bytes 1376264 | tf_op jit(solution)/shard_map/ppermute | solution.py:19
  5.6 2.4 collective-permute-start
  8.0 9.2 %collective-permute-start.4 = (f32[16,64,256]{2,1,0:T(8,128)}, f32[16,64,256]{2,1,0:T(8,128)S(1)}, u32[]{:S(2)}, u32[]{:S(2)}) collective-permute-start(f32[16,64,256]{2,1,0:T(8,128)} %param.5), channel_id=1, source_target_pairs={{0,240},{16,224},{32,208},{48,192},{64,176},{80,160},{96,144},{112... | collective-permute-start | bytes 3145736 | tf_op jit(solution)/shard_map/ppermute | solution.py:19
  17.2 0.8 reduce_sum.9
  18.0 0.8 broadcast_divide_fusion
  21.6 9.4 %reduce-precision_convert_fusion.7 = (bf16[64,80]{1,0:T(8,128)(2,1)S(1)}, bf16[64,80]{1,0:T(8,128)(2,1)S(1)}) fusion(f32[]{:T(128)} %bitcast.15, f32[]{:T(128)} %bitcast.14, f32[]{:T(128)} %bitcast.13, f32[]{:T(128)} %bitcast.12, f32[]{:T(128)} %bitcast.11, f32[]{:T(128)} %bitcast.10, f32[]{:T(128)} %bitcast.9, f32[]{:T(128)} %bitcast.8, f32[]{:T(128)} %bitcast.7, ...), kind=kLoop, calls=%fused_computation.91 | loop fusion | flops 256000 | bytes 20540 | tf_op jit(solution)/shard_map/convert_element_type | solution.py:30
  31.0 9.4 %reduce-precision_convert_fusion.5 = (bf16[80,64]{1,0:T(8,128)(2,1)S(1)}, bf16[80,64]{1,0:T(8,128)(2,1)S(1)}) fusion(f32[]{:T(128)} %bitcast.15, f32[]{:T(128)} %bitcast.14, f32[]{:T(128)} %bitcast.13, f32[]{:T(128)} %bitcast.12, f32[]{:T(128)} %bitcast.11, f32[]{:T(128)} %bitcast.10, f32[]{:T(128)} %bitcast.9, f32[]{:T(128)} %bitcast.8, f32[]{:T(128)} %bitcast.7, ...), kind=kLoop, calls=%fused_computation.87 | loop fusion | flops 256000 | bytes 20540 | tf_op jit(solution)/shard_map/convert_element_type | solution.py:30
  40.5 9.4 %reduce-precision_convert_fusion.6 = (bf16[64,80]{1,0:T(8,128)(2,1)S(1)}, bf16[64,80]{1,0:T(8,128)(2,1)S(1)}) fusion(f32[]{:T(128)} %bitcast.45, f32[]{:T(128)} %bitcast.44, f32[]{:T(128)} %bitcast.43, f32[]{:T(128)} %bitcast.42, f32[]{:T(128)} %bitcast.41, f32[]{:T(128)} %bitcast.40, f32[]{:T(128)} %bitcast.39, f32[]{:T(128)} %bitcast.38, f32[]{:T(128)} %bitcast.37, ...), kind=kLoop, calls=%fused_computation.89 | loop fusion | flops 256000 | bytes 20540 | tf_op jit(solution)/shard_map/convert_element_type | solution.py:30
  49.9 9.4 %reduce-precision_convert_fusion.4 = (bf16[80,64]{1,0:T(8,128)(2,1)S(1)}, bf16[80,64]{1,0:T(8,128)(2,1)S(1)}) fusion(f32[]{:T(128)} %bitcast.45, f32[]{:T(128)} %bitcast.44, f32[]{:T(128)} %bitcast.43, f32[]{:T(128)} %bitcast.42, f32[]{:T(128)} %bitcast.41, f32[]{:T(128)} %bitcast.40, f32[]{:T(128)} %bitcast.39, f32[]{:T(128)} %bitcast.38, f32[]{:T(128)} %bitcast.37, ...), kind=kLoop, calls=%fused_computation.85 | loop fusion | flops 256000 | bytes 20540 | tf_op jit(solution)/shard_map/convert_element_type | solution.py:30
  59.3 9.7 %reduce-precision_convert_fusion.2 = (bf16[1,256,256]{2,1,0:T(8,128)(2,1)S(1)}, bf16[1,256,256]{2,1,0:T(8,128)(2,1)S(1)}) fusion(f32[]{:T(128)} %bitcast.30, f32[]{:T(128)} %bitcast.29, f32[]{:T(128)} %bitcast.28, f32[]{:T(128)} %bitcast.27, f32[]{:T(128)} %bitcast.26, f32[]{:T(128)} %bitcast.25, f32[]{:T(128)} %bitcast.24, f32[]{:T(128)} %bitcast.23, ...), kind=kLoop, calls=%fused_computation.29 | loop fusion | flops 6291456 | bytes 262204 | tf_op jit(solution)/shard_map/convert_element_type | solution.py:30
  69.0 9.7 %fusion.11 = (bf16[1,256,256]{2,1,0:T(8,128)(2,1)S(1)}, bf16[1,256,256]{2,1,0:T(8,128)(2,1)S(1)}) fusion(f32[]{:T(128)} %bitcast.30, f32[]{:T(128)} %bitcast.29, f32[]{:T(128)} %bitcast.28, f32[]{:T(128)} %bitcast.27, f32[]{:T(128)} %bitcast.26, f32[]{:T(128)} %bitcast.25, f32[]{:T(128)} %bitcast.24, f32[]{:T(128)} %bitcast.23, f32[]{:T(128)} %bitcast.22, ...), kind=kLoop, calls=%fused_computation.32 | loop fusion | flops 6422528 | bytes 262204 | tf_op jit(solution)/shard_map/convert_element_type | solution.py:30
  78.8 9.8 %reduce-precision_convert_fusion = (bf16[1,256,256]{2,1,0:T(8,128)(2,1)S(1)}, bf16[1,256,256]{2,1,0:T(8,128)(2,1)S(1)}) fusion(f32[]{:T(128)} %bitcast.60, f32[]{:T(128)} %bitcast.59, f32[]{:T(128)} %bitcast.58, f32[]{:T(128)} %bitcast.57, f32[]{:T(128)} %bitcast.56, f32[]{:T(128)} %bitcast.55, f32[]{:T(128)} %bitcast.54, f32[]{:T(128)} %bitcast.53, ...), kind=kLoop, calls=%fused_computation.25 | loop fusion | flops 6291456 | bytes 262204 | tf_op jit(solution)/shard_map/convert_element_type | solution.py:30
  88.6 9.9 %fusion.13 = (bf16[1,256,256]{2,1,0:T(8,128)(2,1)S(1)}, bf16[1,256,256]{2,1,0:T(8,128)(2,1)S(1)}) fusion(f32[]{:T(128)} %bitcast.60, f32[]{:T(128)} %bitcast.59, f32[]{:T(128)} %bitcast.58, f32[]{:T(128)} %bitcast.57, f32[]{:T(128)} %bitcast.56, f32[]{:T(128)} %bitcast.55, f32[]{:T(128)} %bitcast.54, f32[]{:T(128)} %bitcast.53, f32[]{:T(128)} %bitcast.52, ...), kind=kLoop, calls=%fused_computation.34 | loop fusion | flops 6422528 | bytes 262204 | tf_op jit(solution)/shard_map/convert_element_type | solution.py:30
  99.9 0.7 pad_maximum_fusion.3.refs_8_.refs_9_
  100.7 0.7 pad_maximum_fusion.4.refs_9_.refs_10_
  101.4 0.7 pad_maximum_fusion.5.refs_11_.refs_13_
  102.1 1.0 fusion.81
  103.1 0.7 pad_maximum_fusion.6.back_right.refs_14_
  104.6 3.7 %collective-permute-start.2 = (f32[30,8,256]{2,1,0:T(8,128)S(1)}, f32[30,8,256]{2,1,0:T(8,128)S(1)}, u32[]{:S(2)}, u32[]{:S(2)}) collective-permute-start(f32[30,8,256]{2,1,0:T(8,128)S(1)} %pad_maximum_fusion.7), channel_id=1, source_target_pairs={{0,1},{1,2},{2,3},{3,4},{4,5},{5,6},{6,7},{7,8},{8,9},{9,10},{10,1... | collective-permute-start | bytes 737288 | tf_op jit(solution)/shard_map/ppermute | solution.py:19
  108.4 1.9 collective-permute-start.3
  111.6 5.0 %collective-permute-done.3.refs_4_ = f32[30,8,256]{2,1,0:T(8,128)S(1)} collective-permute-done((f32[30,8,256]{2,1,0:T(8,128)S(1)}, f32[30,8,256]{2,1,0:T(8,128)S(1)}, u32[]{:S(2)}, u32[]{:S(2)}) %collective-permute-start.3) | collective-permute-done | bytes 245792 | tf_op jit(solution)/shard_map/ppermute | solution.py:19
  117.3 10.8 %shard_map.46 = (f32[30,64,256]{2,1,0:T(8,128)}, f32[30,8,256]{2,1,0:T(8,128)}, f32[30,8,256]{2,1,0:T(8,128)}, f32[16,64,256]{2,1,0:T(8,128)}) custom-call(f32[2,15]{1,0:T(2,128)} %slice_bitcast_fusion.taps_ref, f32[16,64,256]{2,1,0:T(8,128)} %refs_0_.1, f32[7,64,256]{2,1,0:T(8,128)} %copy-done.6, f32[7,64,256]{2,1,0:T(8,128)} %copy-done.4, ...), custom_call_target="tpu_custom_call" | custom-call | tf_op jit(solution)/shard_map/pallas_call | solution.py:220
  128.1 1.0 copy-done.3
  129.1 6.5 %shard_map.47 = (f32[30,64,256]{2,1,0:T(8,128)}, f32[30,8,256]{2,1,0:T(8,128)}, f32[30,8,256]{2,1,0:T(8,128)}) custom-call(f32[2,15]{1,0:T(2,128)} %slice_bitcast_fusion.taps_ref, f32[16,64,256]{2,1,0:T(8,128)} %get-tuple-element.15.blurred_two, f32[16,64,256]{2,1,0:T(8,128)} %copy-done.3, bf16[80,192]{1,0:T(8,128)(2,1)} %pad_maximum_fusion.12.back_left.refs_12_, ...), custom_call_target="tpu_custom_call" | custom-call | tf_op jit(solution)/shard_map/pallas_call | solution.py:220
  135.6 1.9 collective-permute-start.5
  137.5 2.4 collective-permute-start.6
  139.9 1.5 slice.489
  141.4 5.7 %collective-permute-done.6 = f32[30,8,256]{2,1,0:T(8,128)S(1)} collective-permute-done((f32[30,8,256]{2,1,0:T(8,128)}, f32[30,8,256]{2,1,0:T(8,128)S(1)}, u32[]{:S(2)}, u32[]{:S(2)}) %collective-permute-start.6) | collective-permute-done | bytes 245792 | tf_op jit(solution)/shard_map/ppermute | solution.py:19
  147.1 1.1 slice_add_fusion.4
  148.6 1.9 collective-permute-start.7
  150.5 5.9 %collective-permute-start.8 = (f32[14,64,256]{2,1,0:T(8,128)S(1)}, f32[14,64,256]{2,1,0:T(8,128)S(1)}, u32[]{:S(2)}, u32[]{:S(2)}) collective-permute-start(f32[14,64,256]{2,1,0:T(8,128)S(1)} %get-tuple-element.30), channel_id=1, source_target_pairs={{16,0},{32,16},{48,32},{64,48},{80,64},{96,80},{112,96},{128,112},... | collective-permute-start | bytes 2752520 | tf_op jit(solution)/shard_map/ppermute | solution.py:19
  156.4 33.0 %collective-permute-done.7 = f32[14,64,256]{2,1,0:T(8,128)S(1)} collective-permute-done((f32[14,64,256]{2,1,0:T(8,128)S(1)}, f32[14,64,256]{2,1,0:T(8,128)S(1)}, u32[]{:S(2)}, u32[]{:S(2)}) %collective-permute-start.7) | collective-permute-done | bytes 917536 | tf_op jit(solution)/shard_map/ppermute | solution.py:19
  189.5 4.8 %collective-permute-done.8 = f32[14,64,256]{2,1,0:T(8,128)S(1)} collective-permute-done((f32[14,64,256]{2,1,0:T(8,128)S(1)}, f32[14,64,256]{2,1,0:T(8,128)S(1)}, u32[]{:S(2)}, u32[]{:S(2)}) %collective-permute-start.8) | collective-permute-done | bytes 917536 | tf_op jit(solution)/shard_map/ppermute | solution.py:19
  194.8 0.9 copy-done.5
  196.6 1.9 collective-permute-start.9
  198.5 2.6 collective-permute-start.10
  201.6 5.7 %collective-permute-done.10.refs_4_ = f32[30,8,256]{2,1,0:T(8,128)S(1)} collective-permute-done((f32[30,8,256]{2,1,0:T(8,128)S(1)}, f32[30,8,256]{2,1,0:T(8,128)S(1)}, u32[]{:S(2)}, u32[]{:S(2)}) %collective-permute-start.10) | collective-permute-done | bytes 245792 | tf_op jit(solution)/shard_map/ppermute | solution.py:19
  208.0 15.0 %shard_map.48 = (f32[30,64,256]{2,1,0:T(8,128)}, f32[30,8,256]{2,1,0:T(8,128)}, f32[30,8,256]{2,1,0:T(8,128)}) custom-call(f32[2,15]{1,0:T(2,128)} %slice_bitcast_fusion.taps_ref, f32[16,64,256]{2,1,0:T(8,128)} %copy-done, f32[7,64,256]{2,1,0:T(8,128)} %copy-done.8, f32[7,64,256]{2,1,0:T(8,128)} %copy-done.9, f32[30,8,256]{2,1,0:T(8,128)} %copy-done.10, ...), custom_call_target="tpu_custom_call" | custom-call | tf_op jit(solution)/shard_map/pallas_call | solution.py:220
  223.0 1.9 collective-permute-start.11
  224.9 2.4 collective-permute-start.12
  227.3 1.5 slice.505
  228.8 10.4 %collective-permute-done.12 = f32[30,8,256]{2,1,0:T(8,128)S(1)} collective-permute-done((f32[30,8,256]{2,1,0:T(8,128)}, f32[30,8,256]{2,1,0:T(8,128)S(1)}, u32[]{:S(2)}, u32[]{:S(2)}) %collective-permute-start.12) | collective-permute-done | bytes 245792 | tf_op jit(solution)/shard_map/ppermute | solution.py:19
  239.2 1.1 slice_add_fusion.2
  240.3 1.9 collective-permute-start.14
  242.5 5.0 %collective-permute-start.13 = (f32[7,64,256]{2,1,0:T(8,128)S(1)}, f32[7,64,256]{2,1,0:T(8,128)S(1)}, u32[]{:S(2)}, u32[]{:S(2)}) collective-permute-start(f32[7,64,256]{2,1,0:T(8,128)S(1)} %slice.590), channel_id=1, source_target_pairs={{0,16},{16,32},{32,48},{48,64},{64,80},{80,96},{96,112},{112,128},... | collective-permute-start | bytes 1376264 | tf_op jit(solution)/shard_map/ppermute | solution.py:19
  247.5 13.1 %collective-permute-done.14 = f32[7,64,256]{2,1,0:T(8,128)S(1)} collective-permute-done((f32[7,64,256]{2,1,0:T(8,128)S(1)}, f32[7,64,256]{2,1,0:T(8,128)S(1)}, u32[]{:S(2)}, u32[]{:S(2)}) %collective-permute-start.14) | collective-permute-done | bytes 458784 | tf_op jit(solution)/shard_map/ppermute | solution.py:19
  260.8 1.1 fusion.3
  (63 shorter events, 10.1 us)
Async XLA Ops:
  1.2 103.3 %collective-permute-start.1 = (f32[7,64,256]{2,1,0:T(8,128)S(1)}, f32[7,64,256]{2,1,0:T(8,128)S(1)}, u32[]{:S(2)}, u32[]{:S(2)}) collective-permute-start(f32[7,64,256]{2,1,0:T(8,128)S(1)} %get-tuple-element.37), channel_id=1, source_target_pairs={{16,0},{32,16},{48,32},{64,48},{80,64},{96,80},{112,96},{128,112},... | collective-permute-start | bytes 1376264 | tf_op jit(solution)/shard_map/ppermute | solution.py:19
  5.6 99.0 %collective-permute-start = (f32[7,64,256]{2,1,0:T(8,128)S(1)}, f32[7,64,256]{2,1,0:T(8,128)S(1)}, u32[]{:S(2)}, u32[]{:S(2)}) collective-permute-start(f32[7,64,256]{2,1,0:T(8,128)S(1)} %get-tuple-element.38), channel_id=1, source_target_pairs={{0,16},{16,32},{32,48},{48,64},{64,80},{80,96},{96,112},{112,128},... | collective-permute-start | bytes 1376264 | tf_op jit(solution)/shard_map/ppermute | solution.py:19
  8.0 120.0 %collective-permute-start.4 = (f32[16,64,256]{2,1,0:T(8,128)}, f32[16,64,256]{2,1,0:T(8,128)S(1)}, u32[]{:S(2)}, u32[]{:S(2)}) collective-permute-start(f32[16,64,256]{2,1,0:T(8,128)} %param.5), channel_id=1, source_target_pairs={{0,240},{16,224},{32,208},{48,192},{64,176},{80,160},{96,144},{112... | collective-permute-start | bytes 3145736 | tf_op jit(solution)/shard_map/ppermute | solution.py:19
  104.6 12.0 %copy-start.4 = (f32[7,64,256]{2,1,0:T(8,128)}, f32[7,64,256]{2,1,0:T(8,128)S(1)}, u32[]{:S(2)}) copy-start(f32[7,64,256]{2,1,0:T(8,128)S(1)} %collective-permute-done.1.refs_2_) | copy-start | bytes 1376260
  104.6 11.9 %copy-start.6 = (f32[7,64,256]{2,1,0:T(8,128)}, f32[7,64,256]{2,1,0:T(8,128)S(1)}, u32[]{:S(2)}) copy-start(f32[7,64,256]{2,1,0:T(8,128)S(1)} %collective-permute-done.refs_1_) | copy-start | bytes 1376260
  104.6 6.9 %collective-permute-start.2 = (f32[30,8,256]{2,1,0:T(8,128)S(1)}, f32[30,8,256]{2,1,0:T(8,128)S(1)}, u32[]{:S(2)}, u32[]{:S(2)}) collective-permute-start(f32[30,8,256]{2,1,0:T(8,128)S(1)} %pad_maximum_fusion.7), channel_id=1, source_target_pairs={{0,1},{1,2},{2,3},{3,4},{4,5},{5,6},{6,7},{7,8},{8,9},{9,10},{10,1... | collective-permute-start | bytes 737288 | tf_op jit(solution)/shard_map/ppermute | solution.py:19
  108.4 8.1 %collective-permute-start.3 = (f32[30,8,256]{2,1,0:T(8,128)S(1)}, f32[30,8,256]{2,1,0:T(8,128)S(1)}, u32[]{:S(2)}, u32[]{:S(2)}) collective-permute-start(f32[30,8,256]{2,1,0:T(8,128)S(1)} %pad_maximum_fusion.8), channel_id=1, source_target_pairs={{1,0},{2,1},{3,2},{4,3},{5,4},{6,5},{7,6},{8,7},{9,8},{10,9},{11,1... | collective-permute-start | bytes 737288 | tf_op jit(solution)/shard_map/ppermute | solution.py:19
  111.6 5.0 %copy-start.11 = (f32[30,8,256]{2,1,0:T(8,128)}, f32[30,8,256]{2,1,0:T(8,128)S(1)}, u32[]{:S(2)}) copy-start(f32[30,8,256]{2,1,0:T(8,128)S(1)} %collective-permute-done.2.refs_3_) | copy-start | bytes 737284
  116.5 0.7 copy-start.13
  128.1 1.0 copy-start.3
  135.6 5.8 %collective-permute-start.5 = (f32[30,8,256]{2,1,0:T(8,128)}, f32[30,8,256]{2,1,0:T(8,128)S(1)}, u32[]{:S(2)}, u32[]{:S(2)}) collective-permute-start(f32[30,8,256]{2,1,0:T(8,128)} %get-tuple-element.20), channel_id=1, source_target_pairs={{0,1},{1,2},{2,3},{3,4},{4,5},{5,6},{6,7},{7,8},{8,9},{9,10},{10,1... | collective-permute-start | bytes 737288 | tf_op jit(solution)/shard_map/ppermute | solution.py:19
  137.5 9.6 %collective-permute-start.6 = (f32[30,8,256]{2,1,0:T(8,128)}, f32[30,8,256]{2,1,0:T(8,128)S(1)}, u32[]{:S(2)}, u32[]{:S(2)}) collective-permute-start(f32[30,8,256]{2,1,0:T(8,128)} %get-tuple-element.21), channel_id=1, source_target_pairs={{1,0},{2,1},{3,2},{4,3},{5,4},{6,5},{7,6},{8,7},{9,8},{10,9},{11,1... | collective-permute-start | bytes 737288 | tf_op jit(solution)/shard_map/ppermute | solution.py:19
  148.6 40.9 %collective-permute-start.7 = (f32[14,64,256]{2,1,0:T(8,128)S(1)}, f32[14,64,256]{2,1,0:T(8,128)S(1)}, u32[]{:S(2)}, u32[]{:S(2)}) collective-permute-start(f32[14,64,256]{2,1,0:T(8,128)S(1)} %get-tuple-element.29), channel_id=1, source_target_pairs={{0,16},{16,32},{32,48},{48,64},{64,80},{80,96},{96,112},{112,128},... | collective-permute-start | bytes 2752520 | tf_op jit(solution)/shard_map/ppermute | solution.py:19
  150.5 44.1 %copy-start.7 = (f32[7,64,256]{2,1,0:T(8,128)S(1)}, f32[7,64,256]{2,1,0:T(8,128)}, u32[]{:S(2)}) copy-start(f32[7,64,256]{2,1,0:T(8,128)} %copy-done.6) | copy-start | bytes 1376260
  150.5 43.8 %collective-permute-start.8 = (f32[14,64,256]{2,1,0:T(8,128)S(1)}, f32[14,64,256]{2,1,0:T(8,128)S(1)}, u32[]{:S(2)}, u32[]{:S(2)}) collective-permute-start(f32[14,64,256]{2,1,0:T(8,128)S(1)} %get-tuple-element.30), channel_id=1, source_target_pairs={{16,0},{32,16},{48,32},{64,48},{80,64},{96,80},{112,96},{128,112},... | collective-permute-start | bytes 2752520 | tf_op jit(solution)/shard_map/ppermute | solution.py:19
  194.6 1.0 copy-start.5
  194.6 1.5 copy-start.2
  194.7 1.6 copy-start.8
  195.7 0.8 copy-start.9
  196.5 10.8 %copy-start = (f32[16,64,256]{2,1,0:T(8,128)}, f32[16,64,256]{2,1,0:T(8,128)S(1)}, u32[]{:S(2)}) copy-start(f32[16,64,256]{2,1,0:T(8,128)S(1)} %fusion.7.refs_0_) | copy-start | bytes 3145732
  196.6 5.0 %collective-permute-start.9 = (f32[30,8,256]{2,1,0:T(8,128)S(1)}, f32[30,8,256]{2,1,0:T(8,128)S(1)}, u32[]{:S(2)}, u32[]{:S(2)}) collective-permute-start(f32[30,8,256]{2,1,0:T(8,128)S(1)} %pad_maximum_fusion.9), channel_id=1, source_target_pairs={{0,1},{1,2},{2,3},{3,4},{4,5},{5,6},{6,7},{7,8},{8,9},{9,10},{10,1... | collective-permute-start | bytes 737288 | tf_op jit(solution)/shard_map/ppermute | solution.py:19
  198.5 8.8 %collective-permute-start.10 = (f32[30,8,256]{2,1,0:T(8,128)S(1)}, f32[30,8,256]{2,1,0:T(8,128)S(1)}, u32[]{:S(2)}, u32[]{:S(2)}) collective-permute-start(f32[30,8,256]{2,1,0:T(8,128)S(1)} %pad_maximum_fusion.10), channel_id=1, source_target_pairs={{1,0},{2,1},{3,2},{4,3},{5,4},{6,5},{7,6},{8,7},{9,8},{10,9},{11,1... | collective-permute-start | bytes 737288 | tf_op jit(solution)/shard_map/ppermute | solution.py:19
  201.6 5.7 %copy-start.10 = (f32[30,8,256]{2,1,0:T(8,128)}, f32[30,8,256]{2,1,0:T(8,128)S(1)}, u32[]{:S(2)}) copy-start(f32[30,8,256]{2,1,0:T(8,128)S(1)} %collective-permute-done.9.refs_3_) | copy-start | bytes 737284
  207.3 0.7 copy-start.12
  223.0 5.8 %collective-permute-start.11 = (f32[30,8,256]{2,1,0:T(8,128)}, f32[30,8,256]{2,1,0:T(8,128)S(1)}, u32[]{:S(2)}, u32[]{:S(2)}) collective-permute-start(f32[30,8,256]{2,1,0:T(8,128)} %get-tuple-element.23), channel_id=1, source_target_pairs={{0,1},{1,2},{2,3},{3,4},{4,5},{5,6},{6,7},{7,8},{8,9},{9,10},{10,1... | collective-permute-start | bytes 737288 | tf_op jit(solution)/shard_map/ppermute | solution.py:19
  224.9 14.3 %collective-permute-start.12 = (f32[30,8,256]{2,1,0:T(8,128)}, f32[30,8,256]{2,1,0:T(8,128)S(1)}, u32[]{:S(2)}, u32[]{:S(2)}) collective-permute-start(f32[30,8,256]{2,1,0:T(8,128)} %get-tuple-element.24), channel_id=1, source_target_pairs={{1,0},{2,1},{3,2},{4,3},{5,4},{6,5},{7,6},{8,7},{9,8},{10,9},{11,1... | collective-permute-start | bytes 737288 | tf_op jit(solution)/shard_map/ppermute | solution.py:19
  240.3 20.2 %collective-permute-start.14 = (f32[7,64,256]{2,1,0:T(8,128)S(1)}, f32[7,64,256]{2,1,0:T(8,128)S(1)}, u32[]{:S(2)}, u32[]{:S(2)}) collective-permute-start(f32[7,64,256]{2,1,0:T(8,128)S(1)} %pad_maximum_fusion.2), channel_id=1, source_target_pairs={{16,0},{32,16},{48,32},{64,48},{80,64},{96,80},{112,96},{128,112},... | collective-permute-start | bytes 1376264 | tf_op jit(solution)/shard_map/ppermute | solution.py:19
  242.4 18.3 %copy-start.1 = (f32[16,64,256]{2,1,0:T(8,128)S(1)}, f32[16,64,256]{2,1,0:T(8,128)}, u32[]{:S(2)}) copy-start(f32[16,64,256]{2,1,0:T(8,128)} %copy-done) | copy-start | bytes 3145732
  242.5 18.2 %collective-permute-start.13 = (f32[7,64,256]{2,1,0:T(8,128)S(1)}, f32[7,64,256]{2,1,0:T(8,128)S(1)}, u32[]{:S(2)}, u32[]{:S(2)}) collective-permute-start(f32[7,64,256]{2,1,0:T(8,128)S(1)} %slice.590), channel_id=1, source_target_pairs={{0,16},{16,32},{32,48},{48,64},{64,80},{80,96},{96,112},{112,128},... | collective-permute-start | bytes 1376264 | tf_op jit(solution)/shard_map/ppermute | solution.py:19

commit v2 on v1

--- a/solution.py
+++ b/solution.py
@@ -13,10 +13,39 @@
 BF16 = jnp.bfloat16
 
 
-def moved(value, axis, target):
-    count = lax.axis_size(axis)
-    pairs = [(i, target(i)) for i in range(count) if 0 <= target(i) < count]
-    return lax.ppermute(value, axis, pairs)
+AXES = ("gz", "xy")
+SLABS = 16
+TILES = 16
+
+
+def given(slab, tile):
+    return slab * TILES + tile
+
+
+def working(slab, tile):
+    return given(slab - slab % 2 + tile % 2, tile - tile % 2 + slab % 2)
+
+
+def moved(value, source, target, change):
+    pairs = []
+    for slab in range(SLABS):
+        for tile in range(TILES):
+            to_slab, to_tile = change(slab, tile)
+            if 0 <= to_slab < SLABS and 0 <= to_tile < TILES:
+                pairs.append((source(slab, tile), target(to_slab, to_tile)))
+    return lax.ppermute(value, AXES, pairs)
+
+
+def placed(value):
+    return moved(value, given, working, lambda slab, tile: (slab, tile))
+
+
+def along_slabs(value, step):
+    return moved(value, working, working, lambda slab, tile: (slab + step, tile))
+
+
+def along_tiles(value, step):
+    return moved(value, working, working, lambda slab, tile: (slab, tile + step))
 
 
 def split(value):
@@ -25,33 +54,46 @@
     return high, low
 
 
-def split_outside(value):
-    high = lax.reduce_precision(value, 8, 7)
-    return high.astype(BF16), (value - high).astype(BF16)
-
-
-def band(weights, rows, columns, shift):
-    offsets = jnp.arange(rows)[:, None] - jnp.arange(columns)[None, :] + shift
-    matrix = jnp.zeros((rows, columns), F32)
-    for tap in range(weights.shape[0]):
-        matrix = matrix + jnp.where(offsets == tap, weights[tap], 0.0)
-    return matrix
-
-
-def filters(kernels, rows, width):
-    taps = kernels.shape[1]
-    half = taps // 2
-    forward = band(kernels[1], rows + 2 * EDGE, rows, half - EDGE).T
-    lefts = []
-    for matrix in (forward, forward.T):
-        high, low = split_outside(matrix)
-        lefts.append(jnp.concatenate([high, high, low], axis=1))
-    across = band(kernels[2], width, width, half)
-    rights = []
-    for matrix in (across, across.T):
-        high, low = split_outside(matrix)
-        rights.append(jnp.stack([high, low]))
-    return kernels[0], lefts[0], lefts[1], rights[0], rights[1]
+def banded(taps, shape, period, axis, shift, low_from):
+    i = lax.broadcasted_iota(jnp.int32, shape, 0)
+    j = lax.broadcasted_iota(jnp.int32, shape, 1)
+    is_low = j >= low_from
+    for _ in range(2):
+        j = jnp.where(j >= period, j - period, j)
+    offset = j - i + shift if axis == 1 else i - j + shift
+    value = jnp.zeros(shape, F32)
+    for t, tap in enumerate(taps):
+        value = jnp.where(offset == t, tap, value)
+    high, low = split(value)
+    return jnp.where(is_low, low.astype(F32), high.astype(F32)).astype(BF16)
+
+
+def matrix_kernel(kernels_ref, *outs):
+    for v in range(2):
+        left, back_left, right, back_right = outs[4 * v : 4 * v + 4]
+        rows, tall = left.shape[0], back_left.shape[0]
+        width = right.shape[1]
+        along_y = [kernels_ref[v, 1, t] for t in range(kernels_ref.shape[2])]
+        along_x = [kernels_ref[v, 2, t] for t in range(kernels_ref.shape[2])]
+        half = len(along_y) // 2
+        left[...] = banded(along_y, left.shape, tall, 1, half - EDGE, 2 * tall)
+        back_left[...] = banded(along_y, back_left.shape, rows, 0, half - EDGE, 2 * rows)
+        for part in range(2):
+            low_from = width * (1 - part)
+            right[part] = banded(along_x, right.shape[1:], width, 0, half, low_from)
+            back_right[part] = banded(along_x, right.shape[1:], width, 1, half, low_from)
+
+
+def filter_matrices(kernels, rows, width):
+    tall = rows + 2 * EDGE
+    shapes = [(rows, 3 * tall), (tall, 3 * rows), (2, width, width), (2, width, width)] * 2
+    out = pl.pallas_call(
+        matrix_kernel,
+        out_shape=[jax.ShapeDtypeStruct(shape, BF16) for shape in shapes],
+        in_specs=[pl.BlockSpec(memory_space=pltpu.SMEM)],
+        out_specs=[pl.BlockSpec(memory_space=pltpu.VMEM)] * len(shapes),
+    )(kernels)
+    return out[:4], out[4:]
 
 
 def gather_planes(taps, planes, depth):
@@ -230,15 +272,15 @@
     def rows(window):
         return jnp.concatenate([z_low[:, window], center[:, window], z_high[:, window]], axis=0)
 
-    low = moved(rows(slice(-EDGE, None)), "xy", lambda i: i + 1)
-    high = moved(rows(slice(None, EDGE)), "xy", lambda i: i - 1)
+    low = along_tiles(rows(slice(-EDGE, None)), 1)
+    high = along_tiles(rows(slice(None, EDGE)), -1)
     return low, high
 
 
 def rows_added(partial):
     center, low, high = partial
-    from_below = moved(high, "xy", lambda i: i + 1)
-    from_above = moved(low, "xy", lambda i: i - 1)
+    from_below = along_tiles(high, 1)
+    from_above = along_tiles(low, -1)
     rows = center.shape[1]
     return jnp.concatenate(
         [
@@ -255,13 +297,13 @@
     kernels = psf / jnp.sum(psf, axis=2, keepdims=True)
     reach = psf.shape[2] // 2
     z_taps = kernels[:, 0]
-    one = filters(kernels[0], rows, width)[1:]
-    two = filters(kernels[1], rows, width)[1:]
-
-    z_low = moved(estimate[depth - reach :], "gz", lambda i: i + 1)
-    z_high = moved(estimate[:reach], "gz", lambda i: i - 1)
-    count = lax.axis_size("gz")
-    view_two = moved(view_two, "gz", lambda i: count - 1 - i)
+    one, two = filter_matrices(kernels, rows, width)
+    estimate = placed(estimate)
+
+    z_low = along_slabs(estimate[depth - reach :], 1)
+    z_high = along_slabs(estimate[:reach], -1)
+    view_two = moved(view_two, given, working, lambda slab, tile: (SLABS - 1 - slab, tile))
+    view_one = placed(view_one)
 
     full = depth + 2 * reach
     partial_shapes = [(full, rows, width), (full, EDGE, width), (full, EDGE, width)]
@@ -283,8 +325,8 @@
     )
     total = rows_added(partial)
     overlap = 2 * reach
-    below = total[:overlap] + moved(total[full - overlap :], "gz", lambda i: i + 1)
-    above = total[full - overlap :] + moved(total[:overlap], "gz", lambda i: i - 1)
+    below = total[:overlap] + along_slabs(total[full - overlap :], 1)
+    above = total[full - overlap :] + along_slabs(total[:overlap], -1)
     z_low = z_low * below[:reach] * 0.5
     z_high = z_high * above[reach:] * 0.5
     estimate = (
@@ -302,8 +344,8 @@
         [tall, tall, tall],
     )
     total = rows_added(partial)
-    from_below = moved(total[full - reach :], "gz", lambda i: i + 1)
-    from_above = moved(total[:reach], "gz", lambda i: i - 1)
+    from_below = along_slabs(total[full - reach :], 1)
+    from_above = along_slabs(total[:reach], -1)
     center = total[reach : full - reach]
     center = jnp.concatenate(
         [
@@ -313,7 +355,7 @@
         ],
         axis=0,
     )
-    return estimate * center * 0.5
+    return moved(estimate * center * 0.5, working, given, lambda slab, tile: (slab, tile))
 
 
 def solution(mesh):

time: 264 us -> 224 us (0.85)
  the two profiles are of different devices: /device:TPU:39 before, /device:TPU:152 now
where the time goes in v2:
time: 224 us; the launch traced here: 223 us
  waiting for transfers between devices  120 us (54%)
  starting transfers between devices  52.2 us (23%)
  Pallas kernels  35.3 us (16%)
  local copies, waits for them, and re-layouts  9.37 us (4%)
  other arithmetic  5.25 us (2%)
    ppermute x18, waiting for transfers between devices, moved(): return lax.ppermute(value, AXES, pairs)  120 us
    ppermute x18, starting transfers between devices, moved(): return lax.ppermute(value, AXES, pairs)  52.2 us
    pallas_call x3, Pallas kernels, call(): pl.pallas_call(kernel, out_shape=[jax.ShapeDtypeStruct(shape, F32) for sh...  32.3 us
    unnamed x35, local copies, waits for them, and re-layouts  5.4 us
  transfers between devices with their start and end apart: 18, of which 15 were waited for; matrix products, arithmetic and copies ran while one was open for 2% of the time, Pallas kernels for 6%

profile of v2, /device:TPU:152, one launch (start us, length us, event | category | flops | bytes accessed | tf_op | source)
XLA Modules:
  0.0 222.9 jit_solution(1077173888881758690)
XLA Ops:
  0.0 2.7 %collective-permute-start = (f32[16,64,256]{2,1,0:T(8,128)}, f32[16,64,256]{2,1,0:T(8,128)S(1)}, u32[]{:S(2)}, u32[]{:S(2)}) collective-permute-start(f32[16,64,256]{2,1,0:T(8,128)} %param.6), channel_id=1, source_target_pairs={{0,0},{1,16},{2,2},{3,18},{4,4},{5,20},{6,6},{7,22},{8,8},{9,24},{... | collective-permute-start | bytes 3145736 | tf_op jit(solution)/shard_map/ppermute | solution.py:36
  2.7 15.2 %collective-permute-done.refs_0_ = f32[16,64,256]{2,1,0:T(8,128)S(1)} collective-permute-done((f32[16,64,256]{2,1,0:T(8,128)}, f32[16,64,256]{2,1,0:T(8,128)S(1)}, u32[]{:S(2)}, u32[]{:S(2)}) %collective-permute-start) | collective-permute-done | bytes 1048608 | tf_op jit(solution)/shard_map/ppermute | solution.py:36
  18.0 1.9 collective-permute-start.2
  20.0 2.6 %collective-permute-start.5 = (f32[16,64,256]{2,1,0:T(8,128)}, f32[16,64,256]{2,1,0:T(8,128)S(1)}, u32[]{:S(2)}, u32[]{:S(2)}) collective-permute-start(f32[16,64,256]{2,1,0:T(8,128)} %param.4), channel_id=1, source_target_pairs={{0,0},{1,16},{2,2},{3,18},{4,4},{5,20},{6,6},{7,22},{8,8},{9,24},{... | collective-permute-start | bytes 3145736 | tf_op jit(solution)/shard_map/ppermute | solution.py:36
  22.7 2.1 collective-permute-start.1
  24.8 26.1 %collective-permute-done.2.refs_2_ = f32[7,64,256]{2,1,0:T(8,128)S(1)} collective-permute-done((f32[7,64,256]{2,1,0:T(8,128)S(1)}, f32[7,64,256]{2,1,0:T(8,128)S(1)}, u32[]{:S(2)}, u32[]{:S(2)}) %collective-permute-start.2) | collective-permute-done | bytes 458784 | tf_op jit(solution)/shard_map/ppermute | solution.py:36
  50.9 0.8 copy-done.6
  51.7 25.2 %collective-permute-done.1.refs_1_ = f32[7,64,256]{2,1,0:T(8,128)S(1)} collective-permute-done((f32[7,64,256]{2,1,0:T(8,128)S(1)}, f32[7,64,256]{2,1,0:T(8,128)S(1)}, u32[]{:S(2)}, u32[]{:S(2)}) %collective-permute-start.1) | collective-permute-done | bytes 458784 | tf_op jit(solution)/shard_map/ppermute | solution.py:36
  76.9 0.8 copy-done.8
  77.7 0.7 pad_maximum_fusion.3
  78.4 5.0 %collective-permute-start.3 = (f32[30,8,256]{2,1,0:T(8,128)}, f32[30,8,256]{2,1,0:T(8,128)S(1)}, u32[]{:S(2)}, u32[]{:S(2)}) collective-permute-start(f32[30,8,256]{2,1,0:T(8,128)} %pad_maximum_fusion.3), channel_id=1, source_target_pairs={{0,16},{16,2},{2,18},{18,4},{4,20},{20,6},{6,22},{22,8},{8,24},{24... | collective-permute-start | bytes 737288 | tf_op jit(solution)/shard_map/ppermute | solution.py:36
  83.4 0.7 pad_maximum_fusion.4
  84.2 2.3 %collective-permute-start.4 = (f32[30,8,256]{2,1,0:T(8,128)}, f32[30,8,256]{2,1,0:T(8,128)}, u32[]{:S(2)}, u32[]{:S(2)}) collective-permute-start(f32[30,8,256]{2,1,0:T(8,128)} %pad_maximum_fusion.4), channel_id=1, source_target_pairs={{16,0},{2,16},{18,2},{4,18},{20,4},{6,20},{22,6},{8,22},{24,8},{10... | collective-permute-start | bytes 737288 | tf_op jit(solution)/shard_map/ppermute | solution.py:36
  87.4 3.0 %shard_map.46 = (bf16[64,240]{1,0:T(8,128)(2,1)}, bf16[80,192]{1,0:T(8,128)(2,1)}, bf16[2,256,256]{2,1,0:T(8,128)(2,1)}, bf16[2,256,256]{2,1,0:T(8,128)(2,1)}, b...) custom-call(f32[2,3,15]{2,1,0:T(4,128)} %copy-done.15), custom_call_target="tpu_custom_call" | custom-call | tf_op jit(solution)/shard_map/pallas_call | solution.py:90
  90.3 4.3 %collective-permute-done.4.refs_4_ = f32[30,8,256]{2,1,0:T(8,128)} collective-permute-done((f32[30,8,256]{2,1,0:T(8,128)}, f32[30,8,256]{2,1,0:T(8,128)}, u32[]{:S(2)}, u32[]{:S(2)}) %collective-permute-start.4) | collective-permute-done | bytes 245792 | tf_op jit(solution)/shard_map/ppermute | solution.py:36
  94.7 10.9 %shard_map.47 = (f32[30,64,256]{2,1,0:T(8,128)}, f32[30,8,256]{2,1,0:T(8,128)}, f32[30,8,256]{2,1,0:T(8,128)}, f32[16,64,256]{2,1,0:T(8,128)}) custom-call(f32[2,15]{1,0:T(2,128)} %bitcast.1, f32[16,64,256]{2,1,0:T(8,128)} %copy-done.2, f32[7,64,256]{2,1,0:T(8,128)} %copy-done.8, f32[7,64,256]{2,1,0:T(8,128)} %copy-done.6, f32[30,8,256]{2,1,0:T(8,128)} %copy-done.12, ...), custom_call_target="tpu_custom_call" | custom-call | tf_op jit(solution)/shard_map/pallas_call | solution.py:262
  105.6 1.0 copy-done.5
  106.5 6.4 %shard_map.48 = (f32[30,64,256]{2,1,0:T(8,128)}, f32[30,8,256]{2,1,0:T(8,128)}, f32[30,8,256]{2,1,0:T(8,128)}) custom-call(f32[2,15]{1,0:T(2,128)} %bitcast.2, f32[16,64,256]{2,1,0:T(8,128)} %get-tuple-element.29.blurred_two, f32[16,64,256]{2,1,0:T(8,128)} %copy-done.5, bf16[80,192]{1,0:T(8,128)(2,1)} %get-tuple-element.30.back_left.refs_12_, ...), custom_call_target="tpu_custom_call" | custom-call | tf_op jit(solution)/shard_map/pallas_call | solution.py:262
  113.0 2.3 %collective-permute-start.7 = (f32[30,8,256]{2,1,0:T(8,128)}, f32[30,8,256]{2,1,0:T(8,128)S(1)}, u32[]{:S(2)}, u32[]{:S(2)}) collective-permute-start(f32[30,8,256]{2,1,0:T(8,128)} %get-tuple-element.36), channel_id=1, source_target_pairs={{0,16},{16,2},{2,18},{18,4},{4,20},{20,6},{6,22},{22,8},{8,24},{24... | collective-permute-start | bytes 737288 | tf_op jit(solution)/shard_map/ppermute | solution.py:36
  115.3 5.0 %collective-permute-start.8 = (f32[30,8,256]{2,1,0:T(8,128)}, f32[30,8,256]{2,1,0:T(8,128)S(1)}, u32[]{:S(2)}, u32[]{:S(2)}) collective-permute-start(f32[30,8,256]{2,1,0:T(8,128)} %get-tuple-element.37), channel_id=1, source_target_pairs={{16,0},{2,16},{18,2},{4,18},{20,4},{6,20},{22,6},{8,22},{24,8},{10... | collective-permute-start | bytes 737288 | tf_op jit(solution)/shard_map/ppermute | solution.py:36
  120.3 1.5 slice.115
  121.8 1.0 collective-permute-done.7
  122.8 2.9 %collective-permute-done.8 = f32[30,8,256]{2,1,0:T(8,128)S(1)} collective-permute-done((f32[30,8,256]{2,1,0:T(8,128)}, f32[30,8,256]{2,1,0:T(8,128)S(1)}, u32[]{:S(2)}, u32[]{:S(2)}) %collective-permute-start.8) | collective-permute-done | bytes 245792 | tf_op jit(solution)/shard_map/ppermute | solution.py:36
  125.7 1.1 slice_add_fusion.4
  127.2 1.9 collective-permute-start.9
  129.2 5.0 %collective-permute-start.10 = (f32[14,64,256]{2,1,0:T(8,128)S(1)}, f32[14,64,256]{2,1,0:T(8,128)S(1)}, u32[]{:S(2)}, u32[]{:S(2)}) collective-permute-start(f32[14,64,256]{2,1,0:T(8,128)S(1)} %get-tuple-element.46), channel_id=1, source_target_pairs={{1,0},{17,16},{3,2},{19,18},{5,4},{21,20},{7,6},{23,22},{9,8},{25,... | collective-permute-start | bytes 2752520 | tf_op jit(solution)/shard_map/ppermute | solution.py:36
  134.2 9.0 %collective-permute-done.9 = f32[14,64,256]{2,1,0:T(8,128)S(1)} collective-permute-done((f32[14,64,256]{2,1,0:T(8,128)S(1)}, f32[14,64,256]{2,1,0:T(8,128)S(1)}, u32[]{:S(2)}, u32[]{:S(2)}) %collective-permute-start.9) | collective-permute-done | bytes 917536 | tf_op jit(solution)/shard_map/ppermute | solution.py:36
  143.1 1.9 collective-permute-done.10
  145.7 1.0 copy-done.3
  147.0 2.6 %collective-permute-start.11 = (f32[30,8,256]{2,1,0:T(8,128)S(1)}, f32[30,8,256]{2,1,0:T(8,128)S(1)}, u32[]{:S(2)}, u32[]{:S(2)}) collective-permute-start(f32[30,8,256]{2,1,0:T(8,128)S(1)} %pad_maximum_fusion.5), channel_id=1, source_target_pairs={{0,16},{16,2},{2,18},{18,4},{4,20},{20,6},{6,22},{22,8},{8,24},{24... | collective-permute-start | bytes 737288 | tf_op jit(solution)/shard_map/ppermute | solution.py:36
  149.6 4.9 %collective-permute-start.12 = (f32[30,8,256]{2,1,0:T(8,128)S(1)}, f32[30,8,256]{2,1,0:T(8,128)S(1)}, u32[]{:S(2)}, u32[]{:S(2)}) collective-permute-start(f32[30,8,256]{2,1,0:T(8,128)S(1)} %pad_maximum_fusion.6), channel_id=1, source_target_pairs={{16,0},{2,16},{18,2},{4,18},{20,4},{6,20},{22,6},{8,22},{24,8},{10... | collective-permute-start | bytes 737288 | tf_op jit(solution)/shard_map/ppermute | solution.py:36
  154.5 2.0 collective-permute-done.11.refs_3_
  156.6 3.3 %collective-permute-done.12.refs_4_ = f32[30,8,256]{2,1,0:T(8,128)S(1)} collective-permute-done((f32[30,8,256]{2,1,0:T(8,128)S(1)}, f32[30,8,256]{2,1,0:T(8,128)S(1)}, u32[]{:S(2)}, u32[]{:S(2)}) %collective-permute-start.12) | collective-permute-done | bytes 245792 | tf_op jit(solution)/shard_map/ppermute | solution.py:36
  159.8 0.7 copy-done.14
  160.5 15.0 %shard_map.49 = (f32[30,64,256]{2,1,0:T(8,128)}, f32[30,8,256]{2,1,0:T(8,128)}, f32[30,8,256]{2,1,0:T(8,128)}) custom-call(f32[2,15]{1,0:T(2,128)} %bitcast.3, f32[16,64,256]{2,1,0:T(8,128)} %copy-done, f32[7,64,256]{2,1,0:T(8,128)} %copy-done.11, f32[7,64,256]{2,1,0:T(8,128)} %copy-done.10, f32[30,8,256]{2,1,0:T(8,128)} %copy-done.13, ...), custom_call_target="tpu_custom_call" | custom-call | tf_op jit(solution)/shard_map/pallas_call | solution.py:262
  175.5 3.1 %collective-permute-start.13 = (f32[30,8,256]{2,1,0:T(8,128)}, f32[30,8,256]{2,1,0:T(8,128)S(1)}, u32[]{:S(2)}, u32[]{:S(2)}) collective-permute-start(f32[30,8,256]{2,1,0:T(8,128)} %get-tuple-element.39), channel_id=1, source_target_pairs={{0,16},{16,2},{2,18},{18,4},{4,20},{20,6},{6,22},{22,8},{8,24},{24... | collective-permute-start | bytes 737288 | tf_op jit(solution)/shard_map/ppermute | solution.py:36
  178.7 4.2 %collective-permute-start.14 = (f32[30,8,256]{2,1,0:T(8,128)}, f32[30,8,256]{2,1,0:T(8,128)S(1)}, u32[]{:S(2)}, u32[]{:S(2)}) collective-permute-start(f32[30,8,256]{2,1,0:T(8,128)} %get-tuple-element.40), channel_id=1, source_target_pairs={{16,0},{2,16},{18,2},{4,18},{20,4},{6,20},{22,6},{8,22},{24,8},{10... | collective-permute-start | bytes 737288 | tf_op jit(solution)/shard_map/ppermute | solution.py:36
  182.9 1.5 slice.131
  184.4 1.0 collective-permute-done.13
  185.3 3.7 %collective-permute-done.14 = f32[30,8,256]{2,1,0:T(8,128)S(1)} collective-permute-done((f32[30,8,256]{2,1,0:T(8,128)}, f32[30,8,256]{2,1,0:T(8,128)S(1)}, u32[]{:S(2)}, u32[]{:S(2)}) %collective-permute-start.14) | collective-permute-done | bytes 245792 | tf_op jit(solution)/shard_map/ppermute | solution.py:36
  189.1 1.1 slice_add_fusion.2
  190.2 2.4 %collective-permute-start.16 = (f32[7,64,256]{2,1,0:T(8,128)S(1)}, f32[7,64,256]{2,1,0:T(8,128)S(1)}, u32[]{:S(2)}, u32[]{:S(2)}) collective-permute-start(f32[7,64,256]{2,1,0:T(8,128)S(1)} %pad_maximum_fusion.2), channel_id=1, source_target_pairs={{1,0},{17,16},{3,2},{19,18},{5,4},{21,20},{7,6},{23,22},{9,8},{25,... | collective-permute-start | bytes 1376264 | tf_op jit(solution)/shard_map/ppermute | solution.py:36
  192.9 2.1 collective-permute-start.15
  195.0 3.7 %collective-permute-done.16 = f32[7,64,256]{2,1,0:T(8,128)S(1)} collective-permute-done((f32[7,64,256]{2,1,0:T(8,128)S(1)}, f32[7,64,256]{2,1,0:T(8,128)S(1)}, u32[]{:S(2)}, u32[]{:S(2)}) %collective-permute-start.16) | collective-permute-done | bytes 458784 | tf_op jit(solution)/shard_map/ppermute | solution.py:36
  198.7 5.3 %collective-permute-done.15 = f32[7,64,256]{2,1,0:T(8,128)S(1)} collective-permute-done((f32[7,64,256]{2,1,0:T(8,128)S(1)}, f32[7,64,256]{2,1,0:T(8,128)S(1)}, u32[]{:S(2)}, u32[]{:S(2)}) %collective-permute-start.15) | collective-permute-done | bytes 458784 | tf_op jit(solution)/shard_map/ppermute | solution.py:36
  204.3 1.9 collective-permute-start.17
  206.2 15.7 %collective-permute-done.17 = f32[16,64,256]{2,1,0:T(8,128)S(1)} collective-permute-done((f32[16,64,256]{2,1,0:T(8,128)S(1)}, f32[16,64,256]{2,1,0:T(8,128)S(1)}, u32[]{:S(2)}, u32[]{:S(2)}) %collective-permute-start.17) | collective-permute-done | bytes 1048608 | tf_op jit(solution)/shard_map/ppermute | solution.py:36
  221.9 1.0 copy.10
  (57 shorter events, 2.8 us)
Async XLA Ops:
  0.0 86.5 %copy-start.16 = (f32[2,3,15]{2,0,1:T(2,128)S(1)}, f32[2,3,15]{2,0,1:T(2,128)}, u32[]{:S(2)}) copy-start(f32[2,3,15]{2,0,1:T(2,128)} %param.7) | copy-start | bytes 1084
  0.0 18.0 %collective-permute-start = (f32[16,64,256]{2,1,0:T(8,128)}, f32[16,64,256]{2,1,0:T(8,128)S(1)}, u32[]{:S(2)}, u32[]{:S(2)}) collective-permute-start(f32[16,64,256]{2,1,0:T(8,128)} %param.6), channel_id=1, source_target_pairs={{0,0},{1,16},{2,2},{3,18},{4,4},{5,20},{6,6},{7,22},{8,8},{9,24},{... | collective-permute-start | bytes 3145736 | tf_op jit(solution)/shard_map/ppermute | solution.py:36
  18.0 76.7 %copy-start.2 = (f32[16,64,256]{2,1,0:T(8,128)}, f32[16,64,256]{2,1,0:T(8,128)S(1)}, u32[]{:S(2)}) copy-start(f32[16,64,256]{2,1,0:T(8,128)S(1)} %collective-permute-done.refs_0_) | copy-start | bytes 3145732
  18.0 32.8 %collective-permute-start.2 = (f32[7,64,256]{2,1,0:T(8,128)S(1)}, f32[7,64,256]{2,1,0:T(8,128)S(1)}, u32[]{:S(2)}, u32[]{:S(2)}) collective-permute-start(f32[7,64,256]{2,1,0:T(8,128)S(1)} %get-tuple-element.53), channel_id=1, source_target_pairs={{1,0},{17,16},{3,2},{19,18},{5,4},{21,20},{7,6},{23,22},{9,8},{25,... | collective-permute-start | bytes 1376264 | tf_op jit(solution)/shard_map/ppermute | solution.py:36
  20.0 70.4 %collective-permute-start.5 = (f32[16,64,256]{2,1,0:T(8,128)}, f32[16,64,256]{2,1,0:T(8,128)S(1)}, u32[]{:S(2)}, u32[]{:S(2)}) collective-permute-start(f32[16,64,256]{2,1,0:T(8,128)} %param.4), channel_id=1, source_target_pairs={{0,0},{1,16},{2,2},{3,18},{4,4},{5,20},{6,6},{7,22},{8,8},{9,24},{... | collective-permute-start | bytes 3145736 | tf_op jit(solution)/shard_map/ppermute | solution.py:36
  22.6 83.0 %collective-permute-start.6 = (f32[16,64,256]{2,1,0:T(8,128)}, f32[16,64,256]{2,1,0:T(8,128)S(1)}, u32[]{:S(2)}, u32[]{:S(2)}) collective-permute-start(f32[16,64,256]{2,1,0:T(8,128)} %param.5), channel_id=1, source_target_pairs={{0,225},{1,241},{2,227},{3,243},{4,229},{5,245},{6,231},{7,247},{8... | collective-permute-start | bytes 3145736 | tf_op jit(solution)/shard_map/ppermute | solution.py:36
  22.7 54.2 %collective-permute-start.1 = (f32[7,64,256]{2,1,0:T(8,128)S(1)}, f32[7,64,256]{2,1,0:T(8,128)S(1)}, u32[]{:S(2)}, u32[]{:S(2)}) collective-permute-start(f32[7,64,256]{2,1,0:T(8,128)S(1)} %get-tuple-element.54), channel_id=1, source_target_pairs={{0,1},{16,17},{2,3},{18,19},{4,5},{20,21},{6,7},{22,23},{8,9},{24,... | collective-permute-start | bytes 1376264 | tf_op jit(solution)/shard_map/ppermute | solution.py:36
  50.9 0.8 copy-start.6
  76.9 0.8 copy-start.8
  78.4 11.9 %collective-permute-start.3 = (f32[30,8,256]{2,1,0:T(8,128)}, f32[30,8,256]{2,1,0:T(8,128)S(1)}, u32[]{:S(2)}, u32[]{:S(2)}) collective-permute-start(f32[30,8,256]{2,1,0:T(8,128)} %pad_maximum_fusion.3), channel_id=1, source_target_pairs={{0,16},{16,2},{2,18},{18,4},{4,20},{20,6},{6,22},{22,8},{8,24},{24... | collective-permute-start | bytes 737288 | tf_op jit(solution)/shard_map/ppermute | solution.py:36
  84.2 10.5 %collective-permute-start.4 = (f32[30,8,256]{2,1,0:T(8,128)}, f32[30,8,256]{2,1,0:T(8,128)}, u32[]{:S(2)}, u32[]{:S(2)}) collective-permute-start(f32[30,8,256]{2,1,0:T(8,128)} %pad_maximum_fusion.4), channel_id=1, source_target_pairs={{16,0},{2,16},{18,2},{4,18},{20,4},{6,20},{22,6},{8,22},{24,8},{10... | collective-permute-start | bytes 737288 | tf_op jit(solution)/shard_map/ppermute | solution.py:36
  86.8 0.6 copy-start.15
  90.3 4.3 %copy-start.4 = (f32[16,64,256]{2,1,0:T(8,128)}, f32[16,64,256]{2,1,0:T(8,128)S(1)}, u32[]{:S(2)}) copy-start(f32[16,64,256]{2,1,0:T(8,128)S(1)} %collective-permute-done.5.refs_5_) | copy-start | bytes 3145732
  90.3 4.3 %copy-start.12 = (f32[30,8,256]{2,1,0:T(8,128)}, f32[30,8,256]{2,1,0:T(8,128)S(1)}, u32[]{:S(2)}) copy-start(f32[30,8,256]{2,1,0:T(8,128)S(1)} %collective-permute-done.3.refs_3_) | copy-start | bytes 737284
  105.5 1.0 copy-start.5
  113.0 9.8 %collective-permute-start.7 = (f32[30,8,256]{2,1,0:T(8,128)}, f32[30,8,256]{2,1,0:T(8,128)S(1)}, u32[]{:S(2)}, u32[]{:S(2)}) collective-permute-start(f32[30,8,256]{2,1,0:T(8,128)} %get-tuple-element.36), channel_id=1, source_target_pairs={{0,16},{16,2},{2,18},{18,4},{4,20},{20,6},{6,22},{22,8},{8,24},{24... | collective-permute-start | bytes 737288 | tf_op jit(solution)/shard_map/ppermute | solution.py:36
  115.3 10.4 %collective-permute-start.8 = (f32[30,8,256]{2,1,0:T(8,128)}, f32[30,8,256]{2,1,0:T(8,128)S(1)}, u32[]{:S(2)}, u32[]{:S(2)}) collective-permute-start(f32[30,8,256]{2,1,0:T(8,128)} %get-tuple-element.37), channel_id=1, source_target_pairs={{16,0},{2,16},{18,2},{4,18},{20,4},{6,20},{22,6},{8,22},{24,8},{10... | collective-permute-start | bytes 737288 | tf_op jit(solution)/shard_map/ppermute | solution.py:36
  127.2 15.9 %collective-permute-start.9 = (f32[14,64,256]{2,1,0:T(8,128)S(1)}, f32[14,64,256]{2,1,0:T(8,128)S(1)}, u32[]{:S(2)}, u32[]{:S(2)}) collective-permute-start(f32[14,64,256]{2,1,0:T(8,128)S(1)} %get-tuple-element.45), channel_id=1, source_target_pairs={{0,1},{16,17},{2,3},{18,19},{4,5},{20,21},{6,7},{22,23},{8,9},{24,... | collective-permute-start | bytes 2752520 | tf_op jit(solution)/shard_map/ppermute | solution.py:36
  129.1 16.2 %copy-start.7 = (f32[7,64,256]{2,1,0:T(8,128)S(1)}, f32[7,64,256]{2,1,0:T(8,128)}, u32[]{:S(2)}) copy-start(f32[7,64,256]{2,1,0:T(8,128)} %copy-done.6) | copy-start | bytes 1376260
  129.1 16.2 %copy-start.9 = (f32[7,64,256]{2,1,0:T(8,128)S(1)}, f32[7,64,256]{2,1,0:T(8,128)}, u32[]{:S(2)}) copy-start(f32[7,64,256]{2,1,0:T(8,128)} %copy-done.8) | copy-start | bytes 1376260
  129.2 15.9 %collective-permute-start.10 = (f32[14,64,256]{2,1,0:T(8,128)S(1)}, f32[14,64,256]{2,1,0:T(8,128)S(1)}, u32[]{:S(2)}, u32[]{:S(2)}) collective-permute-start(f32[14,64,256]{2,1,0:T(8,128)S(1)} %get-tuple-element.46), channel_id=1, source_target_pairs={{1,0},{17,16},{3,2},{19,18},{5,4},{21,20},{7,6},{23,22},{9,8},{25,... | collective-permute-start | bytes 2752520 | tf_op jit(solution)/shard_map/ppermute | solution.py:36
  145.4 1.3 copy-start.3
  145.6 1.2 copy-start.10
  145.6 1.2 copy-start.11
  146.9 12.9 %copy-start = (f32[16,64,256]{2,1,0:T(8,128)}, f32[16,64,256]{2,1,0:T(8,128)S(1)}, u32[]{:S(2)}) copy-start(f32[16,64,256]{2,1,0:T(8,128)S(1)} %fusion.7.refs_0_) | copy-start | bytes 3145732
  147.0 9.6 %collective-permute-start.11 = (f32[30,8,256]{2,1,0:T(8,128)S(1)}, f32[30,8,256]{2,1,0:T(8,128)S(1)}, u32[]{:S(2)}, u32[]{:S(2)}) collective-permute-start(f32[30,8,256]{2,1,0:T(8,128)S(1)} %pad_maximum_fusion.5), channel_id=1, source_target_pairs={{0,16},{16,2},{2,18},{18,4},{4,20},{20,6},{6,22},{22,8},{8,24},{24... | collective-permute-start | bytes 737288 | tf_op jit(solution)/shard_map/ppermute | solution.py:36
  149.6 10.2 %collective-permute-start.12 = (f32[30,8,256]{2,1,0:T(8,128)S(1)}, f32[30,8,256]{2,1,0:T(8,128)S(1)}, u32[]{:S(2)}, u32[]{:S(2)}) collective-permute-start(f32[30,8,256]{2,1,0:T(8,128)S(1)} %pad_maximum_fusion.6), channel_id=1, source_target_pairs={{16,0},{2,16},{18,2},{4,18},{20,4},{6,20},{22,6},{8,22},{24,8},{10... | collective-permute-start | bytes 737288 | tf_op jit(solution)/shard_map/ppermute | solution.py:36
  156.6 3.3 %copy-start.13 = (f32[30,8,256]{2,1,0:T(8,128)}, f32[30,8,256]{2,1,0:T(8,128)S(1)}, u32[]{:S(2)}) copy-start(f32[30,8,256]{2,1,0:T(8,128)S(1)} %collective-permute-done.11.refs_3_) | copy-start | bytes 737284
  159.8 0.7 copy-start.14
  175.5 9.8 %collective-permute-start.13 = (f32[30,8,256]{2,1,0:T(8,128)}, f32[30,8,256]{2,1,0:T(8,128)S(1)}, u32[]{:S(2)}, u32[]{:S(2)}) collective-permute-start(f32[30,8,256]{2,1,0:T(8,128)} %get-tuple-element.39), channel_id=1, source_target_pairs={{0,16},{16,2},{2,18},{18,4},{4,20},{20,6},{6,22},{22,8},{8,24},{24... | collective-permute-start | bytes 737288 | tf_op jit(solution)/shard_map/ppermute | solution.py:36
  178.7 10.4 %collective-permute-start.14 = (f32[30,8,256]{2,1,0:T(8,128)}, f32[30,8,256]{2,1,0:T(8,128)S(1)}, u32[]{:S(2)}, u32[]{:S(2)}) collective-permute-start(f32[30,8,256]{2,1,0:T(8,128)} %get-tuple-element.40), channel_id=1, source_target_pairs={{16,0},{2,16},{18,2},{4,18},{20,4},{6,20},{22,6},{8,22},{24,8},{10... | collective-permute-start | bytes 737288 | tf_op jit(solution)/shard_map/ppermute | solution.py:36
  190.2 8.4 %collective-permute-start.16 = (f32[7,64,256]{2,1,0:T(8,128)S(1)}, f32[7,64,256]{2,1,0:T(8,128)S(1)}, u32[]{:S(2)}, u32[]{:S(2)}) collective-permute-start(f32[7,64,256]{2,1,0:T(8,128)S(1)} %pad_maximum_fusion.2), channel_id=1, source_target_pairs={{1,0},{17,16},{3,2},{19,18},{5,4},{21,20},{7,6},{23,22},{9,8},{25,... | collective-permute-start | bytes 1376264 | tf_op jit(solution)/shard_map/ppermute | solution.py:36
  192.9 11.2 %copy-start.1 = (f32[16,64,256]{2,1,0:T(8,128)S(1)}, f32[16,64,256]{2,1,0:T(8,128)}, u32[]{:S(2)}) copy-start(f32[16,64,256]{2,1,0:T(8,128)} %copy-done) | copy-start | bytes 3145732
  192.9 11.1 %collective-permute-start.15 = (f32[7,64,256]{2,1,0:T(8,128)S(1)}, f32[7,64,256]{2,1,0:T(8,128)S(1)}, u32[]{:S(2)}, u32[]{:S(2)}) collective-permute-start(f32[7,64,256]{2,1,0:T(8,128)S(1)} %slice.160), channel_id=1, source_target_pairs={{0,1},{16,17},{2,3},{18,19},{4,5},{20,21},{6,7},{22,23},{8,9},{24,... | collective-permute-start | bytes 1376264 | tf_op jit(solution)/shard_map/ppermute | solution.py:36
  204.3 17.6 %collective-permute-start.17 = (f32[16,64,256]{2,1,0:T(8,128)S(1)}, f32[16,64,256]{2,1,0:T(8,128)S(1)}, u32[]{:S(2)}, u32[]{:S(2)}) collective-permute-start(f32[16,64,256]{2,1,0:T(8,128)S(1)} %fusion.3), channel_id=1, source_target_pairs={{0,0},{16,1},{2,2},{18,3},{4,4},{20,5},{6,6},{22,7},{8,8},{24,9},{... | collective-permute-start | bytes 3145736 | tf_op jit(solution)/shard_map/ppermute | solution.py:36

commit v3 on v2

v3 whole, which is shorter than its diff:
```python
import functools

import jax
import jax.numpy as jnp
from jax import lax
from jax.experimental import pallas as pl
from jax.experimental.pallas import tpu as pltpu
from jax.sharding import PartitionSpec as P


EDGE = 8
CHUNK = 4
F32 = jnp.float32
BF16 = jnp.bfloat16


AXES = ("gz", "xy")
SLABS = 16
TILES = 16


def given(slab, tile):
    return slab * TILES + tile


def working(slab, tile):
    return given(slab - slab % 2 + tile % 2, tile - tile % 2 + slab % 2)


def moved(value, source, target, change):
    pairs = []
    for slab in range(SLABS):
        for tile in range(TILES):
            to_slab, to_tile = change(slab, tile)
            if 0 <= to_slab < SLABS and 0 <= to_tile < TILES:
                pairs.append((source(slab, tile), target(to_slab, to_tile)))
    return lax.ppermute(value, AXES, pairs)


def placed(value):
    return moved(value, given, working, lambda slab, tile: (slab, tile))


def along_slabs(value, step):
    return moved(value, working, working, lambda slab, tile: (slab + step, tile))


def along_tiles(value, step):
    return moved(value, working, working, lambda slab, tile: (slab, tile + step))


def split(value):
    high = value.astype(BF16)
    low = (value - high.astype(F32)).astype(BF16)
    return high, low


def banded(taps, shape, period, axis, shift, low_from):
    i = lax.broadcasted_iota(jnp.int32, shape, 0)
    j = lax.broadcasted_iota(jnp.int32, shape, 1)
    is_low = j >= low_from
    for _ in range(2):
        j = jnp.where(j >= period, j - period, j)
    offset = j - i + shift if axis == 1 else i - j + shift
    value = jnp.zeros(shape, F32)
    for t, tap in enumerate(taps):
        value = jnp.where(offset == t, tap, value)
    high, low = split(value)
    return jnp.where(is_low, low.astype(F32), high.astype(F32)).astype(BF16)


def matrix_kernel(kernels_ref, *outs):
    for v in range(2):
        left, back_left, right, back_right = outs[4 * v : 4 * v + 4]
        rows, tall = left.shape[0], back_left.shape[0]
        width = right.shape[1]
        along_y = [kernels_ref[v, 1, t] for t in range(kernels_ref.shape[2])]
        along_x = [kernels_ref[v, 2, t] for t in range(kernels_ref.shape[2])]
        half = len(along_y) // 2
        left[...] = banded(along_y, left.shape, tall, 1, half - EDGE, 2 * tall)
        back_left[...] = banded(along_y, back_left.shape, rows, 0, half - EDGE, 2 * rows)
        for part in range(2):
            low_from = width * (1 - part)
            right[part] = banded(along_x, right.shape[1:], width, 0, half, low_from)
            back_right[part] = banded(along_x, right.shape[1:], width, 1, half, low_from)


def filter_matrices(kernels, rows, width):
    tall = rows + 2 * EDGE
    shapes = [(rows, 3 * tall), (tall, 3 * rows), (2, width, width), (2, width, width)] * 2
    out = pl.pallas_call(
        matrix_kernel,
        out_shape=[jax.ShapeDtypeStruct(shape, BF16) for shape in shapes],
        in_specs=[pl.BlockSpec(memory_space=pltpu.SMEM)],
        out_specs=[pl.BlockSpec(memory_space=pltpu.VMEM)] * len(shapes),
    )(kernels)
    return out[:4], out[4:]


def gather_planes(taps, planes, depth):
    outs = []
    for z in range(depth):
        total = taps[0] * planes[z]
        for t in range(1, len(taps)):
            total = total + taps[t] * planes[z + t]
        outs.append(total)
    return outs


def scatter_planes(tap_lists, plane_lists):
    depth = len(plane_lists[0])
    count = len(tap_lists[0])
    outs = []
    for o in range(depth + count - 1):
        total = None
        for taps, planes in zip(tap_lists, plane_lists):
            for z in range(max(0, o - count + 1), min(depth, o + 1)):
                term = taps[o - z] * planes[z]
                total = term if total is None else total + term
        outs.append(total)
    return outs


def z_forward(taps, extended, out_ref):
    depth, rows, width = out_ref.shape

    def strip(step, carry):
        window = pl.ds(pl.multiple_of(step * EDGE, EDGE), EDGE)
        for lane in range(0, width, 128):
            lanes = pl.ds(lane, 128)
            planes = [extended[z, window, lanes] for z in range(extended.shape[0])]
            for z, total in enumerate(gather_planes(taps, planes, depth)):
                out_ref[z, window, lanes] = total
        return carry

    lax.fori_loop(0, rows // EDGE, strip, 0)


def left_product(matrix, value):
    high, low = split(value)
    stacked = jnp.concatenate([high, low, high], axis=0)
    return jnp.dot(matrix, stacked, preferred_element_type=F32)


def right_product(value, matrix_ref):
    high, low = split(value)
    dot = functools.partial(jnp.dot, preferred_element_type=F32)
    return dot(high, matrix_ref[0]) + dot(low, matrix_ref[0]) + dot(high, matrix_ref[1])


def blurred_chunk(along_z, first, left, right):
    rows = [left_product(left[...], along_z[first + k]) for k in range(CHUNK)]
    return right_product(jnp.concatenate(rows, axis=0), right)


def back_chunk(ratio, first, left, right, out_ref):
    rows = out_ref.shape[1] - 2 * EDGE
    across = right_product(ratio, right)
    for k in range(CHUNK):
        out_ref[first + k] = left_product(left[...], across[k * rows : (k + 1) * rows])


def z_back(tap_lists, sources, segments):
    depth, _, width = sources[0].shape

    for first, count, store in segments:

        def strip(step, carry, first=first, store=store):
            row = pl.multiple_of(step * EDGE, EDGE)
            for lane in range(0, width, 128):
                lanes = pl.ds(lane, 128)
                window = pl.ds(row + first * EDGE, EDGE)
                plane_lists = [[ref[z, window, lanes] for z in range(depth)] for ref in sources]
                for o, total in enumerate(scatter_planes(tap_lists, plane_lists)):
                    store(o, row, lanes, total)
            return carry

        lax.fori_loop(0, count, strip, 0)


def read_taps(ref, view, flip):
    taps = [ref[view, t] for t in range(ref.shape[1])]
    return taps[::-1] if flip else taps


def blur_into(out_ref, taps, extended, along_z, left, right):
    depth, rows, _ = out_ref.shape
    z_forward(taps, extended, along_z)
    for first in range(0, depth, CHUNK):
        blurred = blurred_chunk(along_z, first, left, right)
        for k in range(CHUNK):
            out_ref[first + k] = blurred[k * rows : (k + 1) * rows]


def ratios_back(seen_planes, blurred, left, right, back):
    for first in range(0, blurred.shape[0], CHUNK):
        ratio = jnp.concatenate(
            [seen_planes[first + k] / blurred[first + k] for k in range(CHUNK)], axis=0
        )
        back_chunk(ratio, first, left, right, back)


class Mirrored:
    def __init__(self, low_half, high_half):
        planes = [(half, z) for half in (low_half, high_half) for z in range(half.shape[0])]
        self.planes = planes[::-1]

    def __getitem__(self, index):
        half, z = self.planes[index]
        return half[z]


def forward_kernel(taps_ref, *refs):
    center, z_low, z_high, y_low, y_high = refs[:5]
    mats = refs[5:9]
    extended, blurred, along_z = refs[9], refs[10:12], refs[12]
    depth, rows, _ = center.shape
    reach = z_low.shape[0]
    inner = pl.ds(EDGE, rows)
    extended[:reach, inner] = z_low[...]
    extended[pl.ds(reach, depth), inner] = center[...]
    extended[pl.ds(reach + depth, reach), inner] = z_high[...]
    extended[:, :EDGE] = y_low[...]
    extended[:, pl.ds(EDGE + rows, EDGE)] = y_high[...]
    for v in range(2):
        taps = read_taps(taps_ref, v, v == 1)
        blur_into(blurred[v], taps, extended, along_z, mats[2 * v], mats[2 * v + 1])


def back_kernel(taps_ref, *refs):
    blurred, view_one, halves, mats = refs[:2], refs[2], refs[3:5], refs[5:9]
    y_low, y_mid, y_high = refs[9:12]
    backs = refs[12:14]
    ratios_back(view_one, blurred[0], mats[0], mats[1], backs[0])
    ratios_back(Mirrored(*halves), blurred[1], mats[2], mats[3], backs[1])
    segments = []
    first = 0
    for ref in (y_low, y_mid, y_high):

        def store(o, row, lanes, total, ref=ref):
            ref[o, pl.ds(row, EDGE), lanes] = total

        segments.append((first, ref.shape[1] // EDGE, store))
        first += ref.shape[1] // EDGE
    z_back([read_taps(taps_ref, 0, False), read_taps(taps_ref, 1, True)], backs, segments)


def row_sum_kernel(y_low, y_mid, y_high, from_below, from_above, z_low, z_mid, z_high):
    edge, inner = y_low.shape[1], y_mid.shape[1]
    first = 0
    for ref in (z_low, z_mid, z_high):
        planes = pl.ds(first, ref.shape[0])
        ref[:, :edge] = y_low[planes] + from_below[planes]
        ref[:, pl.ds(edge, inner)] = y_mid[planes]
        ref[:, pl.ds(edge + inner, edge)] = y_high[planes] + from_above[planes]
        first += ref.shape[0]


def second_kernel(taps_ref, *refs):
    before, z_low, z_mid, z_high, from_below, from_above = refs[:6]
    view_one, halves, mats = refs[6], refs[7:9], refs[9:17]
    y_low_out, y_high_out, z_low_out, z_mid_out, z_high_out = refs[17:22]
    estimate, along_z, backs = refs[22], refs[23], refs[24:26]
    overlap, middle = z_low.shape[0], z_mid.shape[0]
    for o in range(before.shape[0]):
        if o < overlap:
            total = z_low[o] + from_below[o]
        elif o < overlap + middle:
            total = z_mid[o - overlap]
        else:
            total = z_high[o - overlap - middle] + from_above[o - overlap - middle]
        estimate[o] = before[o] * total * 0.5
    taps = [read_taps(taps_ref, 0, False), read_taps(taps_ref, 1, True)]
    seen = (view_one, Mirrored(*halves))
    for v in range(2):
        left, back_left, right, back_right = mats[4 * v : 4 * v + 4]
        z_forward(taps[v], estimate, along_z)
        for first in range(0, view_one.shape[0], CHUNK):
            blurred = blurred_chunk(along_z, first, left, right)
            ratio = jnp.concatenate([seen[v][first + k] for k in range(CHUNK)], axis=0) / blurred
            back_chunk(ratio, first, back_left, back_right, backs[v])
    rows = z_mid_out.shape[1]
    reach = z_low_out.shape[0]
    depth = z_mid_out.shape[0]

    def scaled(o, row, lanes, total):
        return total * estimate[o, pl.ds(row, EDGE), lanes] * 0.5

    def store_low(o, row, lanes, total):
        y_low_out[o, :, lanes] = scaled(o, 0, lanes, total)

    def store_high(o, row, lanes, total):
        y_high_out[o, :, lanes] = scaled(o, rows + EDGE, lanes, total)

    def store_inner(o, row, lanes, total):
        value = scaled(o, pl.multiple_of(row + EDGE, EDGE), lanes, total)
        if o < reach:
            ref, plane = z_low_out, o
        elif o < reach + depth:
            ref, plane = z_mid_out, o - reach
        else:
            ref, plane = z_high_out, o - reach - depth
        ref[plane, pl.ds(row, EDGE), lanes] = value

    strips = rows // EDGE
    z_back(
        taps, backs, [(0, 1, store_low), (1, strips, store_inner), (strips + 1, 1, store_high)]
    )


def last_row_sum_kernel(z_low, z_mid, z_high, from_below, from_above, *outs):
    first = 0
    for ref, out in zip((z_low, z_mid, z_high), outs):
        planes = pl.ds(first, ref.shape[0])
        rows = ref.shape[1]
        out[:, :EDGE] = ref[:, :EDGE] + from_below[planes]
        out[:, pl.ds(EDGE, rows - 2 * EDGE)] = ref[:, pl.ds(EDGE, rows - 2 * EDGE)]
        tail = pl.ds(rows - EDGE, EDGE)
        out[:, tail] = ref[:, tail] + from_above[planes]
        first += ref.shape[0]


def call(kernel, arrays, outs, scratch=(), scalars=1):
    vmem = pl.BlockSpec(memory_space=pltpu.VMEM)
    smem = pl.BlockSpec(memory_space=pltpu.SMEM)
    return pl.pallas_call(
        kernel,
        out_shape=[jax.ShapeDtypeStruct(shape, F32) for shape in outs],
        in_specs=[smem] * scalars + [vmem] * (len(arrays) - scalars),
        out_specs=[vmem] * len(outs),
        scratch_shapes=[pltpu.VMEM(shape, F32) for shape in scratch],
    )(*arrays)


def local(view_one, view_two, estimate, psf):
    depth, rows, width = estimate.shape
    kernels = psf / jnp.sum(psf, axis=2, keepdims=True)
    reach = psf.shape[2] // 2
    z_taps = kernels[:, 0]
    one, two = filter_matrices(kernels, rows, width)
    full = depth + 2 * reach
    half = depth // 2

    def mirror(value):
        return moved(value, given, working, lambda slab, tile: (SLABS - 1 - slab, tile))

    estimate = placed(estimate)
    first_half = mirror(view_two[:half])
    z_low = along_slabs(estimate[depth - reach :], 1)
    z_high = along_slabs(estimate[:reach], -1)
    second_half = mirror(view_two[half:])

    def rows_of(window):
        return jnp.concatenate([z_low[:, window], estimate[:, window], z_high[:, window]], axis=0)

    y_low = along_tiles(rows_of(slice(-EDGE, None)), 1)
    y_high = along_tiles(rows_of(slice(None, EDGE)), -1)
    view_one = placed(view_one)

    tall = (depth, rows + 2 * EDGE, width)
    extended = (full, rows + 2 * EDGE, width)
    before, *blurred = call(
        forward_kernel,
        (z_taps, estimate, z_low, z_high, y_low, y_high, one[0], one[2], two[0], two[2]),
        [extended, view_one.shape, view_one.shape],
        [tall],
    )
    y_low, y_mid, y_high = call(
        back_kernel,
        (z_taps, *blurred, view_one, first_half, second_half, one[1], one[3], two[1], two[3]),
        [(full, 2 * EDGE, width), (full, rows - 2 * EDGE, width), (full, 2 * EDGE, width)],
        [tall, tall],
    )
    from_below = along_tiles(y_high, 1)
    from_above = along_tiles(y_low, -1)
    overlap = 2 * reach
    z_low, z_mid, z_high = call(
        row_sum_kernel,
        (y_low, y_mid, y_high, from_below, from_above),
        [(n, rows + 2 * EDGE, width) for n in (overlap, full - 2 * overlap, overlap)],
        scalars=0,
    )
    from_below = along_slabs(z_high, 1)
    from_above = along_slabs(z_low, -1)
    y_low, y_high, *pieces = call(
        second_kernel,
        (z_taps, before, z_low, z_mid, z_high, from_below, from_above)
        + (view_one, first_half, second_half, *one, *two),
        [(full, EDGE, width)] * 2 + [(n, rows, width) for n in (reach, depth, reach)],
        [extended, tall, tall, tall],
    )
    from_below = along_tiles(y_high, 1)
    from_above = along_tiles(y_low, -1)
    z_low, z_mid, z_high = call(
        last_row_sum_kernel,
        (*pieces, from_below, from_above),
        [piece.shape for piece in pieces],
        scalars=0,
    )
    center = moved(z_mid, working, given, lambda slab, tile: (slab, tile))
    from_below = moved(z_high, working, given, lambda slab, tile: (slab + 1, tile))
    from_above = moved(z_low, working, given, lambda slab, tile: (slab - 1, tile))
    return jnp.concatenate(
        [
            center[:reach] + from_below,
            center[reach : depth - reach],
            center[depth - reach :] + from_above,
        ],
        axis=0,
    )


def solution(mesh):
    return jax.shard_map(
        local,
        mesh=mesh,
        in_specs=(P("gz", "xy", None), P("gz", "xy", None), P("gz", "xy", None), P()),
        out_specs=P("gz", "xy", None),
        check_vma=False,
    )
```

time: 224 us -> 218 us (0.973)
  the two profiles are of different devices: /device:TPU:152 before, /device:TPU:154 now
where the time goes in v3:
time: 218 us; the launch traced here: 217 us
  waiting for transfers between devices  112 us (51%)
  starting transfers between devices  52.6 us (24%)
  Pallas kernels  43.4 us (20%)
  local copies, waits for them, and re-layouts  7.95 us (4%)
    ppermute x17, waiting for transfers between devices, moved(): return lax.ppermute(value, AXES, pairs)  112 us
    ppermute x17, starting transfers between devices, moved(): return lax.ppermute(value, AXES, pairs)  52.6 us
    pallas_call x5, Pallas kernels, call(): pl.pallas_call(kernel, out_shape=[jax.ShapeDtypeStruct(shape, F32) for sh...  40.5 us
    unnamed x34, local copies, waits for them, and re-layouts  6.09 us
  transfers between devices with their start and end apart: 17, of which 11 were waited for; matrix products, arithmetic and copies ran while one was open for 1% of the time, Pallas kernels for 5%

profile of v3, /device:TPU:154, one launch (start us, length us, event | category | flops | bytes accessed | tf_op | source)
XLA Modules:
  0.0 217.4 jit_solution(4146887676846950233)
XLA Ops:
  0.0 2.7 %collective-permute-start = (f32[16,64,256]{2,1,0:T(8,128)}, f32[16,64,256]{2,1,0:T(8,128)S(1)}, u32[]{:S(2)}, u32[]{:S(2)}) collective-permute-start(f32[16,64,256]{2,1,0:T(8,128)} %param.6), channel_id=1, source_target_pairs={{0,0},{1,16},{2,2},{3,18},{4,4},{5,20},{6,6},{7,22},{8,8},{9,24},{... | collective-permute-start | bytes 3145736 | tf_op jit(solution)/shard_map/ppermute | solution.py:37
  2.7 15.2 %collective-permute-done.refs_0_ = f32[16,64,256]{2,1,0:T(8,128)S(1)} collective-permute-done((f32[16,64,256]{2,1,0:T(8,128)}, f32[16,64,256]{2,1,0:T(8,128)S(1)}, u32[]{:S(2)}, u32[]{:S(2)}) %collective-permute-start) | collective-permute-done | bytes 1048608 | tf_op jit(solution)/shard_map/ppermute | solution.py:37
  18.0 1.9 collective-permute-start.2
  20.0 1.1 fusion
  21.0 0.3 collective-permute-start.7
  21.4 3.0 %collective-permute-start.6 = (f32[8,64,256]{2,1,0:T(8,128)}, f32[8,64,256]{2,1,0:T(8,128)S(1)}, u32[]{:S(2)}, u32[]{:S(2)}) collective-permute-start(f32[8,64,256]{2,1,0:T(8,128)} %get-tuple-element.58), channel_id=1, source_target_pairs={{0,225},{1,241},{2,227},{3,243},{4,229},{5,245},{6,231},{7,247},{8... | collective-permute-start | bytes 1572872 | tf_op jit(solution)/shard_map/ppermute | solution.py:37
  24.4 4.2 %collective-permute-start.5 = (f32[16,64,256]{2,1,0:T(8,128)}, f32[16,64,256]{2,1,0:T(8,128)S(1)}, u32[]{:S(2)}, u32[]{:S(2)}) collective-permute-start(f32[16,64,256]{2,1,0:T(8,128)} %param.4), channel_id=1, source_target_pairs={{0,0},{1,16},{2,2},{3,18},{4,4},{5,20},{6,6},{7,22},{8,8},{9,24},{... | collective-permute-start | bytes 3145736 | tf_op jit(solution)/shard_map/ppermute | solution.py:37
  28.6 1.9 collective-permute-start.1
  30.6 21.7 %collective-permute-done.2.refs_2_ = f32[7,64,256]{2,1,0:T(8,128)S(1)} collective-permute-done((f32[7,64,256]{2,1,0:T(8,128)S(1)}, f32[7,64,256]{2,1,0:T(8,128)S(1)}, u32[]{:S(2)}, u32[]{:S(2)}) %collective-permute-start.2) | collective-permute-done | bytes 458784 | tf_op jit(solution)/shard_map/ppermute | solution.py:37
  52.2 0.8 copy-done.7
  53.0 22.3 %collective-permute-done.1.refs_1_ = f32[7,64,256]{2,1,0:T(8,128)S(1)} collective-permute-done((f32[7,64,256]{2,1,0:T(8,128)S(1)}, f32[7,64,256]{2,1,0:T(8,128)S(1)}, u32[]{:S(2)}, u32[]{:S(2)}) %collective-permute-start.1) | collective-permute-done | bytes 458784 | tf_op jit(solution)/shard_map/ppermute | solution.py:37
  75.3 0.8 copy-done.8
  76.2 3.3 %collective-permute-start.3 = (f32[30,8,256]{2,1,0:T(8,128)S(1)}, f32[30,8,256]{2,1,0:T(8,128)S(1)}, u32[]{:S(2)}, u32[]{:S(2)}) collective-permute-start(f32[30,8,256]{2,1,0:T(8,128)S(1)} %pad_maximum_fusion.1), channel_id=1, source_target_pairs={{0,16},{16,2},{2,18},{18,4},{4,20},{20,6},{6,22},{22,8},{8,24},{24... | collective-permute-start | bytes 737288 | tf_op jit(solution)/shard_map/ppermute | solution.py:37
  79.5 4.0 %collective-permute-start.4 = (f32[30,8,256]{2,1,0:T(8,128)S(1)}, f32[30,8,256]{2,1,0:T(8,128)S(1)}, u32[]{:S(2)}, u32[]{:S(2)}) collective-permute-start(f32[30,8,256]{2,1,0:T(8,128)S(1)} %pad_maximum_fusion.2), channel_id=1, source_target_pairs={{16,0},{2,16},{18,2},{4,18},{20,4},{6,20},{22,6},{8,22},{24,8},{10... | collective-permute-start | bytes 737288 | tf_op jit(solution)/shard_map/ppermute | solution.py:37
  83.6 0.1 copy.6
  83.8 0.6 slice.56
  84.4 3.0 %shard_map.46 = (bf16[64,240]{1,0:T(8,128)(2,1)}, bf16[80,192]{1,0:T(8,128)(2,1)}, bf16[2,256,256]{2,1,0:T(8,128)(2,1)}, bf16[2,256,256]{2,1,0:T(8,128)(2,1)}, b...) custom-call(f32[2,3,15]{2,1,0:T(4,128)} %copy-done.15), custom_call_target="tpu_custom_call" | custom-call | tf_op jit(solution)/shard_map/pallas_call | solution.py:91
  87.4 2.3 %collective-permute-done.4.refs_4_ = f32[30,8,256]{2,1,0:T(8,128)S(1)} collective-permute-done((f32[30,8,256]{2,1,0:T(8,128)S(1)}, f32[30,8,256]{2,1,0:T(8,128)S(1)}, u32[]{:S(2)}, u32[]{:S(2)}) %collective-permute-start.4) | collective-permute-done | bytes 245792 | tf_op jit(solution)/shard_map/ppermute | solution.py:37
  89.7 0.7 copy-done.14
  90.4 7.8 %shard_map.47 = (f32[30,80,256]{2,1,0:T(8,128)}, f32[16,64,256]{2,1,0:T(8,128)}, f32[16,64,256]{2,1,0:T(8,128)}) custom-call(f32[2,15]{1,0:T(2,128)} %bitcast.1, f32[16,64,256]{2,1,0:T(8,128)} %copy-done, f32[7,64,256]{2,1,0:T(8,128)} %copy-done.8, f32[7,64,256]{2,1,0:T(8,128)} %copy-done.7, f32[30,8,256]{2,1,0:T(8,128)} %copy-done.13, ...), custom_call_target="tpu_custom_call" | custom-call | tf_op jit(solution)/shard_map/pallas_call | solution.py:326
  98.3 0.7 copy-done.2
  99.0 0.2 copy-done.3
  99.2 0.3 copy-done.1
  99.5 9.2 %shard_map.48 = (f32[30,16,256]{2,1,0:T(8,128)}, f32[30,48,256]{2,1,0:T(8,128)}, f32[30,16,256]{2,1,0:T(8,128)}) custom-call(f32[2,15]{1,0:T(2,128)} %bitcast.2, f32[16,64,256]{2,1,0:T(8,128)} %get-tuple-element.35.refs_0_, f32[16,64,256]{2,1,0:T(8,128)} %get-tuple-element.36.refs_1_, f32[16,64,256]{2,1,0:T(8,128)} %copy-done.1, f32[8,64,256]{2,1,0:T(8,128)} %copy-done.3, ...), custom_call_target="tpu_custom_call" | custom-call | tf_op jit(solution)/shard_map/pallas_call | solution.py:326
  108.7 3.4 %collective-permute-start.9 = (f32[30,16,256]{2,1,0:T(8,128)}, f32[30,16,256]{2,1,0:T(8,128)S(1)}, u32[]{:S(2)}, u32[]{:S(2)}) collective-permute-start(f32[30,16,256]{2,1,0:T(8,128)} %get-tuple-element.41.y_low), channel_id=1, source_target_pairs={{16,0},{2,16},{18,2},{4,18},{20,4},{6,20},{22,6},{8,22},{24,8},{10... | collective-permute-start | bytes 1474568 | tf_op jit(solution)/shard_map/ppermute | solution.py:37
  112.1 4.5 %collective-permute-start.8 = (f32[30,16,256]{2,1,0:T(8,128)}, f32[30,16,256]{2,1,0:T(8,128)S(1)}, u32[]{:S(2)}, u32[]{:S(2)}) collective-permute-start(f32[30,16,256]{2,1,0:T(8,128)} %get-tuple-element.43.y_high), channel_id=1, source_target_pairs={{0,16},{16,2},{2,18},{18,4},{4,20},{20,6},{6,22},{22,8},{8,24},{24... | collective-permute-start | bytes 1474568 | tf_op jit(solution)/shard_map/ppermute | solution.py:37
  116.6 7.5 %collective-permute-done.9.from_above = f32[30,16,256]{2,1,0:T(8,128)S(1)} collective-permute-done((f32[30,16,256]{2,1,0:T(8,128)}, f32[30,16,256]{2,1,0:T(8,128)S(1)}, u32[]{:S(2)}, u32[]{:S(2)}) %collective-permute-start.9) | collective-permute-done | bytes 491552 | tf_op jit(solution)/shard_map/ppermute | solution.py:37
  124.1 2.9 %collective-permute-done.8.from_below = f32[30,16,256]{2,1,0:T(8,128)S(1)} collective-permute-done((f32[30,16,256]{2,1,0:T(8,128)}, f32[30,16,256]{2,1,0:T(8,128)S(1)}, u32[]{:S(2)}, u32[]{:S(2)}) %collective-permute-start.8) | collective-permute-done | bytes 491552 | tf_op jit(solution)/shard_map/ppermute | solution.py:37
  127.0 0.8 copy-done.10
  127.8 3.4 %shard_map.49 = (f32[14,80,256]{2,1,0:T(8,128)}, f32[2,80,256]{2,1,0:T(8,128)}, f32[14,80,256]{2,1,0:T(8,128)}) custom-call(f32[30,16,256]{2,1,0:T(8,128)} %get-tuple-element.41.y_low, f32[30,48,256]{2,1,0:T(8,128)} %get-tuple-element.42.y_mid, f32[30,16,256]{2,1,0:T(8,128)} %get-tuple-element.43.y_high, f32[30,16,256]{2,1,0:T(8,128)} %copy-done.10, ...), custom_call_target="tpu_custom_call" | custom-call | tf_op jit(solution)/shard_map/pallas_call | solution.py:326
  131.2 1.9 collective-permute-start.11
  133.2 2.6 %collective-permute-start.10 = (f32[14,80,256]{2,1,0:T(8,128)}, f32[14,80,256]{2,1,0:T(8,128)S(1)}, u32[]{:S(2)}, u32[]{:S(2)}) collective-permute-start(f32[14,80,256]{2,1,0:T(8,128)} %get-tuple-element.46.refs_3_), channel_id=1, source_target_pairs={{0,1},{16,17},{2,3},{18,19},{4,5},{20,21},{6,7},{22,23},{8,9},{24,... | collective-permute-start | bytes 3440648 | tf_op jit(solution)/shard_map/ppermute | solution.py:37
  135.8 11.1 %collective-permute-done.11.refs_5_ = f32[14,80,256]{2,1,0:T(8,128)S(1)} collective-permute-done((f32[14,80,256]{2,1,0:T(8,128)}, f32[14,80,256]{2,1,0:T(8,128)S(1)}, u32[]{:S(2)}, u32[]{:S(2)}) %collective-permute-start.11) | collective-permute-done | bytes 1146912 | tf_op jit(solution)/shard_map/ppermute | solution.py:37
  146.8 4.9 %collective-permute-done.10.refs_4_ = f32[14,80,256]{2,1,0:T(8,128)S(1)} collective-permute-done((f32[14,80,256]{2,1,0:T(8,128)}, f32[14,80,256]{2,1,0:T(8,128)S(1)}, u32[]{:S(2)}, u32[]{:S(2)}) %collective-permute-start.10) | collective-permute-done | bytes 1146912 | tf_op jit(solution)/shard_map/ppermute | solution.py:37
  151.8 1.0 copy-done.5
  152.7 17.1 %shard_map.50 = (f32[30,8,256]{2,1,0:T(8,128)}, f32[30,8,256]{2,1,0:T(8,128)}, f32[7,64,256]{2,1,0:T(8,128)}, f32[16,64,256]{2,1,0:T(8,128)}, f32[7,64,256]{2,1,0:T(8,128)}) custom-call(f32[2,15]{1,0:T(2,128)} %bitcast.3, f32[30,80,256]{2,1,0:T(8,128)} %get-tuple-element.34.refs_0_, f32[14,80,256]{2,1,0:T(8,128)} %get-tuple-element.44.refs_1_, ...), custom_call_target="tpu_custom_call" | custom-call | tf_op jit(solution)/shard_map/pallas_call | solution.py:326
  169.8 3.7 %collective-permute-start.12 = (f32[30,8,256]{2,1,0:T(8,128)}, f32[30,8,256]{2,1,0:T(8,128)S(1)}, u32[]{:S(2)}, u32[]{:S(2)}) collective-permute-start(f32[30,8,256]{2,1,0:T(8,128)} %get-tuple-element.50), channel_id=1, source_target_pairs={{0,16},{16,2},{2,18},{18,4},{4,20},{20,6},{6,22},{22,8},{8,24},{24... | collective-permute-start | bytes 737288 | tf_op jit(solution)/shard_map/ppermute | solution.py:37
  173.5 3.7 %collective-permute-start.13 = (f32[30,8,256]{2,1,0:T(8,128)}, f32[30,8,256]{2,1,0:T(8,128)S(1)}, u32[]{:S(2)}, u32[]{:S(2)}) collective-permute-start(f32[30,8,256]{2,1,0:T(8,128)} %get-tuple-element.51), channel_id=1, source_target_pairs={{16,0},{2,16},{18,2},{4,18},{20,4},{6,20},{22,6},{8,22},{24,8},{10... | collective-permute-start | bytes 737288 | tf_op jit(solution)/shard_map/ppermute | solution.py:37
  177.2 5.0 %collective-permute-done.12.from_below = f32[30,8,256]{2,1,0:T(8,128)S(1)} collective-permute-done((f32[30,8,256]{2,1,0:T(8,128)}, f32[30,8,256]{2,1,0:T(8,128)S(1)}, u32[]{:S(2)}, u32[]{:S(2)}) %collective-permute-start.12) | collective-permute-done | bytes 245792 | tf_op jit(solution)/shard_map/ppermute | solution.py:37
  182.2 2.6 %collective-permute-done.13.from_above = f32[30,8,256]{2,1,0:T(8,128)S(1)} collective-permute-done((f32[30,8,256]{2,1,0:T(8,128)}, f32[30,8,256]{2,1,0:T(8,128)S(1)}, u32[]{:S(2)}, u32[]{:S(2)}) %collective-permute-start.13) | collective-permute-done | bytes 245792 | tf_op jit(solution)/shard_map/ppermute | solution.py:37
  184.8 0.7 copy-done.12
  185.5 3.0 %shard_map.51 = (f32[7,64,256]{2,1,0:T(8,128)}, f32[16,64,256]{2,1,0:T(8,128)}, f32[7,64,256]{2,1,0:T(8,128)}) custom-call(f32[7,64,256]{2,1,0:T(8,128)} %get-tuple-element.47.z_low, f32[16,64,256]{2,1,0:T(8,128)} %get-tuple-element.48.z_mid, f32[7,64,256]{2,1,0:T(8,128)} %get-tuple-element.49.z_high, f32[30,8,256]{2,1,0:T(8,128)} %copy-done.11, ...), custom_call_target="tpu_custom_call" | custom-call | tf_op jit(solution)/shard_map/pallas_call | solution.py:326
  188.5 1.9 collective-permute-start.14
  190.4 1.9 collective-permute-start.15
  192.4 7.5 %collective-permute-start.16 = (f32[7,64,256]{2,1,0:T(8,128)}, f32[7,64,256]{2,1,0:T(8,128)S(1)}, u32[]{:S(2)}, u32[]{:S(2)}) collective-permute-start(f32[7,64,256]{2,1,0:T(8,128)} %get-tuple-element.54), channel_id=1, source_target_pairs={{1,0},{17,1},{3,2},{19,3},{5,4},{21,5},{7,6},{23,7},{9,8},{25,9},{... | collective-permute-start | bytes 1376264 | tf_op jit(solution)/shard_map/ppermute | solution.py:37
  199.9 16.3 %collective-permute-done.14 = f32[16,64,256]{2,1,0:T(8,128)S(1)} collective-permute-done((f32[16,64,256]{2,1,0:T(8,128)}, f32[16,64,256]{2,1,0:T(8,128)S(1)}, u32[]{:S(2)}, u32[]{:S(2)}) %collective-permute-start.14) | collective-permute-done | bytes 1048608 | tf_op jit(solution)/shard_map/ppermute | solution.py:37
  216.2 0.1 slice_add_fusion.1
  216.3 1.1 pad_maximum_fusion
  (40 shorter events, 0.4 us)
Async XLA Ops:
  0.0 20.0 %copy-start.6 = (f32[16,64,256]{2,1,0:T(8,128)S(1)}, f32[16,64,256]{2,1,0:T(8,128)}, u32[]{:S(2)}) copy-start(f32[16,64,256]{2,1,0:T(8,128)} %param.5) | copy-start | bytes 3145732
  0.0 18.0 %collective-permute-start = (f32[16,64,256]{2,1,0:T(8,128)}, f32[16,64,256]{2,1,0:T(8,128)S(1)}, u32[]{:S(2)}, u32[]{:S(2)}) collective-permute-start(f32[16,64,256]{2,1,0:T(8,128)} %param.6), channel_id=1, source_target_pairs={{0,0},{1,16},{2,2},{3,18},{4,4},{5,20},{6,6},{7,22},{8,8},{9,24},{... | collective-permute-start | bytes 3145736 | tf_op jit(solution)/shard_map/ppermute | solution.py:37
  18.0 12.6 %copy-start = (f32[16,64,256]{2,1,0:T(8,128)}, f32[16,64,256]{2,1,0:T(8,128)S(1)}, u32[]{:S(2)}) copy-start(f32[16,64,256]{2,1,0:T(8,128)S(1)} %collective-permute-done.refs_0_) | copy-start | bytes 3145732
  18.0 34.2 %collective-permute-start.2 = (f32[7,64,256]{2,1,0:T(8,128)S(1)}, f32[7,64,256]{2,1,0:T(8,128)S(1)}, u32[]{:S(2)}, u32[]{:S(2)}) collective-permute-start(f32[7,64,256]{2,1,0:T(8,128)S(1)} %get-tuple-element.61), channel_id=1, source_target_pairs={{1,0},{17,16},{3,2},{19,18},{5,4},{21,20},{7,6},{23,22},{9,8},{25,... | collective-permute-start | bytes 1376264 | tf_op jit(solution)/shard_map/ppermute | solution.py:37
  21.0 62.5 %copy-start.16 = (f32[2,3,15]{2,0,1:T(2,128)S(1)}, f32[2,3,15]{2,0,1:T(2,128)}, u32[]{:S(2)}) copy-start(f32[2,3,15]{2,0,1:T(2,128)} %param.7) | copy-start | bytes 1084
  21.0 77.2 %collective-permute-start.7 = (f32[8,64,256]{2,1,0:T(8,128)}, f32[8,64,256]{2,1,0:T(8,128)S(1)}, u32[]{:S(2)}, u32[]{:S(2)}) collective-permute-start(f32[8,64,256]{2,1,0:T(8,128)} %get-tuple-element.57), channel_id=1, source_target_pairs={{0,225},{1,241},{2,227},{3,243},{4,229},{5,245},{6,231},{7,247},{8... | collective-permute-start | bytes 1572872 | tf_op jit(solution)/shard_map/ppermute | solution.py:37
  21.4 76.9 %collective-permute-start.6 = (f32[8,64,256]{2,1,0:T(8,128)}, f32[8,64,256]{2,1,0:T(8,128)S(1)}, u32[]{:S(2)}, u32[]{:S(2)}) collective-permute-start(f32[8,64,256]{2,1,0:T(8,128)} %get-tuple-element.58), channel_id=1, source_target_pairs={{0,225},{1,241},{2,227},{3,243},{4,229},{5,245},{6,231},{7,247},{8... | collective-permute-start | bytes 1572872 | tf_op jit(solution)/shard_map/ppermute | solution.py:37
  24.4 73.9 %collective-permute-start.5 = (f32[16,64,256]{2,1,0:T(8,128)}, f32[16,64,256]{2,1,0:T(8,128)S(1)}, u32[]{:S(2)}, u32[]{:S(2)}) collective-permute-start(f32[16,64,256]{2,1,0:T(8,128)} %param.4), channel_id=1, source_target_pairs={{0,0},{1,16},{2,2},{3,18},{4,4},{5,20},{6,6},{7,22},{8,8},{9,24},{... | collective-permute-start | bytes 3145736 | tf_op jit(solution)/shard_map/ppermute | solution.py:37
  28.6 46.7 %collective-permute-start.1 = (f32[7,64,256]{2,1,0:T(8,128)S(1)}, f32[7,64,256]{2,1,0:T(8,128)S(1)}, u32[]{:S(2)}, u32[]{:S(2)}) collective-permute-start(f32[7,64,256]{2,1,0:T(8,128)S(1)} %get-tuple-element.62), channel_id=1, source_target_pairs={{0,1},{16,17},{2,3},{18,19},{4,5},{20,21},{6,7},{22,23},{8,9},{24,... | collective-permute-start | bytes 1376264 | tf_op jit(solution)/shard_map/ppermute | solution.py:37
  52.2 0.8 copy-start.7
  75.3 0.8 copy-start.8
  76.2 11.3 %collective-permute-start.3 = (f32[30,8,256]{2,1,0:T(8,128)S(1)}, f32[30,8,256]{2,1,0:T(8,128)S(1)}, u32[]{:S(2)}, u32[]{:S(2)}) collective-permute-start(f32[30,8,256]{2,1,0:T(8,128)S(1)} %pad_maximum_fusion.1), channel_id=1, source_target_pairs={{0,16},{16,2},{2,18},{18,4},{4,20},{20,6},{6,22},{22,8},{8,24},{24... | collective-permute-start | bytes 737288 | tf_op jit(solution)/shard_map/ppermute | solution.py:37
  79.5 10.2 %collective-permute-start.4 = (f32[30,8,256]{2,1,0:T(8,128)S(1)}, f32[30,8,256]{2,1,0:T(8,128)S(1)}, u32[]{:S(2)}, u32[]{:S(2)}) collective-permute-start(f32[30,8,256]{2,1,0:T(8,128)S(1)} %pad_maximum_fusion.2), channel_id=1, source_target_pairs={{16,0},{2,16},{18,2},{4,18},{20,4},{6,20},{22,6},{8,22},{24,8},{10... | collective-permute-start | bytes 737288 | tf_op jit(solution)/shard_map/ppermute | solution.py:37
  83.8 0.6 copy-start.15
  87.4 2.3 %copy-start.13 = (f32[30,8,256]{2,1,0:T(8,128)}, f32[30,8,256]{2,1,0:T(8,128)S(1)}, u32[]{:S(2)}) copy-start(f32[30,8,256]{2,1,0:T(8,128)S(1)} %collective-permute-done.3.refs_3_) | copy-start | bytes 737284
  89.7 0.7 copy-start.14
  98.2 0.8 copy-start.2
  98.2 1.0 copy-start.3
  98.3 1.3 copy-start.1
  108.7 15.4 %collective-permute-start.9 = (f32[30,16,256]{2,1,0:T(8,128)}, f32[30,16,256]{2,1,0:T(8,128)S(1)}, u32[]{:S(2)}, u32[]{:S(2)}) collective-permute-start(f32[30,16,256]{2,1,0:T(8,128)} %get-tuple-element.41.y_low), channel_id=1, source_target_pairs={{16,0},{2,16},{18,2},{4,18},{20,4},{6,20},{22,6},{8,22},{24,8},{10... | collective-permute-start | bytes 1474568 | tf_op jit(solution)/shard_map/ppermute | solution.py:37
  112.1 14.9 %collective-permute-start.8 = (f32[30,16,256]{2,1,0:T(8,128)}, f32[30,16,256]{2,1,0:T(8,128)S(1)}, u32[]{:S(2)}, u32[]{:S(2)}) collective-permute-start(f32[30,16,256]{2,1,0:T(8,128)} %get-tuple-element.43.y_high), channel_id=1, source_target_pairs={{0,16},{16,2},{2,18},{18,4},{4,20},{20,6},{6,22},{22,8},{8,24},{24... | collective-permute-start | bytes 1474568 | tf_op jit(solution)/shard_map/ppermute | solution.py:37
  124.1 2.9 %copy-start.9 = (f32[30,16,256]{2,1,0:T(8,128)}, f32[30,16,256]{2,1,0:T(8,128)S(1)}, u32[]{:S(2)}) copy-start(f32[30,16,256]{2,1,0:T(8,128)S(1)} %collective-permute-done.9.from_above) | copy-start | bytes 1474564
  127.0 0.8 copy-start.10
  131.2 15.6 %collective-permute-start.11 = (f32[14,80,256]{2,1,0:T(8,128)}, f32[14,80,256]{2,1,0:T(8,128)S(1)}, u32[]{:S(2)}, u32[]{:S(2)}) collective-permute-start(f32[14,80,256]{2,1,0:T(8,128)} %get-tuple-element.44.refs_1_), channel_id=1, source_target_pairs={{1,0},{17,16},{3,2},{19,18},{5,4},{21,20},{7,6},{23,22},{9,8},{25,... | collective-permute-start | bytes 3440648 | tf_op jit(solution)/shard_map/ppermute | solution.py:37
  133.2 18.6 %collective-permute-start.10 = (f32[14,80,256]{2,1,0:T(8,128)}, f32[14,80,256]{2,1,0:T(8,128)S(1)}, u32[]{:S(2)}, u32[]{:S(2)}) collective-permute-start(f32[14,80,256]{2,1,0:T(8,128)} %get-tuple-element.46.refs_3_), channel_id=1, source_target_pairs={{0,1},{16,17},{2,3},{18,19},{4,5},{20,21},{6,7},{22,23},{8,9},{24,... | collective-permute-start | bytes 3440648 | tf_op jit(solution)/shard_map/ppermute | solution.py:37
  146.8 4.9 %copy-start.4 = (f32[14,80,256]{2,1,0:T(8,128)}, f32[14,80,256]{2,1,0:T(8,128)S(1)}, u32[]{:S(2)}) copy-start(f32[14,80,256]{2,1,0:T(8,128)S(1)} %collective-permute-done.11.refs_5_) | copy-start | bytes 3440644
  151.7 1.0 copy-start.5
  169.8 12.4 %collective-permute-start.12 = (f32[30,8,256]{2,1,0:T(8,128)}, f32[30,8,256]{2,1,0:T(8,128)S(1)}, u32[]{:S(2)}, u32[]{:S(2)}) collective-permute-start(f32[30,8,256]{2,1,0:T(8,128)} %get-tuple-element.50), channel_id=1, source_target_pairs={{0,16},{16,2},{2,18},{18,4},{4,20},{20,6},{6,22},{22,8},{8,24},{24... | collective-permute-start | bytes 737288 | tf_op jit(solution)/shard_map/ppermute | solution.py:37
  173.5 11.4 %collective-permute-start.13 = (f32[30,8,256]{2,1,0:T(8,128)}, f32[30,8,256]{2,1,0:T(8,128)S(1)}, u32[]{:S(2)}, u32[]{:S(2)}) collective-permute-start(f32[30,8,256]{2,1,0:T(8,128)} %get-tuple-element.51), channel_id=1, source_target_pairs={{16,0},{2,16},{18,2},{4,18},{20,4},{6,20},{22,6},{8,22},{24,8},{10... | collective-permute-start | bytes 737288 | tf_op jit(solution)/shard_map/ppermute | solution.py:37
  182.2 2.6 %copy-start.11 = (f32[30,8,256]{2,1,0:T(8,128)}, f32[30,8,256]{2,1,0:T(8,128)S(1)}, u32[]{:S(2)}) copy-start(f32[30,8,256]{2,1,0:T(8,128)S(1)} %collective-permute-done.12.from_below) | copy-start | bytes 737284
  184.8 0.7 copy-start.12
  188.5 27.7 %collective-permute-start.14 = (f32[16,64,256]{2,1,0:T(8,128)}, f32[16,64,256]{2,1,0:T(8,128)S(1)}, u32[]{:S(2)}, u32[]{:S(2)}) collective-permute-start(f32[16,64,256]{2,1,0:T(8,128)} %get-tuple-element.52), channel_id=1, source_target_pairs={{0,0},{16,1},{2,2},{18,3},{4,4},{20,5},{6,6},{22,7},{8,8},{24,9},{... | collective-permute-start | bytes 3145736 | tf_op jit(solution)/shard_map/ppermute | solution.py:37
  190.4 25.8 %collective-permute-start.15 = (f32[7,64,256]{2,1,0:T(8,128)}, f32[7,64,256]{2,1,0:T(8,128)S(1)}, u32[]{:S(2)}, u32[]{:S(2)}) collective-permute-start(f32[7,64,256]{2,1,0:T(8,128)} %get-tuple-element.53), channel_id=1, source_target_pairs={{0,16},{16,17},{2,18},{18,19},{4,20},{20,21},{6,22},{22,23},{8,24}... | collective-permute-start | bytes 1376264 | tf_op jit(solution)/shard_map/ppermute | solution.py:37
  192.4 23.8 %collective-permute-start.16 = (f32[7,64,256]{2,1,0:T(8,128)}, f32[7,64,256]{2,1,0:T(8,128)S(1)}, u32[]{:S(2)}, u32[]{:S(2)}) collective-permute-start(f32[7,64,256]{2,1,0:T(8,128)} %get-tuple-element.54), channel_id=1, source_target_pairs={{1,0},{17,1},{3,2},{19,3},{5,4},{21,5},{7,6},{23,7},{9,8},{25,9},{... | collective-permute-start | bytes 1376264 | tf_op jit(solution)/shard_map/ppermute | solution.py:37

commit v4 on v3

--- a/solution.py
+++ b/solution.py
@@ -10,6 +10,7 @@
 
 EDGE = 8
 CHUNK = 4
+LIMIT = 24 << 20
 F32 = jnp.float32
 BF16 = jnp.bfloat16
 
@@ -24,7 +25,10 @@
 
 
 def working(slab, tile):
-    return given(slab - slab % 2 + tile % 2, tile - tile % 2 + slab % 2)
+    column, step = divmod(tile, 4)
+    if column % 2:
+        step = 3 - step
+    return given(slab - slab % 2 + step // 2, 4 * column + 2 * (step % 2) + slab % 2)
 
 
 def moved(value, source, target, change):
@@ -35,10 +39,6 @@
             if 0 <= to_slab < SLABS and 0 <= to_tile < TILES:
                 pairs.append((source(slab, tile), target(to_slab, to_tile)))
     return lax.ppermute(value, AXES, pairs)
-
-
-def placed(value):
-    return moved(value, given, working, lambda slab, tile: (slab, tile))
 
 
 def along_slabs(value, step):
@@ -202,12 +202,12 @@
 
 class Mirrored:
     def __init__(self, low_half, high_half):
-        planes = [(half, z) for half in (low_half, high_half) for z in range(half.shape[0])]
+        planes = [(ref, z) for ref in (low_half, high_half) for z in range(ref.shape[0])]
         self.planes = planes[::-1]
 
     def __getitem__(self, index):
-        half, z = self.planes[index]
-        return half[z]
+        ref, z = self.planes[index]
+        return ref[z]
 
 
 def forward_kernel(taps_ref, *refs):
@@ -329,6 +329,7 @@
         in_specs=[smem] * scalars + [vmem] * (len(arrays) - scalars),
         out_specs=[vmem] * len(outs),
         scratch_shapes=[pltpu.VMEM(shape, F32) for shape in scratch],
+        compiler_params=pltpu.CompilerParams(vmem_limit_bytes=LIMIT),
     )(*arrays)
 
 
@@ -339,23 +340,26 @@
     z_taps = kernels[:, 0]
     one, two = filter_matrices(kernels, rows, width)
     full = depth + 2 * reach
+
+    def same(slab, tile):
+        return slab, tile
+
+    def across(slab, tile):
+        return SLABS - 1 - slab, tile
+
     half = depth // 2
-
-    def mirror(value):
-        return moved(value, given, working, lambda slab, tile: (SLABS - 1 - slab, tile))
-
-    estimate = placed(estimate)
-    first_half = mirror(view_two[:half])
-    z_low = along_slabs(estimate[depth - reach :], 1)
-    z_high = along_slabs(estimate[:reach], -1)
-    second_half = mirror(view_two[half:])
+    first_half = moved(view_two[:half], given, working, across)
+    z_low = moved(estimate[depth - reach :], given, working, lambda s, t: (s + 1, t))
+    z_high = moved(estimate[:reach], given, working, lambda s, t: (s - 1, t))
+    second_half = moved(view_two[half:], given, working, across)
+    estimate = moved(estimate, given, working, same)
 
     def rows_of(window):
         return jnp.concatenate([z_low[:, window], estimate[:, window], z_high[:, window]], axis=0)
 
     y_low = along_tiles(rows_of(slice(-EDGE, None)), 1)
     y_high = along_tiles(rows_of(slice(None, EDGE)), -1)
-    view_one = placed(view_one)
+    view_one = moved(view_one, given, working, same)
 
     tall = (depth, rows + 2 * EDGE, width)
     extended = (full, rows + 2 * EDGE, width)
@@ -397,17 +401,17 @@
         [piece.shape for piece in pieces],
         scalars=0,
     )
-    center = moved(z_mid, working, given, lambda slab, tile: (slab, tile))
-    from_below = moved(z_high, working, given, lambda slab, tile: (slab + 1, tile))
-    from_above = moved(z_low, working, given, lambda slab, tile: (slab - 1, tile))
-    return jnp.concatenate(
+    from_below = along_slabs(z_high, 1)
+    from_above = along_slabs(z_low, -1)
+    result = jnp.concatenate(
         [
-            center[:reach] + from_below,
-            center[reach : depth - reach],
-            center[depth - reach :] + from_above,
+            z_mid[:reach] + from_below,
+            z_mid[reach : depth - reach],
+            z_mid[depth - reach :] + from_above,
         ],
         axis=0,
     )
+    return moved(result, working, given, same)
 
 
 def solution(mesh):

time: 218 us -> 198 us (0.908)
  the two profiles are of different devices: /device:TPU:154 before, /device:TPU:127 now
where the time goes in v4:
time: 198 us; the launch traced here: 197 us
  starting transfers between devices  82.9 us (42%)
  waiting for transfers between devices  74.1 us (37%)
  Pallas kernels  28.2 us (14%)
  local copies, waits for them, and re-layouts  10.2 us (5%)
    ppermute x17, starting transfers between devices, moved(): return lax.ppermute(value, AXES, pairs)  82.9 us
    ppermute x17, waiting for transfers between devices, moved(): return lax.ppermute(value, AXES, pairs)  74.1 us
    pallas_call x5, Pallas kernels, call(): pl.pallas_call(kernel, out_shape=[jax.ShapeDtypeStruct(shape, F32) for sh...  25.2 us
    unnamed x35, local copies, waits for them, and re-layouts  7.75 us
  transfers between devices with their start and end apart: 17, of which 12 were waited for; matrix products, arithmetic and copies ran while one was open for 2% of the time, Pallas kernels for 5%

profile of v4, /device:TPU:127, one launch (start us, length us, event | category | flops | bytes accessed | tf_op | source)
XLA Modules:
  0.0 197.5 jit_solution(5461623899205458022)
XLA Ops:
  0.0 2.0 %collective-permute-start = (f32[16,64,256]{2,1,0:T(8,128)}, f32[16,64,256]{2,1,0:T(8,128)S(1)}, u32[]{:S(2)}, u32[]{:S(2)}) collective-permute-start(f32[16,64,256]{2,1,0:T(8,128)} %param.6), channel_id=1, source_target_pairs={{0,0},{1,2},{2,16},{3,18},{4,22},{5,20},{6,6},{7,4},{8,8},{9,10},{... | collective-permute-start | bytes 3145736 | tf_op jit(solution)/shard_map/ppermute | solution.py:41
  2.0 1.2 fusion.2
  3.3 5.4 %collective-permute-start.2 = (f32[7,64,256]{2,1,0:T(8,128)S(1)}, f32[7,64,256]{2,1,0:T(8,128)S(1)}, u32[]{:S(2)}, u32[]{:S(2)}) collective-permute-start(f32[7,64,256]{2,1,0:T(8,128)S(1)} %get-tuple-element.61), channel_id=1, source_target_pairs={{16,0},{17,2},{18,16},{19,18},{20,22},{21,20},{22,6},{23,4},{24,8}... | collective-permute-start | bytes 1376264 | tf_op jit(solution)/shard_map/ppermute | solution.py:41
  8.7 4.5 %collective-permute-start.1 = (f32[7,64,256]{2,1,0:T(8,128)S(1)}, f32[7,64,256]{2,1,0:T(8,128)S(1)}, u32[]{:S(2)}, u32[]{:S(2)}) collective-permute-start(f32[7,64,256]{2,1,0:T(8,128)S(1)} %get-tuple-element.62), channel_id=1, source_target_pairs={{0,1},{1,3},{2,17},{3,19},{4,23},{5,21},{6,7},{7,5},{8,9},{9,11},{... | collective-permute-start | bytes 1376264 | tf_op jit(solution)/shard_map/ppermute | solution.py:41
  13.2 1.0 fusion
  14.3 2.9 %collective-permute-start.7 = (f32[8,64,256]{2,1,0:T(8,128)}, f32[8,64,256]{2,1,0:T(8,128)S(1)}, u32[]{:S(2)}, u32[]{:S(2)}) collective-permute-start(f32[8,64,256]{2,1,0:T(8,128)} %get-tuple-element.57), channel_id=1, source_target_pairs={{0,225},{1,227},{2,241},{3,243},{4,247},{5,245},{6,231},{7,229},{8... | collective-permute-start | bytes 1572872 | tf_op jit(solution)/shard_map/ppermute | solution.py:41
  17.2 2.1 %collective-permute-start.6 = (f32[8,64,256]{2,1,0:T(8,128)}, f32[8,64,256]{2,1,0:T(8,128)S(1)}, u32[]{:S(2)}, u32[]{:S(2)}) collective-permute-start(f32[8,64,256]{2,1,0:T(8,128)} %get-tuple-element.58), channel_id=1, source_target_pairs={{0,225},{1,227},{2,241},{3,243},{4,247},{5,245},{6,231},{7,229},{8... | collective-permute-start | bytes 1572872 | tf_op jit(solution)/shard_map/ppermute | solution.py:41
  19.3 4.5 %collective-permute-done.2.refs_2_ = f32[7,64,256]{2,1,0:T(8,128)S(1)} collective-permute-done((f32[7,64,256]{2,1,0:T(8,128)S(1)}, f32[7,64,256]{2,1,0:T(8,128)S(1)}, u32[]{:S(2)}, u32[]{:S(2)}) %collective-permute-start.2) | collective-permute-done | bytes 458784 | tf_op jit(solution)/shard_map/ppermute | solution.py:41
  23.8 23.8 %collective-permute-start.5 = (f32[16,64,256]{2,1,0:T(8,128)}, f32[16,64,256]{2,1,0:T(8,128)S(1)}, u32[]{:S(2)}, u32[]{:S(2)}) collective-permute-start(f32[16,64,256]{2,1,0:T(8,128)} %param.4), channel_id=1, source_target_pairs={{0,0},{1,2},{2,16},{3,18},{4,22},{5,20},{6,6},{7,4},{8,8},{9,10},{... | collective-permute-start | bytes 3145736 | tf_op jit(solution)/shard_map/ppermute | solution.py:41
  47.7 0.7 copy-done.8
  48.4 0.7 pad_maximum_fusion.1
  49.1 1.9 collective-permute-start.3
  51.0 0.7 pad_maximum_fusion.2
  51.7 3.4 %collective-permute-start.4 = (f32[30,8,256]{2,1,0:T(8,128)}, f32[30,8,256]{2,1,0:T(8,128)}, u32[]{:S(2)}, u32[]{:S(2)}) collective-permute-start(f32[30,8,256]{2,1,0:T(8,128)} %pad_maximum_fusion.2), channel_id=1, source_target_pairs={{2,0},{16,2},{18,16},{22,18},{20,22},{6,20},{4,6},{8,4},{10,8},{24... | collective-permute-start | bytes 737288 | tf_op jit(solution)/shard_map/ppermute | solution.py:41
  55.4 0.6 copy-done.15
  56.0 3.0 %shard_map.46 = (bf16[64,240]{1,0:T(8,128)(2,1)}, bf16[80,192]{1,0:T(8,128)(2,1)}, bf16[2,256,256]{2,1,0:T(8,128)(2,1)}, bf16[2,256,256]{2,1,0:T(8,128)(2,1)}, b...) custom-call(f32[2,3,15]{2,1,0:T(4,128)} %copy-done.15), custom_call_target="tpu_custom_call" | custom-call | tf_op jit(solution)/shard_map/pallas_call | solution.py:91
  59.0 2.3 %collective-permute-done.3.refs_3_ = f32[30,8,256]{2,1,0:T(8,128)S(1)} collective-permute-done((f32[30,8,256]{2,1,0:T(8,128)}, f32[30,8,256]{2,1,0:T(8,128)S(1)}, u32[]{:S(2)}, u32[]{:S(2)}) %collective-permute-start.3) | collective-permute-done | bytes 245792 | tf_op jit(solution)/shard_map/ppermute | solution.py:41
  61.3 3.3 %collective-permute-done.4.refs_4_ = f32[30,8,256]{2,1,0:T(8,128)} collective-permute-done((f32[30,8,256]{2,1,0:T(8,128)}, f32[30,8,256]{2,1,0:T(8,128)}, u32[]{:S(2)}, u32[]{:S(2)}) %collective-permute-start.4) | collective-permute-done | bytes 245792 | tf_op jit(solution)/shard_map/ppermute | solution.py:41
  64.5 0.9 copy-done
  65.5 0.9 copy-done.2
  66.4 1.0 copy-done.7
  67.4 1.0 copy-done.9
  68.5 0.8 copy-done.12
  69.2 0.8 copy-done.13
  70.0 6.0 %shard_map.47 = (f32[30,80,256]{2,1,0:T(8,128)S(1)}, f32[16,64,256]{2,1,0:T(8,128)S(1)}, f32[16,64,256]{2,1,0:T(8,128)S(1)}) custom-call(f32[2,15]{1,0:T(2,128)S(1)} %bitcast.1, f32[16,64,256]{2,1,0:T(8,128)S(1)} %collective-permute-done.refs_0_, f32[7,64,256]{2,1,0:T(8,128)S(1)} %copy-done.9, f32[7,64,256]{2,1,0:T(8,128)S(1)} %copy-done.7, ...), custom_call_target="tpu_custom_call" | custom-call | tf_op jit(solution)/shard_map/pallas_call | solution.py:326
  76.1 6.2 %shard_map.48 = (f32[30,16,256]{2,1,0:T(8,128)S(1)}, f32[30,48,256]{2,1,0:T(8,128)S(1)}, f32[30,16,256]{2,1,0:T(8,128)S(1)}) custom-call(f32[2,15]{1,0:T(2,128)S(1)} %bitcast.2, f32[16,64,256]{2,1,0:T(8,128)S(1)} %get-tuple-element.35.refs_0_, f32[16,64,256]{2,1,0:T(8,128)S(1)} %get-tuple-element.36.refs_1_, ...), custom_call_target="tpu_custom_call" | custom-call | tf_op jit(solution)/shard_map/pallas_call | solution.py:326
  82.2 1.9 collective-permute-start.9
  84.1 12.5 %collective-permute-start.8 = (f32[30,16,256]{2,1,0:T(8,128)S(1)}, f32[30,16,256]{2,1,0:T(8,128)S(1)}, u32[]{:S(2)}, u32[]{:S(2)}) collective-permute-start(f32[30,16,256]{2,1,0:T(8,128)S(1)} %get-tuple-element.43.y_high), channel_id=1, source_target_pairs={{0,2},{2,16},{16,18},{18,22},{22,20},{20,6},{6,4},{4,8},{8,10},{10... | collective-permute-start | bytes 1474568 | tf_op jit(solution)/shard_map/ppermute | solution.py:41
  96.6 9.3 %collective-permute-done.9.from_above = f32[30,16,256]{2,1,0:T(8,128)S(1)} collective-permute-done((f32[30,16,256]{2,1,0:T(8,128)S(1)}, f32[30,16,256]{2,1,0:T(8,128)S(1)}, u32[]{:S(2)}, u32[]{:S(2)}) %collective-permute-start.9) | collective-permute-done | bytes 491552 | tf_op jit(solution)/shard_map/ppermute | solution.py:41
  105.9 0.9 collective-permute-done.8.from_below
  106.8 0.2 shard_map.49
  107.0 3.2 %collective-permute-start.11 = (f32[14,80,256]{2,1,0:T(8,128)S(1)}, f32[14,80,256]{2,1,0:T(8,128)S(1)}, u32[]{:S(2)}, u32[]{:S(2)}) collective-permute-start(f32[14,80,256]{2,1,0:T(8,128)S(1)} %get-tuple-element.44.refs_1_), channel_id=1, source_target_pairs={{1,0},{3,2},{17,16},{19,18},{23,22},{21,20},{7,6},{5,4},{9,8},{11,... | collective-permute-start | bytes 3440648 | tf_op jit(solution)/shard_map/ppermute | solution.py:41
  110.1 3.8 %collective-permute-start.10 = (f32[14,80,256]{2,1,0:T(8,128)S(1)}, f32[14,80,256]{2,1,0:T(8,128)S(1)}, u32[]{:S(2)}, u32[]{:S(2)}) collective-permute-start(f32[14,80,256]{2,1,0:T(8,128)S(1)} %get-tuple-element.46.refs_3_), channel_id=1, source_target_pairs={{0,1},{2,3},{16,17},{18,19},{22,23},{20,21},{6,7},{4,5},{8,9},{10,... | collective-permute-start | bytes 3440648 | tf_op jit(solution)/shard_map/ppermute | solution.py:41
  113.9 11.4 %collective-permute-done.11.refs_5_ = f32[14,80,256]{2,1,0:T(8,128)S(1)} collective-permute-done((f32[14,80,256]{2,1,0:T(8,128)S(1)}, f32[14,80,256]{2,1,0:T(8,128)S(1)}, u32[]{:S(2)}, u32[]{:S(2)}) %collective-permute-start.11) | collective-permute-done | bytes 1146912 | tf_op jit(solution)/shard_map/ppermute | solution.py:41
  125.4 1.2 collective-permute-done.10.refs_4_
  126.5 12.7 %shard_map.50 = (f32[30,8,256]{2,1,0:T(8,128)S(1)}, f32[30,8,256]{2,1,0:T(8,128)S(1)}, f32[7,64,256]{2,1,0:T(8,128)S(1)}, f32[16,64,256]{2,1,0:T(8,128)S(1)}, f32[7,64,256]{2,1,0:T(8,128)S(1)}) custom-call(f32[2,15]{1,0:T(2,128)S(1)} %bitcast.3, f32[30,80,256]{2,1,0:T(8,128)S(1)} %get-tuple-element.34.refs_0_, f32[14,80,256]{2,1,0:T(8,128)S(1)} %get-tuple-element.44.refs_1_, ...), custom_call_target="tpu_custom_call" | custom-call | tf_op jit(solution)/shard_map/pallas_call | solution.py:326
  139.3 4.1 %collective-permute-start.12 = (f32[30,8,256]{2,1,0:T(8,128)S(1)}, f32[30,8,256]{2,1,0:T(8,128)S(1)}, u32[]{:S(2)}, u32[]{:S(2)}) collective-permute-start(f32[30,8,256]{2,1,0:T(8,128)S(1)} %get-tuple-element.50), channel_id=1, source_target_pairs={{0,2},{2,16},{16,18},{18,22},{22,20},{20,6},{6,4},{4,8},{8,10},{10... | collective-permute-start | bytes 737288 | tf_op jit(solution)/shard_map/ppermute | solution.py:41
  143.4 1.9 collective-permute-start.13
  145.3 2.6 %collective-permute-done.12.from_below = f32[30,8,256]{2,1,0:T(8,128)S(1)} collective-permute-done((f32[30,8,256]{2,1,0:T(8,128)S(1)}, f32[30,8,256]{2,1,0:T(8,128)S(1)}, u32[]{:S(2)}, u32[]{:S(2)}) %collective-permute-start.12) | collective-permute-done | bytes 245792 | tf_op jit(solution)/shard_map/ppermute | solution.py:41
  147.9 3.8 %collective-permute-done.13.from_above = f32[30,8,256]{2,1,0:T(8,128)S(1)} collective-permute-done((f32[30,8,256]{2,1,0:T(8,128)S(1)}, f32[30,8,256]{2,1,0:T(8,128)S(1)}, u32[]{:S(2)}, u32[]{:S(2)}) %collective-permute-start.13) | collective-permute-done | bytes 245792 | tf_op jit(solution)/shard_map/ppermute | solution.py:41
  151.7 0.2 shard_map.51
  151.9 5.6 %collective-permute-start.14 = (f32[7,64,256]{2,1,0:T(8,128)S(1)}, f32[7,64,256]{2,1,0:T(8,128)S(1)}, u32[]{:S(2)}, u32[]{:S(2)}) collective-permute-start(f32[7,64,256]{2,1,0:T(8,128)S(1)} %get-tuple-element.53), channel_id=1, source_target_pairs={{0,1},{2,3},{16,17},{18,19},{22,23},{20,21},{6,7},{4,5},{8,9},{10,... | collective-permute-start | bytes 1376264 | tf_op jit(solution)/shard_map/ppermute | solution.py:41
  157.5 1.9 collective-permute-start.15
  159.5 3.5 %collective-permute-done.14 = f32[7,64,256]{2,1,0:T(8,128)S(1)} collective-permute-done((f32[7,64,256]{2,1,0:T(8,128)S(1)}, f32[7,64,256]{2,1,0:T(8,128)S(1)}, u32[]{:S(2)}, u32[]{:S(2)}) %collective-permute-start.14) | collective-permute-done | bytes 458784 | tf_op jit(solution)/shard_map/ppermute | solution.py:41
  163.0 5.6 %collective-permute-done.15 = f32[7,64,256]{2,1,0:T(8,128)S(1)} collective-permute-done((f32[7,64,256]{2,1,0:T(8,128)S(1)}, f32[7,64,256]{2,1,0:T(8,128)S(1)}, u32[]{:S(2)}, u32[]{:S(2)}) %collective-permute-start.15) | collective-permute-done | bytes 458784 | tf_op jit(solution)/shard_map/ppermute | solution.py:41
  168.8 1.9 collective-permute-start.16
  170.7 25.8 %collective-permute-done.16 = f32[16,64,256]{2,1,0:T(8,128)S(1)} collective-permute-done((f32[16,64,256]{2,1,0:T(8,128)S(1)}, f32[16,64,256]{2,1,0:T(8,128)S(1)}, u32[]{:S(2)}, u32[]{:S(2)}) %collective-permute-start.16) | collective-permute-done | bytes 1048608 | tf_op jit(solution)/shard_map/ppermute | solution.py:41
  196.5 1.0 copy.10
  (41 shorter events, 0.6 us)
Async XLA Ops:
  0.0 13.2 %copy-start.14 = (f32[16,64,256]{2,1,0:T(8,128)S(1)}, f32[16,64,256]{2,1,0:T(8,128)}, u32[]{:S(2)}) copy-start(f32[16,64,256]{2,1,0:T(8,128)} %param.5) | copy-start | bytes 3145732
  0.0 47.7 %collective-permute-start = (f32[16,64,256]{2,1,0:T(8,128)}, f32[16,64,256]{2,1,0:T(8,128)S(1)}, u32[]{:S(2)}, u32[]{:S(2)}) collective-permute-start(f32[16,64,256]{2,1,0:T(8,128)} %param.6), channel_id=1, source_target_pairs={{0,0},{1,2},{2,16},{3,18},{4,22},{5,20},{6,6},{7,4},{8,8},{9,10},{... | collective-permute-start | bytes 3145736 | tf_op jit(solution)/shard_map/ppermute | solution.py:41
  3.3 20.6 %collective-permute-start.2 = (f32[7,64,256]{2,1,0:T(8,128)S(1)}, f32[7,64,256]{2,1,0:T(8,128)S(1)}, u32[]{:S(2)}, u32[]{:S(2)}) collective-permute-start(f32[7,64,256]{2,1,0:T(8,128)S(1)} %get-tuple-element.61), channel_id=1, source_target_pairs={{16,0},{17,2},{18,16},{19,18},{20,22},{21,20},{22,6},{23,4},{24,8}... | collective-permute-start | bytes 1376264 | tf_op jit(solution)/shard_map/ppermute | solution.py:41
  8.7 38.9 %collective-permute-start.1 = (f32[7,64,256]{2,1,0:T(8,128)S(1)}, f32[7,64,256]{2,1,0:T(8,128)S(1)}, u32[]{:S(2)}, u32[]{:S(2)}) collective-permute-start(f32[7,64,256]{2,1,0:T(8,128)S(1)} %get-tuple-element.62), channel_id=1, source_target_pairs={{0,1},{1,3},{2,17},{3,19},{4,23},{5,21},{6,7},{7,5},{8,9},{9,11},{... | collective-permute-start | bytes 1376264 | tf_op jit(solution)/shard_map/ppermute | solution.py:41
  14.2 40.9 %copy-start.16 = (f32[2,3,15]{2,0,1:T(2,128)S(1)}, f32[2,3,15]{2,0,1:T(2,128)}, u32[]{:S(2)}) copy-start(f32[2,3,15]{2,0,1:T(2,128)} %param.7) | copy-start | bytes 1084
  14.3 61.7 %collective-permute-start.7 = (f32[8,64,256]{2,1,0:T(8,128)}, f32[8,64,256]{2,1,0:T(8,128)S(1)}, u32[]{:S(2)}, u32[]{:S(2)}) collective-permute-start(f32[8,64,256]{2,1,0:T(8,128)} %get-tuple-element.57), channel_id=1, source_target_pairs={{0,225},{1,227},{2,241},{3,243},{4,247},{5,245},{6,231},{7,229},{8... | collective-permute-start | bytes 1572872 | tf_op jit(solution)/shard_map/ppermute | solution.py:41
  17.2 58.8 %collective-permute-start.6 = (f32[8,64,256]{2,1,0:T(8,128)}, f32[8,64,256]{2,1,0:T(8,128)S(1)}, u32[]{:S(2)}, u32[]{:S(2)}) collective-permute-start(f32[8,64,256]{2,1,0:T(8,128)} %get-tuple-element.58), channel_id=1, source_target_pairs={{0,225},{1,227},{2,241},{3,243},{4,247},{5,245},{6,231},{7,229},{8... | collective-permute-start | bytes 1572872 | tf_op jit(solution)/shard_map/ppermute | solution.py:41
  23.8 23.8 %copy-start.6 = (f32[7,64,256]{2,1,0:T(8,128)}, f32[7,64,256]{2,1,0:T(8,128)S(1)}, u32[]{:S(2)}) copy-start(f32[7,64,256]{2,1,0:T(8,128)S(1)} %collective-permute-done.2.refs_2_) | copy-start | bytes 1376260
  23.8 52.2 %collective-permute-start.5 = (f32[16,64,256]{2,1,0:T(8,128)}, f32[16,64,256]{2,1,0:T(8,128)S(1)}, u32[]{:S(2)}, u32[]{:S(2)}) collective-permute-start(f32[16,64,256]{2,1,0:T(8,128)} %param.4), channel_id=1, source_target_pairs={{0,0},{1,2},{2,16},{3,18},{4,22},{5,20},{6,6},{7,4},{8,8},{9,10},{... | collective-permute-start | bytes 3145736 | tf_op jit(solution)/shard_map/ppermute | solution.py:41
  47.6 0.8 copy-start.8
  49.1 12.1 %collective-permute-start.3 = (f32[30,8,256]{2,1,0:T(8,128)}, f32[30,8,256]{2,1,0:T(8,128)S(1)}, u32[]{:S(2)}, u32[]{:S(2)}) collective-permute-start(f32[30,8,256]{2,1,0:T(8,128)} %pad_maximum_fusion.1), channel_id=1, source_target_pairs={{0,2},{2,16},{16,18},{18,22},{22,20},{20,6},{6,4},{4,8},{8,10},{10... | collective-permute-start | bytes 737288 | tf_op jit(solution)/shard_map/ppermute | solution.py:41
  51.7 12.8 %collective-permute-start.4 = (f32[30,8,256]{2,1,0:T(8,128)}, f32[30,8,256]{2,1,0:T(8,128)}, u32[]{:S(2)}, u32[]{:S(2)}) collective-permute-start(f32[30,8,256]{2,1,0:T(8,128)} %pad_maximum_fusion.2), channel_id=1, source_target_pairs={{2,0},{16,2},{18,16},{22,18},{20,22},{6,20},{4,6},{8,4},{10,8},{24... | collective-permute-start | bytes 737288 | tf_op jit(solution)/shard_map/ppermute | solution.py:41
  55.4 0.6 copy-start.15
  64.5 1.0 copy-start
  65.5 0.9 copy-start.2
  66.4 1.0 copy-start.7
  67.4 1.0 copy-start.9
  68.5 0.8 copy-start.12
  69.2 0.8 copy-start.13
  70.0 6.0 %copy-start.4 = (bf16[2,256,256]{2,1,0:T(8,128)(2,1)S(1)}, bf16[2,256,256]{2,1,0:T(8,128)(2,1)}, u32[]{:S(2)}) copy-start(bf16[2,256,256]{2,1,0:T(8,128)(2,1)} %get-tuple-element.38.refs_6_.refs_12_) | copy-start | bytes 786436
  70.0 6.0 %copy-start.5 = (bf16[2,256,256]{2,1,0:T(8,128)(2,1)S(1)}, bf16[2,256,256]{2,1,0:T(8,128)(2,1)}, u32[]{:S(2)}) copy-start(bf16[2,256,256]{2,1,0:T(8,128)(2,1)} %get-tuple-element.40.refs_8_.refs_16_) | copy-start | bytes 786436
  70.0 6.1 %copy-start.10 = (bf16[80,192]{1,0:T(8,128)(2,1)S(1)}, bf16[80,192]{1,0:T(8,128)(2,1)}, u32[]{:S(2)}) copy-start(bf16[80,192]{1,0:T(8,128)(2,1)} %get-tuple-element.37.refs_5_.refs_10_) | copy-start | bytes 92164
  70.0 6.1 %copy-start.11 = (bf16[80,192]{1,0:T(8,128)(2,1)S(1)}, bf16[80,192]{1,0:T(8,128)(2,1)}, u32[]{:S(2)}) copy-start(bf16[80,192]{1,0:T(8,128)(2,1)} %get-tuple-element.39.refs_7_.refs_14_) | copy-start | bytes 92164
  82.2 23.6 %collective-permute-start.9 = (f32[30,16,256]{2,1,0:T(8,128)S(1)}, f32[30,16,256]{2,1,0:T(8,128)S(1)}, u32[]{:S(2)}, u32[]{:S(2)}) collective-permute-start(f32[30,16,256]{2,1,0:T(8,128)S(1)} %get-tuple-element.41.y_low), channel_id=1, source_target_pairs={{2,0},{16,2},{18,16},{22,18},{20,22},{6,20},{4,6},{8,4},{10,8},{24... | collective-permute-start | bytes 1474568 | tf_op jit(solution)/shard_map/ppermute | solution.py:41
  84.1 22.6 %collective-permute-start.8 = (f32[30,16,256]{2,1,0:T(8,128)S(1)}, f32[30,16,256]{2,1,0:T(8,128)S(1)}, u32[]{:S(2)}, u32[]{:S(2)}) collective-permute-start(f32[30,16,256]{2,1,0:T(8,128)S(1)} %get-tuple-element.43.y_high), channel_id=1, source_target_pairs={{0,2},{2,16},{16,18},{18,22},{22,20},{20,6},{6,4},{4,8},{8,10},{10... | collective-permute-start | bytes 1474568 | tf_op jit(solution)/shard_map/ppermute | solution.py:41
  106.8 19.8 %copy-start.1 = (bf16[2,256,256]{2,1,0:T(8,128)(2,1)S(1)}, bf16[2,256,256]{2,1,0:T(8,128)(2,1)}, u32[]{:S(2)}) copy-start(bf16[2,256,256]{2,1,0:T(8,128)(2,1)} %get-tuple-element.31.refs_6_.refs_11_) | copy-start | bytes 786436
  106.8 19.8 %copy-start.3 = (bf16[2,256,256]{2,1,0:T(8,128)(2,1)S(1)}, bf16[2,256,256]{2,1,0:T(8,128)(2,1)}, u32[]{:S(2)}) copy-start(bf16[2,256,256]{2,1,0:T(8,128)(2,1)} %get-tuple-element.33.refs_8_.refs_15_) | copy-start | bytes 786436
  107.0 18.4 %collective-permute-start.11 = (f32[14,80,256]{2,1,0:T(8,128)S(1)}, f32[14,80,256]{2,1,0:T(8,128)S(1)}, u32[]{:S(2)}, u32[]{:S(2)}) collective-permute-start(f32[14,80,256]{2,1,0:T(8,128)S(1)} %get-tuple-element.44.refs_1_), channel_id=1, source_target_pairs={{1,0},{3,2},{17,16},{19,18},{23,22},{21,20},{7,6},{5,4},{9,8},{11,... | collective-permute-start | bytes 3440648 | tf_op jit(solution)/shard_map/ppermute | solution.py:41
  110.1 16.4 %collective-permute-start.10 = (f32[14,80,256]{2,1,0:T(8,128)S(1)}, f32[14,80,256]{2,1,0:T(8,128)S(1)}, u32[]{:S(2)}, u32[]{:S(2)}) collective-permute-start(f32[14,80,256]{2,1,0:T(8,128)S(1)} %get-tuple-element.46.refs_3_), channel_id=1, source_target_pairs={{0,1},{2,3},{16,17},{18,19},{22,23},{20,21},{6,7},{4,5},{8,9},{10,... | collective-permute-start | bytes 3440648 | tf_op jit(solution)/shard_map/ppermute | solution.py:41
  139.3 8.6 %collective-permute-start.12 = (f32[30,8,256]{2,1,0:T(8,128)S(1)}, f32[30,8,256]{2,1,0:T(8,128)S(1)}, u32[]{:S(2)}, u32[]{:S(2)}) collective-permute-start(f32[30,8,256]{2,1,0:T(8,128)S(1)} %get-tuple-element.50), channel_id=1, source_target_pairs={{0,2},{2,16},{16,18},{18,22},{22,20},{20,6},{6,4},{4,8},{8,10},{10... | collective-permute-start | bytes 737288 | tf_op jit(solution)/shard_map/ppermute | solution.py:41
  143.4 8.3 %collective-permute-start.13 = (f32[30,8,256]{2,1,0:T(8,128)S(1)}, f32[30,8,256]{2,1,0:T(8,128)S(1)}, u32[]{:S(2)}, u32[]{:S(2)}) collective-permute-start(f32[30,8,256]{2,1,0:T(8,128)S(1)} %get-tuple-element.51), channel_id=1, source_target_pairs={{2,0},{16,2},{18,16},{22,18},{20,22},{6,20},{4,6},{8,4},{10,8},{24... | collective-permute-start | bytes 737288 | tf_op jit(solution)/shard_map/ppermute | solution.py:41
  151.9 11.0 %collective-permute-start.14 = (f32[7,64,256]{2,1,0:T(8,128)S(1)}, f32[7,64,256]{2,1,0:T(8,128)S(1)}, u32[]{:S(2)}, u32[]{:S(2)}) collective-permute-start(f32[7,64,256]{2,1,0:T(8,128)S(1)} %get-tuple-element.53), channel_id=1, source_target_pairs={{0,1},{2,3},{16,17},{18,19},{22,23},{20,21},{6,7},{4,5},{8,9},{10,... | collective-permute-start | bytes 1376264 | tf_op jit(solution)/shard_map/ppermute | solution.py:41
  157.5 11.0 %collective-permute-start.15 = (f32[7,64,256]{2,1,0:T(8,128)S(1)}, f32[7,64,256]{2,1,0:T(8,128)S(1)}, u32[]{:S(2)}, u32[]{:S(2)}) collective-permute-start(f32[7,64,256]{2,1,0:T(8,128)S(1)} %get-tuple-element.54), channel_id=1, source_target_pairs={{1,0},{3,2},{17,16},{19,18},{23,22},{21,20},{7,6},{5,4},{9,8},{11,... | collective-permute-start | bytes 1376264 | tf_op jit(solution)/shard_map/ppermute | solution.py:41
  168.8 27.7 %collective-permute-start.16 = (f32[16,64,256]{2,1,0:T(8,128)S(1)}, f32[16,64,256]{2,1,0:T(8,128)S(1)}, u32[]{:S(2)}, u32[]{:S(2)}) collective-permute-start(f32[16,64,256]{2,1,0:T(8,128)S(1)} %pad_maximum_fusion), channel_id=1, source_target_pairs={{0,0},{2,1},{16,2},{18,3},{22,4},{20,5},{6,6},{4,7},{8,8},{10,9},{... | collective-permute-start | bytes 3145736 | tf_op jit(solution)/shard_map/ppermute | solution.py:41
